TPU v7x, 256 devices: a whole 4x4x8 slice. The times are simulated.
256 devices in a mesh: sec: 4 (over y_hi, core), row: 4 (over x), col: 16 (over z, y_lo).
Axes of the slice: x: 4, y: 4 (y_hi: 2, y_lo: 2; y = y_hi * 2 + y_lo), z: 8, core: 2. Of those that a mesh axis runs over, the one named last changes fastest.
Arguments:
- images: float32 [4, 1024, 4096], P('sec', 'row', 'col'), may hold values from -6 to 6
- stiffness: float32 [4, 1024, 4096], P('sec', 'row', 'col'), may hold values from 0.1 to 1
Outputs:
- tensor: float32 [5, 4, 1024, 4096], P(None, 'sec', 'row', 'col')
- field: float32 [2, 4, 1024, 4096], P(None, 'sec', 'row', 'col')
All inputs are finite; a program needn't handle non-finite values.
Results may differ from a plain program's by a relative error of at most 0.00002.
Values sent between devices are 32-bit elements; how exact they have to be, the bound alone decides.
No kernel may reach another device: no remote copies, remote signals or barrier semaphores. Data moves between devices by JAX's collectives and lax.ppermute only.
A program may use at most 64 MiB of HBM per device.

v0:
```python
import jax
import jax.numpy as jnp
from jax import lax
from jax.sharding import PartitionSpec as P

RADIUS = 4
SWEEPS = 4
ROUNDS = 2


coupling = 0.25


def from_behind(value, axis, steps):
    count = lax.axis_size(axis)
    first, last = (max(0, -steps), min(count, count - steps))
    return lax.ppermute(value, axis, [(source, source + steps) for source in range(first, last)])


def extended(x, sides, width):
    for axis, dim in sides:
        size, length = (lax.axis_size(axis), x.shape[dim])
        up = [(i, (i + 1) % size) for i in range(size - 1)]
        down = [(j, i) for i, j in up]
        last = lax.slice_in_dim(x, length - width, length, axis=dim)
        first = lax.slice_in_dim(x, 0, width, axis=dim)
        before = lax.ppermute(last, axis, up)
        after = lax.ppermute(first, axis, down)
        x = jnp.concatenate([before, x, after], axis=dim)
    return x


def gradients(padded):
    grad_y = (padded[..., 2:, 1:-1] - padded[..., :-2, 1:-1]) * 0.5
    grad_x = (padded[..., 1:-1, 2:] - padded[..., 1:-1, :-2]) * 0.5
    return (grad_y, grad_x)


def products(grad_y, grad_x, change):
    return jnp.stack(
        [grad_x * grad_x, grad_x * grad_y, grad_y * grad_y, grad_x * change, grad_y * change]
    )


def window_mean(widened, radius):
    row_count = widened.shape[-2] - 2 * radius
    col_count = widened.shape[-1] - 2 * radius
    partial_rows = widened[..., 0:row_count, :]
    for offset in range(1, 2 * radius + 1):
        partial_rows = partial_rows + widened[..., offset : offset + row_count, :]
    summed = partial_rows[..., 0:col_count]
    for offset in range(1, 2 * radius + 1):
        summed = summed + partial_rows[..., offset : offset + col_count]
    return summed / float((2 * radius + 1) ** 2)


def couplings(stiff_pad):
    centre = stiff_pad[..., 1:-1, 1:-1]
    kappa_up = jnp.sqrt(centre * stiff_pad[..., :-2, 1:-1])
    kappa_down = jnp.sqrt(centre * stiff_pad[..., 2:, 1:-1])
    kappa_left = jnp.sqrt(centre * stiff_pad[..., 1:-1, :-2])
    kappa_right = jnp.sqrt(centre * stiff_pad[..., 1:-1, 2:])
    kappa_sum = kappa_up + kappa_down + kappa_left + kappa_right
    return ((kappa_up, kappa_down, kappa_left, kappa_right), kappa_sum)


def jacobi(field_pad, kappas, kappa_sum, tensor, beside):
    neighbour = kappas[0] * field_pad[..., :-2, 1:-1] + kappas[1] * field_pad[..., 2:, 1:-1]
    neighbour = (
        neighbour + kappas[2] * field_pad[..., 1:-1, :-2] + kappas[3] * field_pad[..., 1:-1, 2:]
    )
    diagonal = kappa_sum + 2.0 * coupling
    first_diag = tensor[0] + diagonal
    second_diag = tensor[2] + diagonal
    off_diag = tensor[1]
    determinant = first_diag * second_diag - off_diag * off_diag
    right_x = coupling * beside[0] + neighbour[0] - tensor[3]
    right_y = coupling * beside[1] + neighbour[1] - tensor[4]
    new_x = (second_diag * right_x - off_diag * right_y) / determinant
    new_y = (first_diag * right_y - off_diag * right_x) / determinant
    return jnp.stack([new_x, new_y])


def neighbours(field, round_index):
    if round_index == 0:
        return jnp.zeros_like(field)
    before = from_behind(field, "sec", 1)
    after = from_behind(field, "sec", -1)
    below_part = jnp.concatenate([before, field[:, :-1]], axis=1)
    above_part = jnp.concatenate([field[:, 1:], after], axis=1)
    return below_part + above_part


def local(images, stiffness):
    local_count = images.shape[0]
    earlier = from_behind(images, "sec", 1)
    first = jnp.concatenate([earlier, images[: local_count - 1]], axis=0)
    rimmed = extended(first, (("row", 1), ("col", 2)), 1)
    grad_y, grad_x = gradients(rimmed)
    stacked = products(grad_y, grad_x, images - first)
    widened = extended(stacked, (("row", 2), ("col", 3)), RADIUS)
    tensor = window_mean(widened, RADIUS)
    returned = from_behind(tensor, "sec", -1)
    tensor = jnp.concatenate([tensor[:, 1:], returned], axis=1)
    field = jnp.zeros((2,) + images.shape, jnp.float32)
    stiff_rim = extended(stiffness, (("row", 1), ("col", 2)), 1)
    kappas, kappa_sum = couplings(stiff_rim)
    for round_index in range(ROUNDS):
        beside = neighbours(field, round_index)
        for sweep_index in range(SWEEPS):
            field_pad = extended(field, (("row", 2), ("col", 3)), 1)
            field = jacobi(field_pad, kappas, kappa_sum, tensor, beside)
    return (tensor, field)


def solution(mesh):
    in_specs = (P("sec", "row", "col"), P("sec", "row", "col"))
    out_specs = (P(None, "sec", "row", "col"), P(None, "sec", "row", "col"))
    return jax.shard_map(local, mesh=mesh, in_specs=in_specs, out_specs=out_specs, check_vma=False)
```

profile of v0, /device:TPU:120, one launch (start us, length us, event | category | flops | bytes accessed | tf_op | source)
XLA Modules:
  0.0 276.4 jit_solution(11610499401364159785)
XLA Ops:
  2.6 7.5 %collective-permute-done = f32[1,256,256]{2,1,0:T(8,128)S(1)} collective-permute-done((f32[1,256,256]{2,1,0:T(8,128)}, f32[1,256,256]{2,1,0:T(8,128)S(1)}, u32[]{:S(2)}, u32[]{:S(2)}) %collective-permute-start) | collective-permute-done | bytes 262176 | tf_op jit(solution)/shard_map/ppermute | solution.py:17
  10.0 3.4 %collective-permute-start.1 = (f32[1,1,256]{2,1,0:T(1,128)S(1)}, f32[1,1,256]{2,1,0:T(1,128)S(1)}, u32[]{:S(2)}, u32[]{:S(2)}) collective-permute-start(f32[1,1,256]{2,1,0:T(1,128)S(1)} %get-tuple-element.65), channel_id=1, source_target_pairs={{0,16},{16,32},{32,48},{1,17},{17,33},{33,49},{2,18},{18,34},{34,5... | collective-permute-start | bytes 3080 | tf_op jit(solution)/shard_map/ppermute | solution.py:27
  14.7 4.2 %collective-permute-done.2 = f32[1,1,256]{2,1,0:T(1,128)S(1)} collective-permute-done((f32[1,1,256]{2,1,0:T(1,128)S(1)}, f32[1,1,256]{2,1,0:T(1,128)S(1)}, u32[]{:S(2)}, u32[]{:S(2)}) %collective-permute-start.2) | collective-permute-done | bytes 1056 | tf_op jit(solution)/shard_map/ppermute | solution.py:28
  19.0 2.7 collective-permute-start.3
  21.7 5.3 %collective-permute-start.4 = (f32[1,258,1]{2,1,0:T(8,128)S(1)}, f32[1,258,1]{2,1,0:T(8,128)S(1)}, u32[]{:S(2)}, u32[]{:S(2)}) collective-permute-start(f32[1,258,1]{2,1,0:T(8,128)S(1)} %get-tuple-element.58), channel_id=1, source_target_pairs={{0,1},{1,2},{2,3},{3,4},{4,5},{5,6},{6,7},{7,8},{8,9},{9,10},{10,1... | collective-permute-start | bytes 3104 | tf_op jit(solution)/shard_map/ppermute | solution.py:27
  30.5 3.4 %collective-permute-start.5 = (f32[5,1,4,256]{3,2,1,0:T(4,128)S(1)}, f32[5,1,4,256]{3,2,1,0:T(4,128)S(1)}, u32[]{:S(2)}, u32[]{:S(2)}) collective-permute-start(f32[5,1,4,256]{3,2,1,0:T(4,128)S(1)} %get-tuple-element.23), channel_id=1, source_target_pairs={{0,16},{16,32},{32,48},{1,17},{17,33},{33,49},{2,18},{18,34},{34,5... | collective-permute-start | bytes 61448 | tf_op jit(solution)/shard_map/ppermute | solution.py:27
  35.4 4.2 %collective-permute-done.6 = f32[5,1,4,256]{3,2,1,0:T(4,128)S(1)} collective-permute-done((f32[5,1,4,256]{3,2,1,0:T(4,128)S(1)}, f32[5,1,4,256]{3,2,1,0:T(4,128)S(1)}, u32[]{:S(2)}, u32[]{:S(2)}) %collective-permute-start.6) | collective-permute-done | bytes 20512 | tf_op jit(solution)/shard_map/ppermute | solution.py:28
  40.3 6.5 %collective-permute-start.7 = (f32[5,1,264,4]{2,3,1,0:T(4,128)S(1)}, f32[5,1,264,4]{2,3,1,0:T(4,128)S(1)}, u32[]{:S(2)}, u32[]{:S(2)}) collective-permute-start(f32[5,1,264,4]{2,3,1,0:T(4,128)S(1)} %copy.17), channel_id=1, source_target_pairs={{0,1},{1,2},{2,3},{3,4},{4,5},{5,6},{6,7},{7,8},{8,9},{9,10},{10,1... | collective-permute-start | bytes 63368 | tf_op jit(solution)/shard_map/ppermute | solution.py:27
  49.3 5.7 %collective-permute-done.8 = f32[5,1,264,4]{2,3,1,0:T(4,128)S(1)} collective-permute-done((f32[5,1,264,4]{2,3,1,0:T(4,128)S(1)}, f32[5,1,264,4]{2,3,1,0:T(4,128)S(1)}, u32[]{:S(2)}, u32[]{:S(2)}) %collective-permute-start.8) | collective-permute-done | bytes 21152 | tf_op jit(solution)/shard_map/ppermute | solution.py:28
  57.5 2.8 fusion
  62.2 3.1 %collective-permute-start.10 = (f32[1,1,256]{2,1,0:T(1,128)S(1)}, f32[1,1,256]{2,1,0:T(1,128)S(1)}, u32[]{:S(2)}, u32[]{:S(2)}) collective-permute-start(f32[1,1,256]{2,1,0:T(1,128)S(1)} %get-tuple-element.63), channel_id=1, source_target_pairs={{0,16},{16,32},{32,48},{1,17},{17,33},{33,49},{2,18},{18,34},{34,5... | collective-permute-start | bytes 3080 | tf_op jit(solution)/shard_map/ppermute | solution.py:27
  66.7 4.5 %collective-permute-start.14 = (f32[2,1,1,256]{3,2,1,0:T(1,128)S(1)}, f32[2,1,1,256]{3,2,1,0:T(1,128)S(1)}, u32[]{:S(2)}, u32[]{:S(2)}) collective-permute-start(f32[2,1,1,256]{3,2,1,0:T(1,128)S(1)} %broadcast.94), channel_id=1, source_target_pairs={{0,16},{16,32},{32,48},{1,17},{17,33},{33,49},{2,18},{18,34},{34,5... | collective-permute-start | bytes 6152 | tf_op jit(solution)/shard_map/ppermute | solution.py:27
  74.6 3.9 %collective-permute-start.13 = (f32[1,258,1]{2,1,0:T(8,128)S(1)}, f32[1,258,1]{2,1,0:T(8,128)S(1)}, u32[]{:S(2)}, u32[]{:S(2)}) collective-permute-start(f32[1,258,1]{2,1,0:T(8,128)S(1)} %get-tuple-element.56), channel_id=1, source_target_pairs={{1,0},{2,1},{3,2},{4,3},{5,4},{6,5},{7,6},{8,7},{9,8},{10,9},{11,1... | collective-permute-start | bytes 3104 | tf_op jit(solution)/shard_map/ppermute | solution.py:28
  78.8 4.0 %collective-permute-start.16 = (f32[2,1,258,1]{3,2,1,0:T(8,128)S(1)}, f32[2,1,258,1]{3,2,1,0:T(8,128)S(1)}, u32[]{:S(2)}, u32[]{:S(2)}) collective-permute-start(f32[2,1,258,1]{3,2,1,0:T(8,128)S(1)} %get-tuple-element.39), channel_id=1, source_target_pairs={{0,1},{1,2},{2,3},{3,4},{4,5},{5,6},{6,7},{7,8},{8,9},{9,10},{10,1... | collective-permute-start | bytes 6200 | tf_op jit(solution)/shard_map/ppermute | solution.py:27
  84.8 5.9 %collective-permute-done.13 = f32[1,258,1]{2,1,0:T(8,128)S(1)} collective-permute-done((f32[1,258,1]{2,1,0:T(8,128)S(1)}, f32[1,258,1]{2,1,0:T(8,128)S(1)}, u32[]{:S(2)}, u32[]{:S(2)}) %collective-permute-start.13) | collective-permute-done | bytes 1064 | tf_op jit(solution)/shard_map/ppermute | solution.py:28
  91.1 4.3 %collective-permute-done.16 = f32[2,1,258,1]{3,2,1,0:T(8,128)S(1)} collective-permute-done((f32[2,1,258,1]{3,2,1,0:T(8,128)S(1)}, f32[2,1,258,1]{3,2,1,0:T(8,128)S(1)}, u32[]{:S(2)}, u32[]{:S(2)}) %collective-permute-start.16) | collective-permute-done | bytes 2096 | tf_op jit(solution)/shard_map/ppermute | solution.py:27
  96.6 4.3 %collective-permute-start.18 = (f32[2,1,1,256]{3,2,1,0:T(1,128)S(1)}, f32[2,1,1,256]{3,2,1,0:T(1,128)S(1)}, u32[]{:S(2)}, u32[]{:S(2)}) collective-permute-start(f32[2,1,1,256]{3,2,1,0:T(1,128)S(1)} %get-tuple-element.53), channel_id=1, source_target_pairs={{0,16},{16,32},{32,48},{1,17},{17,33},{33,49},{2,18},{18,34},{34,5... | collective-permute-start | bytes 6152 | tf_op jit(solution)/shard_map/ppermute | solution.py:27
  102.2 4.2 %collective-permute-done.19 = f32[2,1,1,256]{3,2,1,0:T(1,128)S(1)} collective-permute-done((f32[2,1,1,256]{3,2,1,0:T(1,128)S(1)}, f32[2,1,1,256]{3,2,1,0:T(1,128)S(1)}, u32[]{:S(2)}, u32[]{:S(2)}) %collective-permute-start.19) | collective-permute-done | bytes 2080 | tf_op jit(solution)/shard_map/ppermute | solution.py:28
  106.6 4.8 %collective-permute-start.20 = (f32[2,1,258,1]{3,2,1,0:T(8,128)S(1)}, f32[2,1,258,1]{3,2,1,0:T(8,128)S(1)}, u32[]{:S(2)}, u32[]{:S(2)}) collective-permute-start(f32[2,1,258,1]{3,2,1,0:T(8,128)S(1)} %get-tuple-element.37), channel_id=1, source_target_pairs={{0,1},{1,2},{2,3},{3,4},{4,5},{5,6},{6,7},{7,8},{8,9},{9,10},{10,1... | collective-permute-start | bytes 6200 | tf_op jit(solution)/shard_map/ppermute | solution.py:27
  113.3 2.4 collective-permute-done.20
  115.7 6.2 %collective-permute-done.21 = f32[2,1,258,1]{3,2,1,0:T(8,128)S(1)} collective-permute-done((f32[2,1,258,1]{3,2,1,0:T(8,128)S(1)}, f32[2,1,258,1]{3,2,1,0:T(8,128)S(1)}, u32[]{:S(2)}, u32[]{:S(2)}) %collective-permute-start.21) | collective-permute-done | bytes 2096 | tf_op jit(solution)/shard_map/ppermute | solution.py:28
  122.5 2.2 collective-permute-start.22
  126.0 4.2 %collective-permute-done.23 = f32[2,1,1,256]{3,2,1,0:T(1,128)S(1)} collective-permute-done((f32[2,1,1,256]{3,2,1,0:T(1,128)S(1)}, f32[2,1,1,256]{3,2,1,0:T(1,128)S(1)}, u32[]{:S(2)}, u32[]{:S(2)}) %collective-permute-start.23) | collective-permute-done | bytes 2080 | tf_op jit(solution)/shard_map/ppermute | solution.py:28
  130.3 5.9 %collective-permute-start.24 = (f32[2,1,258,1]{3,2,1,0:T(8,128)S(1)}, f32[2,1,258,1]{3,2,1,0:T(8,128)S(1)}, u32[]{:S(2)}, u32[]{:S(2)}) collective-permute-start(f32[2,1,258,1]{3,2,1,0:T(8,128)S(1)} %get-tuple-element.35), channel_id=1, source_target_pairs={{0,1},{1,2},{2,3},{3,4},{4,5},{5,6},{6,7},{7,8},{8,9},{9,10},{10,1... | collective-permute-start | bytes 6200 | tf_op jit(solution)/shard_map/ppermute | solution.py:27
  138.2 2.4 collective-permute-done.24
  140.6 6.2 %collective-permute-done.25 = f32[2,1,258,1]{3,2,1,0:T(8,128)S(1)} collective-permute-done((f32[2,1,258,1]{3,2,1,0:T(8,128)S(1)}, f32[2,1,258,1]{3,2,1,0:T(8,128)S(1)}, u32[]{:S(2)}, u32[]{:S(2)}) %collective-permute-start.25) | collective-permute-done | bytes 2096 | tf_op jit(solution)/shard_map/ppermute | solution.py:28
  147.3 2.2 collective-permute-start.26
  151.0 4.0 %collective-permute-done.27 = f32[2,1,1,256]{3,2,1,0:T(1,128)S(1)} collective-permute-done((f32[2,1,1,256]{3,2,1,0:T(1,128)S(1)}, f32[2,1,1,256]{3,2,1,0:T(1,128)S(1)}, u32[]{:S(2)}, u32[]{:S(2)}) %collective-permute-start.27) | collective-permute-done | bytes 2080 | tf_op jit(solution)/shard_map/ppermute | solution.py:28
  155.2 5.9 %collective-permute-start.28 = (f32[2,1,258,1]{3,2,1,0:T(8,128)S(1)}, f32[2,1,258,1]{3,2,1,0:T(8,128)S(1)}, u32[]{:S(2)}, u32[]{:S(2)}) collective-permute-start(f32[2,1,258,1]{3,2,1,0:T(8,128)S(1)} %get-tuple-element.33), channel_id=1, source_target_pairs={{0,1},{1,2},{2,3},{3,4},{4,5},{5,6},{6,7},{7,8},{8,9},{9,10},{10,1... | collective-permute-start | bytes 6200 | tf_op jit(solution)/shard_map/ppermute | solution.py:27
  163.0 2.4 collective-permute-done.28
  165.4 6.2 %collective-permute-done.29 = f32[2,1,258,1]{3,2,1,0:T(8,128)S(1)} collective-permute-done((f32[2,1,258,1]{3,2,1,0:T(8,128)S(1)}, f32[2,1,258,1]{3,2,1,0:T(8,128)S(1)}, u32[]{:S(2)}, u32[]{:S(2)}) %collective-permute-start.29) | collective-permute-done | bytes 2096 | tf_op jit(solution)/shard_map/ppermute | solution.py:28
  172.2 2.2 collective-permute-start.32
  177.7 5.1 %collective-permute-start.31 = (f32[2,1,256,256]{3,2,1,0:T(8,128)S(1)}, f32[2,1,256,256]{3,2,1,0:T(8,128)S(1)}, u32[]{:S(2)}, u32[]{:S(2)}) collective-permute-start(f32[2,1,256,256]{3,2,1,0:T(8,128)S(1)} %pad_maximum_fusion.2), channel_id=1, source_target_pairs={{64,0},{128,64},{192,128},{65,1},{129,65},{193,129},{66,2},{130,66... | collective-permute-start | bytes 1572872 | tf_op jit(solution)/shard_map/ppermute | solution.py:17
  183.0 5.9 %collective-permute-start.34 = (f32[2,1,258,1]{3,2,1,0:T(8,128)S(1)}, f32[2,1,258,1]{3,2,1,0:T(8,128)S(1)}, u32[]{:S(2)}, u32[]{:S(2)}) collective-permute-start(f32[2,1,258,1]{3,2,1,0:T(8,128)S(1)} %get-tuple-element.31), channel_id=1, source_target_pairs={{0,1},{1,2},{2,3},{3,4},{4,5},{5,6},{6,7},{7,8},{8,9},{9,10},{10,1... | collective-permute-start | bytes 6200 | tf_op jit(solution)/shard_map/ppermute | solution.py:27
  190.9 8.9 %collective-permute-done.34 = f32[2,1,258,1]{3,2,1,0:T(8,128)S(1)} collective-permute-done((f32[2,1,258,1]{3,2,1,0:T(8,128)S(1)}, f32[2,1,258,1]{3,2,1,0:T(8,128)S(1)}, u32[]{:S(2)}, u32[]{:S(2)}) %collective-permute-start.34) | collective-permute-done | bytes 2096 | tf_op jit(solution)/shard_map/ppermute | solution.py:27
  200.4 4.5 %collective-permute-start.36 = (f32[2,1,1,256]{3,2,1,0:T(1,128)S(1)}, f32[2,1,1,256]{3,2,1,0:T(1,128)S(1)}, u32[]{:S(2)}, u32[]{:S(2)}) collective-permute-start(f32[2,1,1,256]{3,2,1,0:T(1,128)S(1)} %get-tuple-element.45), channel_id=1, source_target_pairs={{0,16},{16,32},{32,48},{1,17},{17,33},{33,49},{2,18},{18,34},{34,5... | collective-permute-start | bytes 6152 | tf_op jit(solution)/shard_map/ppermute | solution.py:27
  206.3 4.2 %collective-permute-done.37 = f32[2,1,1,256]{3,2,1,0:T(1,128)S(1)} collective-permute-done((f32[2,1,1,256]{3,2,1,0:T(1,128)S(1)}, f32[2,1,1,256]{3,2,1,0:T(1,128)S(1)}, u32[]{:S(2)}, u32[]{:S(2)}) %collective-permute-start.37) | collective-permute-done | bytes 2080 | tf_op jit(solution)/shard_map/ppermute | solution.py:28
  210.7 7.2 %collective-permute-start.38 = (f32[2,1,258,1]{3,2,1,0:T(8,128)S(1)}, f32[2,1,258,1]{3,2,1,0:T(8,128)S(1)}, u32[]{:S(2)}, u32[]{:S(2)}) collective-permute-start(f32[2,1,258,1]{3,2,1,0:T(8,128)S(1)} %get-tuple-element.29), channel_id=1, source_target_pairs={{0,1},{1,2},{2,3},{3,4},{4,5},{5,6},{6,7},{7,8},{8,9},{9,10},{10,1... | collective-permute-start | bytes 6200 | tf_op jit(solution)/shard_map/ppermute | solution.py:27
  221.9 6.5 %collective-permute-done.39 = f32[2,1,258,1]{3,2,1,0:T(8,128)S(1)} collective-permute-done((f32[2,1,258,1]{3,2,1,0:T(8,128)S(1)}, f32[2,1,258,1]{3,2,1,0:T(8,128)S(1)}, u32[]{:S(2)}, u32[]{:S(2)}) %collective-permute-start.39) | collective-permute-done | bytes 2096 | tf_op jit(solution)/shard_map/ppermute | solution.py:28
  229.0 2.2 collective-permute-start.40
  232.5 4.2 %collective-permute-done.41 = f32[2,1,1,256]{3,2,1,0:T(1,128)S(1)} collective-permute-done((f32[2,1,1,256]{3,2,1,0:T(1,128)S(1)}, f32[2,1,1,256]{3,2,1,0:T(1,128)S(1)}, u32[]{:S(2)}, u32[]{:S(2)}) %collective-permute-start.41) | collective-permute-done | bytes 2080 | tf_op jit(solution)/shard_map/ppermute | solution.py:28
  236.9 3.5 %collective-permute-start.42 = (f32[2,1,258,1]{3,2,1,0:T(8,128)S(1)}, f32[2,1,258,1]{3,2,1,0:T(8,128)S(1)}, u32[]{:S(2)}, u32[]{:S(2)}) collective-permute-start(f32[2,1,258,1]{3,2,1,0:T(8,128)S(1)} %get-tuple-element.27), channel_id=1, source_target_pairs={{0,1},{1,2},{2,3},{3,4},{4,5},{5,6},{6,7},{7,8},{8,9},{9,10},{10,1... | collective-permute-start | bytes 6200 | tf_op jit(solution)/shard_map/ppermute | solution.py:27
  240.4 2.3 collective-permute-start.43
  242.7 8.3 %collective-permute-done.42 = f32[2,1,258,1]{3,2,1,0:T(8,128)S(1)} collective-permute-done((f32[2,1,258,1]{3,2,1,0:T(8,128)S(1)}, f32[2,1,258,1]{3,2,1,0:T(8,128)S(1)}, u32[]{:S(2)}, u32[]{:S(2)}) %collective-permute-start.42) | collective-permute-done | bytes 2096 | tf_op jit(solution)/shard_map/ppermute | solution.py:27
  255.0 4.2 %collective-permute-done.45 = f32[2,1,1,256]{3,2,1,0:T(1,128)S(1)} collective-permute-done((f32[2,1,1,256]{3,2,1,0:T(1,128)S(1)}, f32[2,1,1,256]{3,2,1,0:T(1,128)S(1)}, u32[]{:S(2)}, u32[]{:S(2)}) %collective-permute-start.45) | collective-permute-done | bytes 2080 | tf_op jit(solution)/shard_map/ppermute | solution.py:28
  259.4 4.0 %collective-permute-start.46 = (f32[2,1,258,1]{3,2,1,0:T(8,128)S(1)}, f32[2,1,258,1]{3,2,1,0:T(8,128)S(1)}, u32[]{:S(2)}, u32[]{:S(2)}) collective-permute-start(f32[2,1,258,1]{3,2,1,0:T(8,128)S(1)} %get-tuple-element.25), channel_id=1, source_target_pairs={{0,1},{1,2},{2,3},{3,4},{4,5},{5,6},{6,7},{7,8},{8,9},{9,10},{10,1... | collective-permute-start | bytes 6200 | tf_op jit(solution)/shard_map/ppermute | solution.py:27
  265.3 5.3 %collective-permute-done.46 = f32[2,1,258,1]{3,2,1,0:T(8,128)S(1)} collective-permute-done((f32[2,1,258,1]{3,2,1,0:T(8,128)S(1)}, f32[2,1,258,1]{3,2,1,0:T(8,128)S(1)}, u32[]{:S(2)}, u32[]{:S(2)}) %collective-permute-start.46) | collective-permute-done | bytes 2096 | tf_op jit(solution)/shard_map/ppermute | solution.py:27
  270.6 3.3 %collective-permute-done.47 = f32[2,1,258,1]{3,2,1,0:T(8,128)S(1)} collective-permute-done((f32[2,1,258,1]{3,2,1,0:T(8,128)S(1)}, f32[2,1,258,1]{3,2,1,0:T(8,128)S(1)}, u32[]{:S(2)}, u32[]{:S(2)}) %collective-permute-start.47) | collective-permute-done | bytes 2096 | tf_op jit(solution)/shard_map/ppermute | solution.py:28
  (120 shorter events, 58.3 us)
Async XLA Ops:
  0.6 9.4 %collective-permute-start = (f32[1,256,256]{2,1,0:T(8,128)}, f32[1,256,256]{2,1,0:T(8,128)S(1)}, u32[]{:S(2)}, u32[]{:S(2)}) collective-permute-start(f32[1,256,256]{2,1,0:T(8,128)} %param.2), channel_id=1, source_target_pairs={{0,64},{64,128},{128,192},{1,65},{65,129},{129,193},{2,66},{66,130... | collective-permute-start | bytes 786440 | tf_op jit(solution)/shard_map/ppermute | solution.py:17
  10.0 4.7 %collective-permute-start.1 = (f32[1,1,256]{2,1,0:T(1,128)S(1)}, f32[1,1,256]{2,1,0:T(1,128)S(1)}, u32[]{:S(2)}, u32[]{:S(2)}) collective-permute-start(f32[1,1,256]{2,1,0:T(1,128)S(1)} %get-tuple-element.65), channel_id=1, source_target_pairs={{0,16},{16,32},{32,48},{1,17},{17,33},{33,49},{2,18},{18,34},{34,5... | collective-permute-start | bytes 3080 | tf_op jit(solution)/shard_map/ppermute | solution.py:27
  13.4 5.5 %collective-permute-start.2 = (f32[1,1,256]{2,1,0:T(1,128)S(1)}, f32[1,1,256]{2,1,0:T(1,128)S(1)}, u32[]{:S(2)}, u32[]{:S(2)}) collective-permute-start(f32[1,1,256]{2,1,0:T(1,128)S(1)} %get-tuple-element.66), channel_id=1, source_target_pairs={{16,0},{32,16},{48,32},{17,1},{33,17},{49,33},{18,2},{34,18},{50,3... | collective-permute-start | bytes 3080 | tf_op jit(solution)/shard_map/ppermute | solution.py:28
  19.0 9.1 %collective-permute-start.3 = (f32[1,258,1]{2,1,0:T(8,128)S(1)}, f32[1,258,1]{2,1,0:T(8,128)S(1)}, u32[]{:S(2)}, u32[]{:S(2)}) collective-permute-start(f32[1,258,1]{2,1,0:T(8,128)S(1)} %get-tuple-element.57), channel_id=1, source_target_pairs={{1,0},{2,1},{3,2},{4,3},{5,4},{6,5},{7,6},{8,7},{9,8},{10,9},{11,1... | collective-permute-start | bytes 3104 | tf_op jit(solution)/shard_map/ppermute | solution.py:28
  21.7 7.8 %collective-permute-start.4 = (f32[1,258,1]{2,1,0:T(8,128)S(1)}, f32[1,258,1]{2,1,0:T(8,128)S(1)}, u32[]{:S(2)}, u32[]{:S(2)}) collective-permute-start(f32[1,258,1]{2,1,0:T(8,128)S(1)} %get-tuple-element.58), channel_id=1, source_target_pairs={{0,1},{1,2},{2,3},{3,4},{4,5},{5,6},{6,7},{7,8},{8,9},{9,10},{10,1... | collective-permute-start | bytes 3104 | tf_op jit(solution)/shard_map/ppermute | solution.py:27
  30.5 4.9 %collective-permute-start.5 = (f32[5,1,4,256]{3,2,1,0:T(4,128)S(1)}, f32[5,1,4,256]{3,2,1,0:T(4,128)S(1)}, u32[]{:S(2)}, u32[]{:S(2)}) collective-permute-start(f32[5,1,4,256]{3,2,1,0:T(4,128)S(1)} %get-tuple-element.23), channel_id=1, source_target_pairs={{0,16},{16,32},{32,48},{1,17},{17,33},{33,49},{2,18},{18,34},{34,5... | collective-permute-start | bytes 61448 | tf_op jit(solution)/shard_map/ppermute | solution.py:27
  33.9 5.7 %collective-permute-start.6 = (f32[5,1,4,256]{3,2,1,0:T(4,128)S(1)}, f32[5,1,4,256]{3,2,1,0:T(4,128)S(1)}, u32[]{:S(2)}, u32[]{:S(2)}) collective-permute-start(f32[5,1,4,256]{3,2,1,0:T(4,128)S(1)} %get-tuple-element.24), channel_id=1, source_target_pairs={{16,0},{32,16},{48,32},{17,1},{33,17},{49,33},{18,2},{34,18},{50,3... | collective-permute-start | bytes 61448 | tf_op jit(solution)/shard_map/ppermute | solution.py:28
  40.3 8.8 %collective-permute-start.7 = (f32[5,1,264,4]{2,3,1,0:T(4,128)S(1)}, f32[5,1,264,4]{2,3,1,0:T(4,128)S(1)}, u32[]{:S(2)}, u32[]{:S(2)}) collective-permute-start(f32[5,1,264,4]{2,3,1,0:T(4,128)S(1)} %copy.17), channel_id=1, source_target_pairs={{0,1},{1,2},{2,3},{3,4},{4,5},{5,6},{6,7},{7,8},{8,9},{9,10},{10,1... | collective-permute-start | bytes 63368 | tf_op jit(solution)/shard_map/ppermute | solution.py:27
  47.1 7.9 %collective-permute-start.8 = (f32[5,1,264,4]{2,3,1,0:T(4,128)S(1)}, f32[5,1,264,4]{2,3,1,0:T(4,128)S(1)}, u32[]{:S(2)}, u32[]{:S(2)}) collective-permute-start(f32[5,1,264,4]{2,3,1,0:T(4,128)S(1)} %copy.18), channel_id=1, source_target_pairs={{1,0},{2,1},{3,2},{4,3},{5,4},{6,5},{7,6},{8,7},{9,8},{10,9},{11,1... | collective-permute-start | bytes 63368 | tf_op jit(solution)/shard_map/ppermute | solution.py:28
  60.3 35.6 %collective-permute-start.9 = (f32[5,1,256,256]{3,2,1,0:T(8,128)S(1)}, f32[5,1,256,256]{3,2,1,0:T(8,128)S(1)}, u32[]{:S(2)}, u32[]{:S(2)}) collective-permute-start(f32[5,1,256,256]{3,2,1,0:T(8,128)S(1)} %fusion), channel_id=1, source_target_pairs={{64,0},{128,64},{192,128},{65,1},{129,65},{193,129},{66,2},{130,66... | collective-permute-start | bytes 3932168 | tf_op jit(solution)/shard_map/ppermute | solution.py:17
  62.2 10.3 %collective-permute-start.10 = (f32[1,1,256]{2,1,0:T(1,128)S(1)}, f32[1,1,256]{2,1,0:T(1,128)S(1)}, u32[]{:S(2)}, u32[]{:S(2)}) collective-permute-start(f32[1,1,256]{2,1,0:T(1,128)S(1)} %get-tuple-element.63), channel_id=1, source_target_pairs={{0,16},{16,32},{32,48},{1,17},{17,33},{33,49},{2,18},{18,34},{34,5... | collective-permute-start | bytes 3080 | tf_op jit(solution)/shard_map/ppermute | solution.py:27
  65.3 7.2 %collective-permute-start.11 = (f32[1,1,256]{2,1,0:T(1,128)S(1)}, f32[1,1,256]{2,1,0:T(1,128)S(1)}, u32[]{:S(2)}, u32[]{:S(2)}) collective-permute-start(f32[1,1,256]{2,1,0:T(1,128)S(1)} %get-tuple-element.64), channel_id=1, source_target_pairs={{16,0},{32,16},{48,32},{17,1},{33,17},{49,33},{18,2},{34,18},{50,3... | collective-permute-start | bytes 3080 | tf_op jit(solution)/shard_map/ppermute | solution.py:28
  66.7 11.9 %collective-permute-start.14 = (f32[2,1,1,256]{3,2,1,0:T(1,128)S(1)}, f32[2,1,1,256]{3,2,1,0:T(1,128)S(1)}, u32[]{:S(2)}, u32[]{:S(2)}) collective-permute-start(f32[2,1,1,256]{3,2,1,0:T(1,128)S(1)} %broadcast.94), channel_id=1, source_target_pairs={{0,16},{16,32},{32,48},{1,17},{17,33},{33,49},{2,18},{18,34},{34,5... | collective-permute-start | bytes 6152 | tf_op jit(solution)/shard_map/ppermute | solution.py:27
  71.2 7.3 %collective-permute-start.15 = (f32[2,1,1,256]{3,2,1,0:T(1,128)S(1)}, f32[2,1,1,256]{3,2,1,0:T(1,128)S(1)}, u32[]{:S(2)}, u32[]{:S(2)}) collective-permute-start(f32[2,1,1,256]{3,2,1,0:T(1,128)S(1)} %broadcast.94), channel_id=1, source_target_pairs={{16,0},{32,16},{48,32},{17,1},{33,17},{49,33},{18,2},{34,18},{50,3... | collective-permute-start | bytes 6152 | tf_op jit(solution)/shard_map/ppermute | solution.py:28
  72.7 12.1 %collective-permute-start.12 = (f32[1,258,1]{2,1,0:T(8,128)S(1)}, f32[1,258,1]{2,1,0:T(8,128)S(1)}, u32[]{:S(2)}, u32[]{:S(2)}) collective-permute-start(f32[1,258,1]{2,1,0:T(8,128)S(1)} %get-tuple-element.55), channel_id=1, source_target_pairs={{0,1},{1,2},{2,3},{3,4},{4,5},{5,6},{6,7},{7,8},{8,9},{9,10},{10,1... | collective-permute-start | bytes 3104 | tf_op jit(solution)/shard_map/ppermute | solution.py:27
  74.6 16.1 %collective-permute-start.13 = (f32[1,258,1]{2,1,0:T(8,128)S(1)}, f32[1,258,1]{2,1,0:T(8,128)S(1)}, u32[]{:S(2)}, u32[]{:S(2)}) collective-permute-start(f32[1,258,1]{2,1,0:T(8,128)S(1)} %get-tuple-element.56), channel_id=1, source_target_pairs={{1,0},{2,1},{3,2},{4,3},{5,4},{6,5},{7,6},{8,7},{9,8},{10,9},{11,1... | collective-permute-start | bytes 3104 | tf_op jit(solution)/shard_map/ppermute | solution.py:28
  78.8 16.6 %collective-permute-start.16 = (f32[2,1,258,1]{3,2,1,0:T(8,128)S(1)}, f32[2,1,258,1]{3,2,1,0:T(8,128)S(1)}, u32[]{:S(2)}, u32[]{:S(2)}) collective-permute-start(f32[2,1,258,1]{3,2,1,0:T(8,128)S(1)} %get-tuple-element.39), channel_id=1, source_target_pairs={{0,1},{1,2},{2,3},{3,4},{4,5},{5,6},{6,7},{7,8},{8,9},{9,10},{10,1... | collective-permute-start | bytes 6200 | tf_op jit(solution)/shard_map/ppermute | solution.py:27
  82.8 12.6 %collective-permute-start.17 = (f32[2,1,258,1]{3,2,1,0:T(8,128)S(1)}, f32[2,1,258,1]{3,2,1,0:T(8,128)S(1)}, u32[]{:S(2)}, u32[]{:S(2)}) collective-permute-start(f32[2,1,258,1]{3,2,1,0:T(8,128)S(1)} %get-tuple-element.40), channel_id=1, source_target_pairs={{1,0},{2,1},{3,2},{4,3},{5,4},{6,5},{7,6},{8,7},{9,8},{10,9},{11,1... | collective-permute-start | bytes 6200 | tf_op jit(solution)/shard_map/ppermute | solution.py:28
  96.6 5.6 %collective-permute-start.18 = (f32[2,1,1,256]{3,2,1,0:T(1,128)S(1)}, f32[2,1,1,256]{3,2,1,0:T(1,128)S(1)}, u32[]{:S(2)}, u32[]{:S(2)}) collective-permute-start(f32[2,1,1,256]{3,2,1,0:T(1,128)S(1)} %get-tuple-element.53), channel_id=1, source_target_pairs={{0,16},{16,32},{32,48},{1,17},{17,33},{33,49},{2,18},{18,34},{34,5... | collective-permute-start | bytes 6152 | tf_op jit(solution)/shard_map/ppermute | solution.py:27
  100.9 5.5 %collective-permute-start.19 = (f32[2,1,1,256]{3,2,1,0:T(1,128)S(1)}, f32[2,1,1,256]{3,2,1,0:T(1,128)S(1)}, u32[]{:S(2)}, u32[]{:S(2)}) collective-permute-start(f32[2,1,1,256]{3,2,1,0:T(1,128)S(1)} %get-tuple-element.54), channel_id=1, source_target_pairs={{16,0},{32,16},{48,32},{17,1},{33,17},{49,33},{18,2},{34,18},{50,3... | collective-permute-start | bytes 6152 | tf_op jit(solution)/shard_map/ppermute | solution.py:28
  106.6 9.1 %collective-permute-start.20 = (f32[2,1,258,1]{3,2,1,0:T(8,128)S(1)}, f32[2,1,258,1]{3,2,1,0:T(8,128)S(1)}, u32[]{:S(2)}, u32[]{:S(2)}) collective-permute-start(f32[2,1,258,1]{3,2,1,0:T(8,128)S(1)} %get-tuple-element.37), channel_id=1, source_target_pairs={{0,1},{1,2},{2,3},{3,4},{4,5},{5,6},{6,7},{7,8},{8,9},{9,10},{10,1... | collective-permute-start | bytes 6200 | tf_op jit(solution)/shard_map/ppermute | solution.py:27
  111.4 10.5 %collective-permute-start.21 = (f32[2,1,258,1]{3,2,1,0:T(8,128)S(1)}, f32[2,1,258,1]{3,2,1,0:T(8,128)S(1)}, u32[]{:S(2)}, u32[]{:S(2)}) collective-permute-start(f32[2,1,258,1]{3,2,1,0:T(8,128)S(1)} %get-tuple-element.38), channel_id=1, source_target_pairs={{1,0},{2,1},{3,2},{4,3},{5,4},{6,5},{7,6},{8,7},{9,8},{10,9},{11,1... | collective-permute-start | bytes 6200 | tf_op jit(solution)/shard_map/ppermute | solution.py:28
  122.5 3.5 %collective-permute-start.22 = (f32[2,1,1,256]{3,2,1,0:T(1,128)S(1)}, f32[2,1,1,256]{3,2,1,0:T(1,128)S(1)}, u32[]{:S(2)}, u32[]{:S(2)}) collective-permute-start(f32[2,1,1,256]{3,2,1,0:T(1,128)S(1)} %get-tuple-element.51), channel_id=1, source_target_pairs={{0,16},{16,32},{32,48},{1,17},{17,33},{33,49},{2,18},{18,34},{34,5... | collective-permute-start | bytes 6152 | tf_op jit(solution)/shard_map/ppermute | solution.py:27
  124.7 5.5 %collective-permute-start.23 = (f32[2,1,1,256]{3,2,1,0:T(1,128)S(1)}, f32[2,1,1,256]{3,2,1,0:T(1,128)S(1)}, u32[]{:S(2)}, u32[]{:S(2)}) collective-permute-start(f32[2,1,1,256]{3,2,1,0:T(1,128)S(1)} %get-tuple-element.52), channel_id=1, source_target_pairs={{16,0},{32,16},{48,32},{17,1},{33,17},{49,33},{18,2},{34,18},{50,3... | collective-permute-start | bytes 6152 | tf_op jit(solution)/shard_map/ppermute | solution.py:28
  130.3 10.2 %collective-permute-start.24 = (f32[2,1,258,1]{3,2,1,0:T(8,128)S(1)}, f32[2,1,258,1]{3,2,1,0:T(8,128)S(1)}, u32[]{:S(2)}, u32[]{:S(2)}) collective-permute-start(f32[2,1,258,1]{3,2,1,0:T(8,128)S(1)} %get-tuple-element.35), channel_id=1, source_target_pairs={{0,1},{1,2},{2,3},{3,4},{4,5},{5,6},{6,7},{7,8},{8,9},{9,10},{10,1... | collective-permute-start | bytes 6200 | tf_op jit(solution)/shard_map/ppermute | solution.py:27
  136.2 10.5 %collective-permute-start.25 = (f32[2,1,258,1]{3,2,1,0:T(8,128)S(1)}, f32[2,1,258,1]{3,2,1,0:T(8,128)S(1)}, u32[]{:S(2)}, u32[]{:S(2)}) collective-permute-start(f32[2,1,258,1]{3,2,1,0:T(8,128)S(1)} %get-tuple-element.36), channel_id=1, source_target_pairs={{1,0},{2,1},{3,2},{4,3},{5,4},{6,5},{7,6},{8,7},{9,8},{10,9},{11,1... | collective-permute-start | bytes 6200 | tf_op jit(solution)/shard_map/ppermute | solution.py:28
  147.3 3.7 %collective-permute-start.26 = (f32[2,1,1,256]{3,2,1,0:T(1,128)S(1)}, f32[2,1,1,256]{3,2,1,0:T(1,128)S(1)}, u32[]{:S(2)}, u32[]{:S(2)}) collective-permute-start(f32[2,1,1,256]{3,2,1,0:T(1,128)S(1)} %get-tuple-element.49), channel_id=1, source_target_pairs={{0,16},{16,32},{32,48},{1,17},{17,33},{33,49},{2,18},{18,34},{34,5... | collective-permute-start | bytes 6152 | tf_op jit(solution)/shard_map/ppermute | solution.py:27
  149.5 5.5 %collective-permute-start.27 = (f32[2,1,1,256]{3,2,1,0:T(1,128)S(1)}, f32[2,1,1,256]{3,2,1,0:T(1,128)S(1)}, u32[]{:S(2)}, u32[]{:S(2)}) collective-permute-start(f32[2,1,1,256]{3,2,1,0:T(1,128)S(1)} %get-tuple-element.50), channel_id=1, source_target_pairs={{16,0},{32,16},{48,32},{17,1},{33,17},{49,33},{18,2},{34,18},{50,3... | collective-permute-start | bytes 6152 | tf_op jit(solution)/shard_map/ppermute | solution.py:28
  155.2 10.2 %collective-permute-start.28 = (f32[2,1,258,1]{3,2,1,0:T(8,128)S(1)}, f32[2,1,258,1]{3,2,1,0:T(8,128)S(1)}, u32[]{:S(2)}, u32[]{:S(2)}) collective-permute-start(f32[2,1,258,1]{3,2,1,0:T(8,128)S(1)} %get-tuple-element.33), channel_id=1, source_target_pairs={{0,1},{1,2},{2,3},{3,4},{4,5},{5,6},{6,7},{7,8},{8,9},{9,10},{10,1... | collective-permute-start | bytes 6200 | tf_op jit(solution)/shard_map/ppermute | solution.py:27
  161.1 10.5 %collective-permute-start.29 = (f32[2,1,258,1]{3,2,1,0:T(8,128)S(1)}, f32[2,1,258,1]{3,2,1,0:T(8,128)S(1)}, u32[]{:S(2)}, u32[]{:S(2)}) collective-permute-start(f32[2,1,258,1]{3,2,1,0:T(8,128)S(1)} %get-tuple-element.34), channel_id=1, source_target_pairs={{1,0},{2,1},{3,2},{4,3},{5,4},{6,5},{7,6},{8,7},{9,8},{10,9},{11,1... | collective-permute-start | bytes 6200 | tf_op jit(solution)/shard_map/ppermute | solution.py:28
  172.2 10.6 %collective-permute-start.32 = (f32[2,1,1,256]{3,2,1,0:T(1,128)S(1)}, f32[2,1,1,256]{3,2,1,0:T(1,128)S(1)}, u32[]{:S(2)}, u32[]{:S(2)}) collective-permute-start(f32[2,1,1,256]{3,2,1,0:T(1,128)S(1)} %get-tuple-element.47), channel_id=1, source_target_pairs={{0,16},{16,32},{32,48},{1,17},{17,33},{33,49},{2,18},{18,34},{34,5... | collective-permute-start | bytes 6152 | tf_op jit(solution)/shard_map/ppermute | solution.py:27
  174.4 8.4 %collective-permute-start.33 = (f32[2,1,1,256]{3,2,1,0:T(1,128)S(1)}, f32[2,1,1,256]{3,2,1,0:T(1,128)S(1)}, u32[]{:S(2)}, u32[]{:S(2)}) collective-permute-start(f32[2,1,1,256]{3,2,1,0:T(1,128)S(1)} %get-tuple-element.48), channel_id=1, source_target_pairs={{16,0},{32,16},{48,32},{17,1},{33,17},{49,33},{18,2},{34,18},{50,3... | collective-permute-start | bytes 6152 | tf_op jit(solution)/shard_map/ppermute | solution.py:28
  175.7 24.4 %collective-permute-start.30 = (f32[2,1,256,256]{3,2,1,0:T(8,128)S(1)}, f32[2,1,256,256]{3,2,1,0:T(8,128)S(1)}, u32[]{:S(2)}, u32[]{:S(2)}) collective-permute-start(f32[2,1,256,256]{3,2,1,0:T(8,128)S(1)} %pad_maximum_fusion.2), channel_id=1, source_target_pairs={{0,64},{64,128},{128,192},{1,65},{65,129},{129,193},{2,66},{66,130... | collective-permute-start | bytes 1572872 | tf_op jit(solution)/shard_map/ppermute | solution.py:17
  177.7 22.5 %collective-permute-start.31 = (f32[2,1,256,256]{3,2,1,0:T(8,128)S(1)}, f32[2,1,256,256]{3,2,1,0:T(8,128)S(1)}, u32[]{:S(2)}, u32[]{:S(2)}) collective-permute-start(f32[2,1,256,256]{3,2,1,0:T(8,128)S(1)} %pad_maximum_fusion.2), channel_id=1, source_target_pairs={{64,0},{128,64},{192,128},{65,1},{129,65},{193,129},{66,2},{130,66... | collective-permute-start | bytes 1572872 | tf_op jit(solution)/shard_map/ppermute | solution.py:17
  183.0 16.7 %collective-permute-start.34 = (f32[2,1,258,1]{3,2,1,0:T(8,128)S(1)}, f32[2,1,258,1]{3,2,1,0:T(8,128)S(1)}, u32[]{:S(2)}, u32[]{:S(2)}) collective-permute-start(f32[2,1,258,1]{3,2,1,0:T(8,128)S(1)} %get-tuple-element.31), channel_id=1, source_target_pairs={{0,1},{1,2},{2,3},{3,4},{4,5},{5,6},{6,7},{7,8},{8,9},{9,10},{10,1... | collective-permute-start | bytes 6200 | tf_op jit(solution)/shard_map/ppermute | solution.py:27
  188.9 10.8 %collective-permute-start.35 = (f32[2,1,258,1]{3,2,1,0:T(8,128)S(1)}, f32[2,1,258,1]{3,2,1,0:T(8,128)S(1)}, u32[]{:S(2)}, u32[]{:S(2)}) collective-permute-start(f32[2,1,258,1]{3,2,1,0:T(8,128)S(1)} %get-tuple-element.32), channel_id=1, source_target_pairs={{1,0},{2,1},{3,2},{4,3},{5,4},{6,5},{7,6},{8,7},{9,8},{10,9},{11,1... | collective-permute-start | bytes 6200 | tf_op jit(solution)/shard_map/ppermute | solution.py:28
  200.4 5.9 %collective-permute-start.36 = (f32[2,1,1,256]{3,2,1,0:T(1,128)S(1)}, f32[2,1,1,256]{3,2,1,0:T(1,128)S(1)}, u32[]{:S(2)}, u32[]{:S(2)}) collective-permute-start(f32[2,1,1,256]{3,2,1,0:T(1,128)S(1)} %get-tuple-element.45), channel_id=1, source_target_pairs={{0,16},{16,32},{32,48},{1,17},{17,33},{33,49},{2,18},{18,34},{34,5... | collective-permute-start | bytes 6152 | tf_op jit(solution)/shard_map/ppermute | solution.py:27
  205.0 5.5 %collective-permute-start.37 = (f32[2,1,1,256]{3,2,1,0:T(1,128)S(1)}, f32[2,1,1,256]{3,2,1,0:T(1,128)S(1)}, u32[]{:S(2)}, u32[]{:S(2)}) collective-permute-start(f32[2,1,1,256]{3,2,1,0:T(1,128)S(1)} %get-tuple-element.46), channel_id=1, source_target_pairs={{16,0},{32,16},{48,32},{17,1},{33,17},{49,33},{18,2},{34,18},{50,3... | collective-permute-start | bytes 6152 | tf_op jit(solution)/shard_map/ppermute | solution.py:28
  210.7 11.2 %collective-permute-start.38 = (f32[2,1,258,1]{3,2,1,0:T(8,128)S(1)}, f32[2,1,258,1]{3,2,1,0:T(8,128)S(1)}, u32[]{:S(2)}, u32[]{:S(2)}) collective-permute-start(f32[2,1,258,1]{3,2,1,0:T(8,128)S(1)} %get-tuple-element.29), channel_id=1, source_target_pairs={{0,1},{1,2},{2,3},{3,4},{4,5},{5,6},{6,7},{7,8},{8,9},{9,10},{10,1... | collective-permute-start | bytes 6200 | tf_op jit(solution)/shard_map/ppermute | solution.py:27
  217.9 10.5 %collective-permute-start.39 = (f32[2,1,258,1]{3,2,1,0:T(8,128)S(1)}, f32[2,1,258,1]{3,2,1,0:T(8,128)S(1)}, u32[]{:S(2)}, u32[]{:S(2)}) collective-permute-start(f32[2,1,258,1]{3,2,1,0:T(8,128)S(1)} %get-tuple-element.30), channel_id=1, source_target_pairs={{1,0},{2,1},{3,2},{4,3},{5,4},{6,5},{7,6},{8,7},{9,8},{10,9},{11,1... | collective-permute-start | bytes 6200 | tf_op jit(solution)/shard_map/ppermute | solution.py:28
  229.0 3.5 %collective-permute-start.40 = (f32[2,1,1,256]{3,2,1,0:T(1,128)S(1)}, f32[2,1,1,256]{3,2,1,0:T(1,128)S(1)}, u32[]{:S(2)}, u32[]{:S(2)}) collective-permute-start(f32[2,1,1,256]{3,2,1,0:T(1,128)S(1)} %get-tuple-element.43), channel_id=1, source_target_pairs={{0,16},{16,32},{32,48},{1,17},{17,33},{33,49},{2,18},{18,34},{34,5... | collective-permute-start | bytes 6152 | tf_op jit(solution)/shard_map/ppermute | solution.py:27
  231.2 5.5 %collective-permute-start.41 = (f32[2,1,1,256]{3,2,1,0:T(1,128)S(1)}, f32[2,1,1,256]{3,2,1,0:T(1,128)S(1)}, u32[]{:S(2)}, u32[]{:S(2)}) collective-permute-start(f32[2,1,1,256]{3,2,1,0:T(1,128)S(1)} %get-tuple-element.44), channel_id=1, source_target_pairs={{16,0},{32,16},{48,32},{17,1},{33,17},{49,33},{18,2},{34,18},{50,3... | collective-permute-start | bytes 6152 | tf_op jit(solution)/shard_map/ppermute | solution.py:28
  236.9 14.1 %collective-permute-start.42 = (f32[2,1,258,1]{3,2,1,0:T(8,128)S(1)}, f32[2,1,258,1]{3,2,1,0:T(8,128)S(1)}, u32[]{:S(2)}, u32[]{:S(2)}) collective-permute-start(f32[2,1,258,1]{3,2,1,0:T(8,128)S(1)} %get-tuple-element.27), channel_id=1, source_target_pairs={{0,1},{1,2},{2,3},{3,4},{4,5},{5,6},{6,7},{7,8},{8,9},{9,10},{10,1... | collective-permute-start | bytes 6200 | tf_op jit(solution)/shard_map/ppermute | solution.py:27
  240.4 10.6 %collective-permute-start.43 = (f32[2,1,258,1]{3,2,1,0:T(8,128)S(1)}, f32[2,1,258,1]{3,2,1,0:T(8,128)S(1)}, u32[]{:S(2)}, u32[]{:S(2)}) collective-permute-start(f32[2,1,258,1]{3,2,1,0:T(8,128)S(1)} %get-tuple-element.28), channel_id=1, source_target_pairs={{1,0},{2,1},{3,2},{4,3},{5,4},{6,5},{7,6},{8,7},{9,8},{10,9},{11,1... | collective-permute-start | bytes 6200 | tf_op jit(solution)/shard_map/ppermute | solution.py:28
  251.6 3.4 %collective-permute-start.44 = (f32[2,1,1,256]{3,2,1,0:T(1,128)S(1)}, f32[2,1,1,256]{3,2,1,0:T(1,128)S(1)}, u32[]{:S(2)}, u32[]{:S(2)}) collective-permute-start(f32[2,1,1,256]{3,2,1,0:T(1,128)S(1)} %get-tuple-element.41), channel_id=1, source_target_pairs={{0,16},{16,32},{32,48},{1,17},{17,33},{33,49},{2,18},{18,34},{34,5... | collective-permute-start | bytes 6152 | tf_op jit(solution)/shard_map/ppermute | solution.py:27
  253.7 5.5 %collective-permute-start.45 = (f32[2,1,1,256]{3,2,1,0:T(1,128)S(1)}, f32[2,1,1,256]{3,2,1,0:T(1,128)S(1)}, u32[]{:S(2)}, u32[]{:S(2)}) collective-permute-start(f32[2,1,1,256]{3,2,1,0:T(1,128)S(1)} %get-tuple-element.42), channel_id=1, source_target_pairs={{16,0},{32,16},{48,32},{17,1},{33,17},{49,33},{18,2},{34,18},{50,3... | collective-permute-start | bytes 6152 | tf_op jit(solution)/shard_map/ppermute | solution.py:28
  259.4 11.3 %collective-permute-start.46 = (f32[2,1,258,1]{3,2,1,0:T(8,128)S(1)}, f32[2,1,258,1]{3,2,1,0:T(8,128)S(1)}, u32[]{:S(2)}, u32[]{:S(2)}) collective-permute-start(f32[2,1,258,1]{3,2,1,0:T(8,128)S(1)} %get-tuple-element.25), channel_id=1, source_target_pairs={{0,1},{1,2},{2,3},{3,4},{4,5},{5,6},{6,7},{7,8},{8,9},{9,10},{10,1... | collective-permute-start | bytes 6200 | tf_op jit(solution)/shard_map/ppermute | solution.py:27
  263.4 10.5 %collective-permute-start.47 = (f32[2,1,258,1]{3,2,1,0:T(8,128)S(1)}, f32[2,1,258,1]{3,2,1,0:T(8,128)S(1)}, u32[]{:S(2)}, u32[]{:S(2)}) collective-permute-start(f32[2,1,258,1]{3,2,1,0:T(8,128)S(1)} %get-tuple-element.26), channel_id=1, source_target_pairs={{1,0},{2,1},{3,2},{4,3},{5,4},{6,5},{7,6},{8,7},{9,8},{10,9},{11,1... | collective-permute-start | bytes 6200 | tf_op jit(solution)/shard_map/ppermute | solution.py:28
  (2 other events, 15.9 us)
where the time goes:
time: 278 us; the launch traced here: 276 us
  starting transfers between devices  139 us (50%)
  waiting for transfers between devices  119 us (43%)
  other arithmetic  13 us (5%)
  local copies, waits for them, and re-layouts  3.75 us (1%)
    ppermute x22, starting transfers between devices, extended(): before = lax.ppermute(last, axis, up)  89.2 us
    ppermute x22, waiting for transfers between devices, extended(): after = lax.ppermute(first, axis, down)  74.2 us
    ppermute x22, starting transfers between devices, extended(): after = lax.ppermute(first, axis, down)  38.7 us
    ppermute x22, waiting for transfers between devices, extended(): before = lax.ppermute(last, axis, up)  37.6 us
    ppermute x4, starting transfers between devices, from_behind(): lax.ppermute(value, axis, [(source, source + steps) for source in range(f...  10.9 us
    ppermute x4, waiting for transfers between devices, from_behind(): lax.ppermute(value, axis, [(source, source + steps) for source in range(f...  7.49 us
  transfers between devices with their start and end apart: 48, of which 27 were waited for; matrix products, arithmetic and copies ran while one was open for 1% of the time, Pallas kernels for 0%

commit v1 on v0

v1 whole, which is shorter than its diff:
```python
import jax
import jax.numpy as jnp
from jax import lax
from jax.experimental import pallas as pl
from jax.experimental.pallas import tpu as pltpu
from jax.sharding import PartitionSpec as P

RADIUS = 4
COUPLING = 0.25
AXES = ("sec", "row", "col")

TILE = 256
RIM = 16
EXT = TILE + 2 * RIM
BLOCKS = EXT // 8
INNER = BLOCKS - 2
GROUP = 5
FIELD_RIM = 8


def even(i, count):
    j = i ^ 1
    return j if j < count else None


def odd(i, count):
    j = ((i + 1) ^ 1) - 1
    return j if 0 <= j < count else None


def same(i, count):
    return i


def pairs(sec_of, row_of, col_of):
    secs, rows, cols = (lax.axis_size(name) for name in AXES)
    found = []
    for s in range(secs):
        for r in range(rows):
            for c in range(cols):
                to = (sec_of(s, secs), row_of(r, rows), col_of(c, cols))
                if None not in to:
                    found.append(((s * rows + r) * cols + c, (to[0] * rows + to[1]) * cols + to[2]))
    return found


def send(value, sec_of=same, row_of=same, col_of=same):
    return lax.ppermute(value, AXES, pairs(sec_of, row_of, col_of))


def earlier(s, count):
    return s - 1 if s > 0 else None


def lanes():
    return lax.broadcasted_iota(jnp.int32, (8, 128), 1)


def from_left(tiles, steps):
    rolled = [pltpu.roll(t, steps, 1) for t in tiles]
    edge = lanes() < steps
    return [jnp.where(edge, rolled[(k + 2) % 3], rolled[k]) for k in range(3)]


def from_right(tiles, steps):
    rolled = [pltpu.roll(t, 128 - steps, 1) for t in tiles]
    edge = lanes() >= 128 - steps
    return [jnp.where(edge, rolled[(k + 1) % 3], rolled[k]) for k in range(3)]


def ext_block(main, top, bottom, offset, block, k):
    cols = pl.ds(128 * k, 128)
    if block < 2:
        return top(offset + 8 * block, cols)
    if block >= BLOCKS - 2:
        return bottom(offset + 8 * (block - (BLOCKS - 2)), cols)
    return main[0, pl.ds(8 * (block - 2), 8), cols]


def halo_rows(from_odd, from_even):
    is_odd = lax.rem(lax.axis_index("row"), 2) == 1

    def top(row, cols):
        return jnp.where(is_odd, from_even[pl.ds(row, 8), cols], from_odd[pl.ds(row, 8), cols])

    def bottom(row, cols):
        return jnp.where(is_odd, from_odd[pl.ds(row, 8), cols], from_even[pl.ds(row, 8), cols])

    return top, bottom


def strip_kernel(image, stiff, later, row_o, row_e, later_o, later_e, out_o, out_e):
    top, bottom = halo_rows(row_o, row_e)
    later_top, later_bottom = halo_rows(later_o, later_e)
    is_odd = lax.rem(lax.axis_index("col"), 2) == 1
    lane = lanes()
    sources = ((image, top, bottom, 0), (stiff, top, bottom, RIM), (later, later_top, later_bottom, 0))
    for n, (main, up, down, offset) in enumerate(sources):
        left = [jnp.zeros((8, 128), jnp.float32)] * GROUP
        right = [jnp.zeros((8, 128), jnp.float32)] * GROUP
        for block in range(BLOCKS):
            g, place = divmod(block, GROUP)
            here = (lane >= 16 * g) & (lane < 16 * g + 16)
            first = ext_block(main, up, down, offset, block, 0)
            last = ext_block(main, up, down, offset, block, 1)
            first = pltpu.roll(first, 16 * g, 1) if g else first
            last = pltpu.roll(last, (16 + 16 * g) % 128, 1) if g != 7 else last
            left[place] = jnp.where(here, first, left[place])
            right[place] = jnp.where(here, last, right[place])
        for place in range(GROUP):
            rows = pl.ds(8 * (GROUP * n + place), 8)
            out_o[rows, :] = jnp.where(is_odd, right[place], left[place])
            out_e[rows, :] = jnp.where(is_odd, left[place], right[place])


def sweep(g, rhs, matrix, block):
    row = pl.multiple_of(8 * block, 8)
    here = pl.ds(row, 8)
    sums = []
    for comp in range(2):
        cur = [g[comp, k, here, :] for k in range(3)]
        up = [g[comp, k, pl.ds(row - 1, 8), :] for k in range(3)]
        down = [g[comp, k, pl.ds(row + 1, 8), :] for k in range(3)]
        left = from_left(cur, 1)
        right = from_right(cur, 1)
        sums.append([(up[k] + down[k]) + (left[k] + right[k]) for k in range(3)])
    return [
        [
            rhs[0, k, here, :] + (matrix[0, k, here, :] * sums[0][k] - matrix[1, k, here, :] * sums[1][k])
            for k in range(3)
        ],
        [
            rhs[1, k, here, :] + (matrix[2, k, here, :] * sums[1][k] - matrix[1, k, here, :] * sums[0][k])
            for k in range(3)
        ],
    ]


def clear_rims(ref, count):
    zero = jnp.zeros((8, 128), jnp.float32)
    for comp in range(count):
        for k in range(3):
            ref[comp, k, pl.ds(0, 8), :] = zero
            ref[comp, k, pl.ds(EXT - 8, 8), :] = zero


def first_kernel(
    image, stiff, later, row_o, row_e, later_o, later_e, col_o, col_e,
    tensor_out, rhs, matrix, inverse, field, sent,
    img, chg, root, prods, work,
):
    lane = lanes()
    sub = lax.broadcasted_iota(jnp.int32, (8, 128), 0)
    zero = jnp.zeros((8, 128), jnp.float32)
    s, r, c = (lax.axis_index(name) for name in AXES)
    rows, cols = lax.axis_size("row"), lax.axis_size("col")
    top, bottom = halo_rows(row_o, row_e)
    later_top, later_bottom = halo_rows(later_o, later_e)
    is_odd = lax.rem(c, 2) == 1

    for k in range(3):
        img[k, pl.ds(0, 8), :] = zero
        img[k, pl.ds(EXT + 8, 8), :] = zero

    def beside(n, block):
        g, place = divmod(block, GROUP)
        at = pl.ds(8 * (GROUP * n + place), 8)
        a, b = col_o[at, :], col_e[at, :]
        right = jnp.where(is_odd, a, b)
        left = jnp.where(is_odd, b, a)
        right = pltpu.roll(right, (128 - 16 * g) % 128, 1) if g else right
        left = pltpu.roll(left, (112 - 16 * g) % 128, 1) if g != 7 else left
        return jnp.where(lane < 16, right, jnp.where(lane >= 112, left, zero))

    for block in range(BLOCKS):
        at = pl.ds(8 * block, 8)
        for k in range(3):
            if k < 2:
                a = ext_block(image, top, bottom, 0, block, k)
                b = ext_block(later, later_top, later_bottom, 0, block, k)
                q = ext_block(stiff, top, bottom, RIM, block, k)
            else:
                a, q, b = beside(0, block), beside(1, block), beside(2, block)
            img[k, pl.ds(8 * block + 8, 8), :] = a
            chg[k, at, :] = b - a
            root[k, at, :] = jnp.sqrt(q)

    low = jnp.where(r == 0, RIM, 0)
    high = jnp.where(r == rows - 1, RIM + TILE, EXT)
    col_ok = ((lane < 16) & (c < cols - 1)) | ((lane >= 112) & (c > 0))

    def gradient(block, carry):
        row = pl.multiple_of(8 * block, 8)
        at = pl.ds(row, 8)
        here = sub + row
        row_ok = (here >= low) & (here < high)
        cur = [img[k, pl.ds(row + 8, 8), :] for k in range(3)]
        left = from_left(cur, 1)
        right = from_right(cur, 1)
        for k in range(3):
            ok = row_ok & col_ok if k == 2 else row_ok
            gx = jnp.where(ok, (right[k] - left[k]) * 0.5, 0.0)
            gy = jnp.where(ok, (img[k, pl.ds(row + 9, 8), :] - img[k, pl.ds(row + 7, 8), :]) * 0.5, 0.0)
            d = chg[k, at, :]
            prods[0, k, at, :] = gx * gx
            prods[1, k, at, :] = gx * gy
            prods[2, k, at, :] = gy * gy
            prods[3, k, at, :] = gx * d
            prods[4, k, at, :] = gy * d
        return carry

    lax.fori_loop(0, BLOCKS, gradient, 0)

    scale = jnp.where(s < lax.axis_size("sec") - 1, 1.0 / float((2 * RADIUS + 1) ** 2), 0.0)
    clear_rims(field, 2)
    clear_rims(work, 2)

    def system(block, store):
        row = pl.multiple_of(8 * block, 8)
        at = pl.ds(row, 8)
        tensor = []
        for p in range(5):
            tall = []
            for k in range(3):
                terms = [prods[p, k, pl.ds(row + d, 8), :] for d in range(-RADIUS, RADIUS + 1)]
                while len(terms) > 1:
                    terms = [sum(terms[i : i + 2]) for i in range(0, len(terms), 2)]
                tall.append(terms[0])
            two = [a + b for a, b in zip(tall, from_right(tall, 1))]
            four = [a + b for a, b in zip(two, from_right(two, 2))]
            eight = [a + b for a, b in zip(four, from_right(four, 4))]
            whole = [a + b for a, b in zip(from_left(eight, 4), from_right(tall, 4))]
            tensor.append([w * scale for w in whole])
        if store:
            for p in range(5):
                for k in range(2):
                    tensor_out[p, 0, pl.ds(pl.multiple_of(row - RIM, 8), 8), pl.ds(128 * k, 128)] = tensor[p][k]
        cur = [root[k, at, :] for k in range(3)]
        left = from_left(cur, 1)
        right = from_right(cur, 1)
        for k in range(3):
            q = cur[k]
            around = (root[k, pl.ds(row - 1, 8), :] + root[k, pl.ds(row + 1, 8), :]) + (left[k] + right[k])
            diag = q * around + 2.0 * COUPLING
            xx, xy, yy, xt, yt = (tensor[p][k] for p in range(5))
            first, second = xx + diag, yy + diag
            over = q / (first * second - xy * xy)
            a, b, d = second * over, xy * over, first * over
            rx = b * yt - a * xt
            ry = b * xt - d * yt
            rhs[0, k, at, :] = rx
            rhs[1, k, at, :] = ry
            work[0, k, at, :] = rx
            work[1, k, at, :] = ry
            matrix[0, k, at, :] = a * q
            matrix[1, k, at, :] = b * q
            matrix[2, k, at, :] = d * q
            inverse[k, at, :] = jnp.where(q > 0.0, 1.0 / q, 0.0)

    def stored(block, carry):
        system(block, True)
        return carry

    system(1, False)
    lax.fori_loop(2, BLOCKS - 2, stored, 0)
    system(BLOCKS - 2, False)

    def step(src, dst):
        def body(block, carry):
            new = sweep(src, rhs, matrix, block)
            at = pl.ds(pl.multiple_of(8 * block, 8), 8)
            for comp in range(2):
                for k in range(3):
                    dst[comp, k, at, :] = new[comp][k]
            return carry

        lax.fori_loop(1, BLOCKS - 1, body, 0)

    step(work, field)
    step(field, work)

    def last(block, carry):
        new = sweep(work, rhs, matrix, block)
        at = pl.ds(pl.multiple_of(8 * block, 8), 8)
        for comp in range(2):
            for k in range(3):
                field[comp, k, at, :] = new[comp][k]
            for k in range(2):
                base = (2 * comp + k) * 8 * INNER
                sent[pl.ds(pl.multiple_of(base + 8 * block - 8, 8), 8), :] = new[comp][k] * inverse[k, at, :]
        return carry

    lax.fori_loop(1, BLOCKS - 1, last, 0)

    for comp in range(2):
        strip = [zero] * GROUP
        for block in range(INNER):
            g, place = divmod(block, GROUP)
            at = pl.ds(8 * block + 8, 8)
            tile = field[comp, 2, at, :] * inverse[2, at, :]
            tile = pltpu.roll(tile, FIELD_RIM + 16 * g, 1)
            strip[place] = jnp.where((lane >= 16 * g) & (lane < 16 * g + 16), tile, strip[place])
        for place in range(GROUP):
            sent[pl.ds(32 * INNER + 8 * (GROUP * comp + place), 8), :] = strip[place]


def second_kernel(rhs, matrix, inverse, field, far, near, out, moved, work_a, work_b, strips):
    lane = lanes()
    zero = jnp.zeros((8, 128), jnp.float32)
    clear_rims(work_a, 2)
    clear_rims(work_b, 2)
    for comp in range(2):
        for block in range(INNER):
            g, place = divmod(block, GROUP)
            at = pl.ds(32 * INNER + 8 * (GROUP * comp + place), 8)
            tile = pltpu.roll(far[at, :] + near[at, :], 128 - FIELD_RIM - 16 * g, 1)
            strips[comp, pl.ds(8 * block, 8), :] = jnp.where((lane < FIELD_RIM) | (lane >= 128 - FIELD_RIM), tile, zero)

    def right_side(block, carry):
        at = pl.ds(pl.multiple_of(8 * block, 8), 8)
        for k in range(3):
            pair = []
            for comp in range(2):
                if k < 2:
                    base = (2 * comp + k) * 8 * INNER
                    rows = pl.ds(pl.multiple_of(base + 8 * block - 8, 8), 8)
                    value = far[rows, :] + near[rows, :]
                else:
                    value = strips[comp, pl.ds(pl.multiple_of(8 * block - 8, 8), 8), :]
                pair.append(value * (inverse[k, at, :] * COUPLING))
            a, b, d = (matrix[i, k, at, :] for i in range(3))
            moved[0, k, at, :] = rhs[0, k, at, :] + (a * pair[0] - b * pair[1])
            moved[1, k, at, :] = rhs[1, k, at, :] + (d * pair[1] - b * pair[0])
        return carry

    lax.fori_loop(1, BLOCKS - 1, right_side, 0)

    def step(src, dst):
        def body(block, carry):
            new = sweep(src, moved, matrix, block)
            at = pl.ds(pl.multiple_of(8 * block, 8), 8)
            for comp in range(2):
                for k in range(3):
                    dst[comp, k, at, :] = new[comp][k]
            return carry

        lax.fori_loop(1, BLOCKS - 1, body, 0)

    step(field, work_a)
    step(work_a, work_b)
    step(work_b, work_a)

    def last(block, carry):
        new = sweep(work_a, moved, matrix, block)
        at = pl.ds(pl.multiple_of(8 * block, 8), 8)
        for comp in range(2):
            for k in range(2):
                out[comp, 0, pl.ds(pl.multiple_of(8 * block - RIM, 8), 8), pl.ds(128 * k, 128)] = (
                    new[comp][k] * inverse[k, at, :]
                )
        return carry

    lax.fori_loop(2, BLOCKS - 2, last, 0)


def f32(*shape):
    return jax.ShapeDtypeStruct(shape, jnp.float32)


def vmem(*shape):
    return pltpu.VMEM(shape, jnp.float32)


def local(images, stiffness):
    row_odd = lax.rem(lax.axis_index("row"), 2) == 1
    tops = jnp.concatenate([images[0, :RIM], stiffness[0, :RIM]], axis=0)
    bottoms = jnp.concatenate([images[0, TILE - RIM :], stiffness[0, TILE - RIM :]], axis=0)
    to_o = jnp.where(row_odd, bottoms, tops)
    to_e = jnp.where(row_odd, tops, bottoms)
    later = send(images, sec_of=earlier)
    later_o = send(to_o, sec_of=earlier, row_of=odd)
    later_e = send(to_e, sec_of=earlier, row_of=even)
    row_o = send(to_o, row_of=odd)
    row_e = send(to_e, row_of=even)

    pieces = (images, stiffness, later, row_o, row_e, later_o, later_e)
    strip = f32(3 * GROUP * 8, 128)
    strip_o, strip_e = pl.pallas_call(strip_kernel, out_shape=(strip, strip))(*pieces)
    col_o = send(strip_o, col_of=odd)
    col_e = send(strip_e, col_of=even)

    grid = (3, EXT, 128)
    sent_rows = 32 * INNER + 16 * GROUP
    tensor, rhs, matrix, inverse, field, sent = pl.pallas_call(
        first_kernel,
        out_shape=(f32(5, 1, TILE, TILE), f32(2, *grid), f32(3, *grid), f32(*grid), f32(2, *grid), f32(sent_rows, 128)),
        scratch_shapes=[vmem(3, EXT + 16, 128), vmem(*grid), vmem(*grid), vmem(5, *grid), vmem(2, *grid)],
        compiler_params=pltpu.CompilerParams(vmem_limit_bytes=40 << 20),
    )(*pieces, col_o, col_e)

    far = send(sent, sec_of=odd)
    near = send(sent, sec_of=even)
    field = pl.pallas_call(
        second_kernel,
        out_shape=f32(2, 1, TILE, TILE),
        scratch_shapes=[vmem(2, *grid), vmem(2, *grid), vmem(2, *grid), vmem(2, 8 * INNER, 128)],
        compiler_params=pltpu.CompilerParams(vmem_limit_bytes=40 << 20),
    )(rhs, matrix, inverse, field, far, near)
    return tensor, field


def solution(mesh):
    in_specs = (P("sec", "row", "col"), P("sec", "row", "col"))
    out_specs = (P(None, "sec", "row", "col"), P(None, "sec", "row", "col"))
    return jax.shard_map(local, mesh=mesh, in_specs=in_specs, out_specs=out_specs, check_vma=False)
```

time: 278 us -> 86.1 us (0.31)
  the two profiles are of different devices: /device:TPU:120 before, /device:TPU:122 now
where the time goes in v1:
time: 86.1 us; the launch traced here: 85.4 us
  Pallas kernels  40.5 us (47%)
  waiting for transfers between devices  18.9 us (22%)
  starting transfers between devices  18.4 us (21%)
  local copies, waits for them, and re-layouts  6.78 us (8%)
    pallas_call x1, Pallas kernels, local(): pl.pallas_call(first_kernel, out_shape=(f32(5, 1, TILE, TILE), f32(2, *gr...  25.4 us
    ppermute x9, waiting for transfers between devices, send(): return lax.ppermute(value, AXES, pairs(sec_of, row_of, col_of))  18.9 us
    ppermute x9, starting transfers between devices, send(): return lax.ppermute(value, AXES, pairs(sec_of, row_of, col_of))  18.4 us
    pallas_call x1, Pallas kernels, local(): pl.pallas_call(second_kernel, out_shape=f32(2, 1, TILE, TILE), scratch_sh...  13.1 us
    unnamed x24, local copies, waits for them, and re-layouts  5.28 us
    pallas_call x1, Pallas kernels, local(): pl.pallas_call(strip_kernel, out_shape=(strip, strip))(*pieces)  2.07 us
  transfers between devices with their start and end apart: 9, of which 6 were waited for; matrix products, arithmetic and copies ran while one was open for 2% of the time, Pallas kernels for 0%

profile of v1, /device:TPU:122, one launch (start us, length us, event | category | flops | bytes accessed | tf_op | source)
XLA Modules:
  0.0 85.4 jit_solution(14227481198355497750)
XLA Ops:
  0.6 0.0 copy-start
  0.6 0.0 copy-start.1
  0.7 2.7 %collective-permute-start = (f32[1,256,256]{2,1,0:T(8,128)}, f32[1,256,256]{2,1,0:T(8,128)S(1)}, u32[]{:S(2)}, u32[]{:S(2)}) collective-permute-start(f32[1,256,256]{2,1,0:T(8,128)} %image.3), channel_id=1, source_target_pairs={{64,0},{65,1},{66,2},{67,3},{68,4},{69,5},{70,6},{71,7},{72,8},{73... | collective-permute-start | bytes 786440 | tf_op jit(solution)/shard_map/ppermute | solution.py:48
  3.4 0.8 slice_bitcast_fusion.3
  4.1 0.7 slice_bitcast_fusion.2
  4.9 2.5 %collective-permute-start.4 = (f32[32,256]{1,0:T(8,128)S(1)}, f32[32,256]{1,0:T(8,128)S(1)}, u32[]{:S(2)}, u32[]{:S(2)}) collective-permute-start(f32[32,256]{1,0:T(8,128)S(1)} %get-tuple-element.22), channel_id=1, source_target_pairs={{64,16},{65,17},{66,18},{67,19},{68,20},{69,21},{70,22},{71,23},{7... | collective-permute-start | bytes 98312 | tf_op jit(solution)/shard_map/ppermute | solution.py:48
  7.4 1.6 %collective-permute-start.2 = (f32[32,256]{1,0:T(8,128)S(1)}, f32[32,256]{1,0:T(8,128)S(1)}, u32[]{:S(2)}, u32[]{:S(2)}) collective-permute-start(f32[32,256]{1,0:T(8,128)S(1)} %get-tuple-element.22), channel_id=1, source_target_pairs={{0,16},{1,17},{2,18},{3,19},{4,20},{5,21},{6,22},{7,23},{8,24},{9,... | collective-permute-start | bytes 98312 | tf_op jit(solution)/shard_map/ppermute | solution.py:48
  9.0 2.3 %collective-permute-start.3 = (f32[32,256]{1,0:T(8,128)S(1)}, f32[32,256]{1,0:T(8,128)S(1)}, u32[]{:S(2)}, u32[]{:S(2)}) collective-permute-start(f32[32,256]{1,0:T(8,128)S(1)} %get-tuple-element.23), channel_id=1, source_target_pairs={{80,32},{81,33},{82,34},{83,35},{84,36},{85,37},{86,38},{87,39},{8... | collective-permute-start | bytes 98312 | tf_op jit(solution)/shard_map/ppermute | solution.py:48
  11.3 3.0 %collective-permute-start.1 = (f32[32,256]{1,0:T(8,128)S(1)}, f32[32,256]{1,0:T(8,128)S(1)}, u32[]{:S(2)}, u32[]{:S(2)}) collective-permute-start(f32[32,256]{1,0:T(8,128)S(1)} %get-tuple-element.23), channel_id=1, source_target_pairs={{16,32},{17,33},{18,34},{19,35},{20,36},{21,37},{22,38},{23,39},{2... | collective-permute-start | bytes 98312 | tf_op jit(solution)/shard_map/ppermute | solution.py:48
  14.3 0.0 collective-permute-done.4.later_e
  14.3 0.0 copy-start.4
  14.4 0.0 collective-permute-done.2.row_e
  14.4 0.0 copy-start.6
  14.4 0.2 collective-permute-done.3.later_o
  14.5 0.0 copy-start.8
  14.5 2.7 %collective-permute-done.1.row_o = f32[32,256]{1,0:T(8,128)S(1)} collective-permute-done((f32[32,256]{1,0:T(8,128)S(1)}, f32[32,256]{1,0:T(8,128)S(1)}, u32[]{:S(2)}, u32[]{:S(2)}) %collective-permute-start.1) | collective-permute-done | bytes 32800 | tf_op jit(solution)/shard_map/ppermute | solution.py:48
  17.2 0.0 copy-start.10
  17.2 0.0 collective-permute-done.later
  17.2 0.0 copy-done.4
  17.2 0.0 copy-done.6
  17.2 0.0 copy-done.8
  17.3 0.6 copy-done.10
  17.8 0.0 copy-start.2
  17.8 0.7 copy-done.2
  18.5 2.1 %shard_map.41 = (f32[120,128]{1,0:T(8,128)}, f32[120,128]{1,0:T(8,128)}) custom-call(f32[1,256,256]{2,1,0:T(8,128)} %image.3, f32[1,256,256]{2,1,0:T(8,128)} %stiff.3, f32[1,256,256]{2,1,0:T(8,128)} %copy-done.2, f32[32,256]{1,0:T(8,128)} %copy-done.10, f32[32,256]{1,0:T(8,128)} %copy-done.6, f32[32,256]{1,0:T(8,128)} %copy-done.8, f32[32,256]{1,0:T(8,128)} %copy-done.4), custom_call_target="tpu_custom_call" | custom-call | tf_op jit(solution)/shard_map/pallas_call | solution.py:388
  20.6 4.3 %collective-permute-start.5 = (f32[120,128]{1,0:T(8,128)}, f32[120,128]{1,0:T(8,128)S(1)}, u32[]{:S(2)}, u32[]{:S(2)}) collective-permute-start(f32[120,128]{1,0:T(8,128)} %get-tuple-element.10), channel_id=1, source_target_pairs={{1,2},{2,1},{3,4},{4,3},{5,6},{6,5},{7,8},{8,7},{9,10},{10,9},{11,... | collective-permute-start | bytes 184328 | tf_op jit(solution)/shard_map/ppermute | solution.py:48
  24.9 0.1 collective-permute-start.6
  25.0 4.1 %collective-permute-done.5.col_o = f32[120,128]{1,0:T(8,128)S(1)} collective-permute-done((f32[120,128]{1,0:T(8,128)}, f32[120,128]{1,0:T(8,128)S(1)}, u32[]{:S(2)}, u32[]{:S(2)}) %collective-permute-start.5) | collective-permute-done | bytes 61472 | tf_op jit(solution)/shard_map/ppermute | solution.py:48
  29.1 1.1 %collective-permute-done.6.col_e = f32[120,128]{1,0:T(8,128)S(1)} collective-permute-done((f32[120,128]{1,0:T(8,128)}, f32[120,128]{1,0:T(8,128)S(1)}, u32[]{:S(2)}, u32[]{:S(2)}) %collective-permute-start.6) | collective-permute-done | bytes 61472 | tf_op jit(solution)/shard_map/ppermute | solution.py:48
  30.1 0.0 copy-done
  30.2 0.0 copy-done.1
  30.2 0.0 copy-start.3
  30.2 0.9 %copy-done.3 = f32[1,256,256]{2,1,0:T(8,128)S(1)} copy-done((f32[1,256,256]{2,1,0:T(8,128)S(1)}, f32[1,256,256]{2,1,0:T(8,128)}, u32[]{:S(2)}) %copy-start.3) | copy-done | bytes 262168
  31.1 0.0 copy-start.5
  31.1 0.8 copy-done.5
  31.9 0.0 copy-start.7
  31.9 0.8 copy-done.7
  32.6 0.0 copy-start.9
  32.6 0.8 copy-done.9
  33.4 0.0 copy-start.11
  33.4 0.8 copy-done.11
  34.1 25.4 %shard_map.42 = (f32[5,1,256,256]{3,2,1,0:T(8,128)}, f32[2,3,288,128]{3,2,1,0:T(8,128)S(1)}, f32[3,3,288,128]{3,2,1,0:T(8,128)S(1)}, f32[3,288,128]{2,1,0:T(8,12...) custom-call(f32[1,256,256]{2,1,0:T(8,128)S(1)} %copy-done, f32[1,256,256]{2,1,0:T(8,128)S(1)} %copy-done.1, ...), custom_call_target="tpu_custom_call" | custom-call | tf_op jit(solution)/shard_map/pallas_call | solution.py:394
  59.5 0.0 collective-permute-start.8
  59.5 1.9 %collective-permute-start.7 = (f32[1168,128]{1,0:T(8,128)S(1)}, f32[1168,128]{1,0:T(8,128)S(1)}, u32[]{:S(2)}, u32[]{:S(2)}) collective-permute-start(f32[1168,128]{1,0:T(8,128)S(1)} %get-tuple-element.17), channel_id=1, source_target_pairs={{64,128},{65,129},{66,130},{67,131},{68,132},{69,133},{70,134},{71... | collective-permute-start | bytes 1794056 | tf_op jit(solution)/shard_map/ppermute | solution.py:48
  61.4 0.1 collective-permute-done.8.near
  61.5 10.8 %collective-permute-done.7.far = f32[1168,128]{1,0:T(8,128)S(1)} collective-permute-done((f32[1168,128]{1,0:T(8,128)S(1)}, f32[1168,128]{1,0:T(8,128)S(1)}, u32[]{:S(2)}, u32[]{:S(2)}) %collective-permute-start.7) | collective-permute-done | bytes 598048 | tf_op jit(solution)/shard_map/ppermute | solution.py:48
  72.3 13.1 %shard_map.43 = f32[2,1,256,256]{3,2,1,0:T(8,128)} custom-call(f32[2,3,288,128]{3,2,1,0:T(8,128)S(1)} %get-tuple-element.13.rhs, f32[3,3,288,128]{3,2,1,0:T(8,128)S(1)} %get-tuple-element.14.matrix, f32[3,288,128]{2,1,0:T(8,128)S(1)} %get-tuple-element.15.inverse, f32[2,3,288,128]{3,2,1,0:T(8,128)S(1)} %get-tuple-element.16.field, ...), custom_call_target="tpu_custom_call" | custom-call | tf_op jit(solution)/shard_map/pallas_call | solution.py:403
  (1 shorter events, 0.0 us)
Async XLA Ops:
  0.6 29.5 %copy-start = (f32[1,256,256]{2,1,0:T(8,128)S(1)}, f32[1,256,256]{2,1,0:T(8,128)}, u32[]{:S(2)}) copy-start(f32[1,256,256]{2,1,0:T(8,128)} %image.3) | copy-start | bytes 786436
  0.6 29.5 %copy-start.1 = (f32[1,256,256]{2,1,0:T(8,128)S(1)}, f32[1,256,256]{2,1,0:T(8,128)}, u32[]{:S(2)}) copy-start(f32[1,256,256]{2,1,0:T(8,128)} %stiff.3) | copy-start | bytes 786436
  0.7 16.6 %collective-permute-start = (f32[1,256,256]{2,1,0:T(8,128)}, f32[1,256,256]{2,1,0:T(8,128)S(1)}, u32[]{:S(2)}, u32[]{:S(2)}) collective-permute-start(f32[1,256,256]{2,1,0:T(8,128)} %image.3), channel_id=1, source_target_pairs={{64,0},{65,1},{66,2},{67,3},{68,4},{69,5},{70,6},{71,7},{72,8},{73... | collective-permute-start | bytes 786440 | tf_op jit(solution)/shard_map/ppermute | solution.py:48
  4.9 9.4 %collective-permute-start.4 = (f32[32,256]{1,0:T(8,128)S(1)}, f32[32,256]{1,0:T(8,128)S(1)}, u32[]{:S(2)}, u32[]{:S(2)}) collective-permute-start(f32[32,256]{1,0:T(8,128)S(1)} %get-tuple-element.22), channel_id=1, source_target_pairs={{64,16},{65,17},{66,18},{67,19},{68,20},{69,21},{70,22},{71,23},{7... | collective-permute-start | bytes 98312 | tf_op jit(solution)/shard_map/ppermute | solution.py:48
  7.4 6.9 %collective-permute-start.2 = (f32[32,256]{1,0:T(8,128)S(1)}, f32[32,256]{1,0:T(8,128)S(1)}, u32[]{:S(2)}, u32[]{:S(2)}) collective-permute-start(f32[32,256]{1,0:T(8,128)S(1)} %get-tuple-element.22), channel_id=1, source_target_pairs={{0,16},{1,17},{2,18},{3,19},{4,20},{5,21},{6,22},{7,23},{8,24},{9,... | collective-permute-start | bytes 98312 | tf_op jit(solution)/shard_map/ppermute | solution.py:48
  9.0 5.5 %collective-permute-start.3 = (f32[32,256]{1,0:T(8,128)S(1)}, f32[32,256]{1,0:T(8,128)S(1)}, u32[]{:S(2)}, u32[]{:S(2)}) collective-permute-start(f32[32,256]{1,0:T(8,128)S(1)} %get-tuple-element.23), channel_id=1, source_target_pairs={{80,32},{81,33},{82,34},{83,35},{84,36},{85,37},{86,38},{87,39},{8... | collective-permute-start | bytes 98312 | tf_op jit(solution)/shard_map/ppermute | solution.py:48
  11.3 5.9 %collective-permute-start.1 = (f32[32,256]{1,0:T(8,128)S(1)}, f32[32,256]{1,0:T(8,128)S(1)}, u32[]{:S(2)}, u32[]{:S(2)}) collective-permute-start(f32[32,256]{1,0:T(8,128)S(1)} %get-tuple-element.23), channel_id=1, source_target_pairs={{16,32},{17,33},{18,34},{19,35},{20,36},{21,37},{22,38},{23,39},{2... | collective-permute-start | bytes 98312 | tf_op jit(solution)/shard_map/ppermute | solution.py:48
  14.3 2.9 %copy-start.4 = (f32[32,256]{1,0:T(8,128)}, f32[32,256]{1,0:T(8,128)S(1)}, u32[]{:S(2)}) copy-start(f32[32,256]{1,0:T(8,128)S(1)} %collective-permute-done.4.later_e) | copy-start | bytes 98308
  14.4 2.9 %copy-start.6 = (f32[32,256]{1,0:T(8,128)}, f32[32,256]{1,0:T(8,128)S(1)}, u32[]{:S(2)}) copy-start(f32[32,256]{1,0:T(8,128)S(1)} %collective-permute-done.2.row_e) | copy-start | bytes 98308
  14.5 2.7 %copy-start.8 = (f32[32,256]{1,0:T(8,128)}, f32[32,256]{1,0:T(8,128)S(1)}, u32[]{:S(2)}) copy-start(f32[32,256]{1,0:T(8,128)S(1)} %collective-permute-done.3.later_o) | copy-start | bytes 98308
  17.2 0.6 copy-start.10
  17.8 0.7 copy-start.2
  20.6 8.5 %collective-permute-start.5 = (f32[120,128]{1,0:T(8,128)}, f32[120,128]{1,0:T(8,128)S(1)}, u32[]{:S(2)}, u32[]{:S(2)}) collective-permute-start(f32[120,128]{1,0:T(8,128)} %get-tuple-element.10), channel_id=1, source_target_pairs={{1,2},{2,1},{3,4},{4,3},{5,6},{6,5},{7,8},{8,7},{9,10},{10,9},{11,... | collective-permute-start | bytes 184328 | tf_op jit(solution)/shard_map/ppermute | solution.py:48
  24.9 5.2 %collective-permute-start.6 = (f32[120,128]{1,0:T(8,128)}, f32[120,128]{1,0:T(8,128)S(1)}, u32[]{:S(2)}, u32[]{:S(2)}) collective-permute-start(f32[120,128]{1,0:T(8,128)} %get-tuple-element.11), channel_id=1, source_target_pairs={{0,1},{1,0},{2,3},{3,2},{4,5},{5,4},{6,7},{7,6},{8,9},{9,8},{10,11... | collective-permute-start | bytes 184328 | tf_op jit(solution)/shard_map/ppermute | solution.py:48
  30.2 1.0 %copy-start.3 = (f32[1,256,256]{2,1,0:T(8,128)S(1)}, f32[1,256,256]{2,1,0:T(8,128)}, u32[]{:S(2)}) copy-start(f32[1,256,256]{2,1,0:T(8,128)} %copy-done.2) | copy-start | bytes 786436
  31.1 0.8 copy-start.5
  31.9 0.8 copy-start.7
  32.6 0.8 copy-start.9
  33.4 0.8 copy-start.11
  59.5 2.0 %collective-permute-start.8 = (f32[1168,128]{1,0:T(8,128)S(1)}, f32[1168,128]{1,0:T(8,128)S(1)}, u32[]{:S(2)}, u32[]{:S(2)}) collective-permute-start(f32[1168,128]{1,0:T(8,128)S(1)} %get-tuple-element.17), channel_id=1, source_target_pairs={{0,64},{1,65},{2,66},{3,67},{4,68},{5,69},{6,70},{7,71},{8,72},{9,... | collective-permute-start | bytes 1794056 | tf_op jit(solution)/shard_map/ppermute | solution.py:48
  59.5 12.8 %collective-permute-start.7 = (f32[1168,128]{1,0:T(8,128)S(1)}, f32[1168,128]{1,0:T(8,128)S(1)}, u32[]{:S(2)}, u32[]{:S(2)}) collective-permute-start(f32[1168,128]{1,0:T(8,128)S(1)} %get-tuple-element.17), channel_id=1, source_target_pairs={{64,128},{65,129},{66,130},{67,131},{68,132},{69,133},{70,134},{71... | collective-permute-start | bytes 1794056 | tf_op jit(solution)/shard_map/ppermute | solution.py:48

commit v2 on v1

v2 whole, which is shorter than its diff:
```python
import jax
import jax.numpy as jnp
from jax import lax
from jax.experimental import pallas as pl
from jax.experimental.pallas import tpu as pltpu
from jax.sharding import PartitionSpec as P

RADIUS = 4
COUPLING = 0.25
AXES = ("sec", "row", "col")

TILE = 256
RIM = 16
EXT = TILE + 2 * RIM
BLOCKS = EXT // 8
INNER = BLOCKS - 2
GROUP = 5
FIELD_RIM = 8
STRIP = GROUP * 8


def even(i, count):
    j = i ^ 1
    return j if j < count else None


def odd(i, count):
    j = ((i + 1) ^ 1) - 1
    return j if 0 <= j < count else None


def same(i, count):
    return i


def pairs(sec_of, row_of, col_of):
    secs, rows, cols = (lax.axis_size(name) for name in AXES)
    found = []
    for s in range(secs):
        for r in range(rows):
            for c in range(cols):
                to = (sec_of(s, secs), row_of(r, rows), col_of(c, cols))
                if None not in to:
                    found.append(((s * rows + r) * cols + c, (to[0] * rows + to[1]) * cols + to[2]))
    return found


def send(value, sec_of=same, row_of=same, col_of=same):
    return lax.ppermute(value, AXES, pairs(sec_of, row_of, col_of))


def earlier(s, count):
    return s - 1 if s > 0 else None


def lanes():
    return lax.broadcasted_iota(jnp.int32, (8, 128), 1)


def from_left(tiles, steps):
    rolled = [pltpu.roll(t, steps, 1) for t in tiles]
    edge = lanes() < steps
    return [jnp.where(edge, rolled[(k + 2) % 3], rolled[k]) for k in range(3)]


def from_right(tiles, steps):
    rolled = [pltpu.roll(t, 128 - steps, 1) for t in tiles]
    edge = lanes() >= 128 - steps
    return [jnp.where(edge, rolled[(k + 1) % 3], rolled[k]) for k in range(3)]


def ext_block(main, top, bottom, block, k):
    cols = pl.ds(128 * k, 128)
    if block < 2:
        return top(8 * block, cols)
    if block >= BLOCKS - 2:
        return bottom(8 * (block - (BLOCKS - 2)), cols)
    return main(8 * (block - 2), cols)


def reader(ref, offset=0):
    return lambda row, cols: ref[pl.ds(offset + row, 8), cols]


def choose(flag, a, b):
    return lambda row, cols: jnp.where(flag, a(row, cols), b(row, cols))


def is_odd(axis):
    return lax.rem(lax.axis_index(axis), 2) == 1


def prepare_kernel(image, stiff, img, root, out_o, out_e):
    flag = is_odd("row")
    for n in range(TILE // 8):
        rows = pl.ds(8 * n, 8)
        img[rows, :] = image[0, rows, :]
        root[rows, :] = jnp.sqrt(stiff[0, rows, :])
    for m, ref in enumerate((img, root)):
        for n in range(RIM // 8):
            first = ref[pl.ds(8 * n, 8), :]
            last = ref[pl.ds(TILE - RIM + 8 * n, 8), :]
            rows = pl.ds(RIM * m + 8 * n, 8)
            out_o[rows, :] = jnp.where(flag, last, first)
            out_e[rows, :] = jnp.where(flag, first, last)


def strip_kernel(img, root, row_o, row_e, out_o, out_e):
    row_flag, col_flag = is_odd("row"), is_odd("col")
    lane = lanes()
    for n, main in enumerate((img, root)):
        from_o, from_e = reader(row_o, RIM * n), reader(row_e, RIM * n)
        top, bottom = choose(row_flag, from_e, from_o), choose(row_flag, from_o, from_e)
        left = [jnp.zeros((8, 128), jnp.float32)] * GROUP
        right = [jnp.zeros((8, 128), jnp.float32)] * GROUP
        for block in range(BLOCKS):
            g, place = divmod(block, GROUP)
            here = (lane >= 16 * g) & (lane < 16 * g + 16)
            first = ext_block(reader(main), top, bottom, block, 0)
            last = ext_block(reader(main), top, bottom, block, 1)
            first = pltpu.roll(first, 16 * g, 1) if g else first
            last = pltpu.roll(last, (16 + 16 * g) % 128, 1) if g != 7 else last
            left[place] = jnp.where(here, first, left[place])
            right[place] = jnp.where(here, last, right[place])
        for place in range(GROUP):
            rows = pl.ds(STRIP * n + 8 * place, 8)
            out_o[rows, :] = jnp.where(col_flag, right[place], left[place])
            out_e[rows, :] = jnp.where(col_flag, left[place], right[place])


def rims_kernel(row_o, row_e, col_o, col_e, out):
    for m, ref in enumerate((row_o, row_e)):
        for k in range(2):
            for n in range(RIM // 8):
                out[pl.ds(RIM * (2 * m + k) + 8 * n, 8), :] = ref[pl.ds(8 * n, 8), pl.ds(128 * k, 128)]
    for m, ref in enumerate((col_o, col_e)):
        for n in range(GROUP):
            out[pl.ds(4 * RIM + STRIP * m + 8 * n, 8), :] = ref[pl.ds(8 * n, 8), :]


def side_block(from_o, from_e, flag, block):
    lane = lanes()
    g, place = divmod(block, GROUP)
    cols = pl.ds(0, 128)
    a, b = from_o(8 * place, cols), from_e(8 * place, cols)
    right = jnp.where(flag, a, b)
    left = jnp.where(flag, b, a)
    right = pltpu.roll(right, 128 - 16 * g, 1) if g else right
    left = pltpu.roll(left, (112 - 16 * g) % 128, 1) if g != 7 else left
    return jnp.where(lane < 16, right, jnp.where(lane >= 112, left, 0.0))


def window(tiles):
    three = [a + (b + c) for a, b, c in zip(tiles, from_left(tiles, 1), from_right(tiles, 1))]
    return [a + (b + c) for a, b, c in zip(three, from_left(three, 3), from_right(three, 3))]


def tall(ref, p, k, row):
    terms = [ref[p, k, pl.ds(row + d, 8), :] for d in range(-RADIUS, RADIUS + 1)]
    while len(terms) > 1:
        terms = [sum(terms[i : i + 2]) for i in range(0, len(terms), 2)]
    return terms[0]


def mean_scale():
    keep = lax.axis_index("sec") < lax.axis_size("sec") - 1
    return jnp.where(keep, 1.0 / float((2 * RADIUS + 1) ** 2), 0.0)


def matrix_kernel(img, root, row_o, row_e, col_o, col_e, ext, gx_out, gy_out, matrix, inverse, tensor, wide, sums):
    lane = lanes()
    sub = lax.broadcasted_iota(jnp.int32, (8, 128), 0)
    zero = jnp.zeros((8, 128), jnp.float32)
    row_flag, col_flag = is_odd("row"), is_odd("col")
    r, c = lax.axis_index("row"), lax.axis_index("col")
    rows, cols = lax.axis_size("row"), lax.axis_size("col")

    for k in range(3):
        ext[k, pl.ds(0, 8), :] = zero
        ext[k, pl.ds(EXT + 8, 8), :] = zero
    for n, (main, dst, shift) in enumerate(((img, ext, 8), (root, wide, 0))):
        from_o, from_e = reader(row_o, RIM * n), reader(row_e, RIM * n)
        top, bottom = choose(row_flag, from_e, from_o), choose(row_flag, from_o, from_e)
        side_o, side_e = reader(col_o, STRIP * n), reader(col_e, STRIP * n)
        for block in range(BLOCKS):
            at = pl.ds(8 * block + shift, 8)
            for k in range(2):
                dst[k, at, :] = ext_block(reader(main), top, bottom, block, k)
            dst[2, at, :] = side_block(side_o, side_e, col_flag, block)

    low = jnp.where(r == 0, RIM, 0)
    high = jnp.where(r == rows - 1, RIM + TILE, EXT)
    col_ok = ((lane < 16) & (c < cols - 1)) | ((lane >= 112) & (c > 0))

    def gradient(block, carry):
        row = pl.multiple_of(8 * block, 8)
        at = pl.ds(row, 8)
        here = sub + row
        row_ok = (here >= low) & (here < high)
        cur = [ext[k, pl.ds(row + 8, 8), :] for k in range(3)]
        left = from_left(cur, 1)
        right = from_right(cur, 1)
        gx, gy = [], []
        for k in range(3):
            ok = row_ok & col_ok if k == 2 else row_ok
            gx.append(jnp.where(ok, (right[k] - left[k]) * 0.5, 0.0))
            gy.append(jnp.where(ok, (ext[k, pl.ds(row + 9, 8), :] - ext[k, pl.ds(row + 7, 8), :]) * 0.5, 0.0))
            gx_out[k, at, :] = gx[k]
            gy_out[k, at, :] = gy[k]
        for p, (a, b) in enumerate(((gx, gx), (gx, gy), (gy, gy))):
            total = window([u * v for u, v in zip(a, b)])
            for k in range(3):
                sums[p, k, at, :] = total[k]
        return carry

    lax.fori_loop(0, BLOCKS, gradient, 0, unroll=6)
    scale = mean_scale()

    def system(block, carry):
        row = pl.multiple_of(8 * block, 8)
        at = pl.ds(row, 8)
        cur = [wide[k, at, :] for k in range(3)]
        left = from_left(cur, 1)
        right = from_right(cur, 1)
        for k in range(3):
            xx, xy, yy = (tall(sums, p, k, row) * scale for p in range(3))
            if k < 2:
                for p, value in enumerate((xx, xy, yy)):
                    tensor[p, at, pl.ds(128 * k, 128)] = value
            q = cur[k]
            around = (wide[k, pl.ds(row - 1, 8), :] + wide[k, pl.ds(row + 1, 8), :]) + (left[k] + right[k])
            diag = q * around + 2.0 * COUPLING
            first, second = xx + diag, yy + diag
            over = (q * q) / (first * second - xy * xy)
            matrix[0, k, at, :] = second * over
            matrix[1, k, at, :] = xy * over
            matrix[2, k, at, :] = first * over
            inverse[k, at, :] = jnp.where(q > 0.0, 1.0 / q, 0.0)
        return carry

    lax.fori_loop(1, BLOCKS - 1, system, 0, unroll=2)


def clear_rims(ref):
    zero = jnp.zeros((8, 128), jnp.float32)
    for comp in range(2):
        for k in range(3):
            ref[comp, k, pl.ds(0, 8), :] = zero
            ref[comp, k, pl.ds(EXT - 8, 8), :] = zero


def sweep(g, rhs, matrix, block):
    row = pl.multiple_of(8 * block, 8)
    here = pl.ds(row, 8)
    sums = []
    for comp in range(2):
        cur = [g[comp, k, here, :] for k in range(3)]
        up = [g[comp, k, pl.ds(row - 1, 8), :] for k in range(3)]
        down = [g[comp, k, pl.ds(row + 1, 8), :] for k in range(3)]
        left = from_left(cur, 1)
        right = from_right(cur, 1)
        sums.append([(up[k] + down[k]) + (left[k] + right[k]) for k in range(3)])
    first, second = [], []
    for k in range(3):
        a, b, d = (matrix[i, k, here, :] for i in range(3))
        first.append(rhs[0, k, here, :] + (a * sums[0][k] - b * sums[1][k]))
        second.append(rhs[1, k, here, :] + (d * sums[1][k] - b * sums[0][k]))
    return first, second


def step(src, dst, rhs, matrix):
    def body(block, carry):
        new = sweep(src, rhs, matrix, block)
        at = pl.ds(pl.multiple_of(8 * block, 8), 8)
        for comp in range(2):
            for k in range(3):
                dst[comp, k, at, :] = new[comp][k]
        return carry

    lax.fori_loop(1, BLOCKS - 1, body, 0, unroll=17)


def first_kernel(
    ext, gx, gy, matrix, inverse, known, later, rims,
    tensor, rhs, field, sent,
    chg, sums, work, fresh, sems,
):
    lane = lanes()
    zero = jnp.zeros((8, 128), jnp.float32)
    row_flag, col_flag = is_odd("row"), is_odd("col")
    inner = pl.ds(RIM, TILE)
    copies = [pltpu.make_async_copy(known.at[:, inner], tensor.at[pl.ds(0, 3), 0], sems.at[0])]
    copies[0].start()

    def rim_rows(base):
        return lambda row, cols: rims[pl.ds(base + RIM * (cols.start // 128) + row, 8), :]

    from_o, from_e = rim_rows(0), rim_rows(2 * RIM)
    top, bottom = choose(row_flag, from_e, from_o), choose(row_flag, from_o, from_e)
    side_o, side_e = reader(rims, 4 * RIM), reader(rims, 4 * RIM + STRIP)
    main = lambda row, cols: later[0, pl.ds(row, 8), cols]
    for block in range(BLOCKS):
        at = pl.ds(8 * block, 8)
        old = pl.ds(8 * block + 8, 8)
        for k in range(2):
            chg[k, at, :] = ext_block(main, top, bottom, block, k) - ext[k, old, :]
        chg[2, at, :] = side_block(side_o, side_e, col_flag, block) - ext[2, old, :]

    def products(block, carry):
        at = pl.ds(pl.multiple_of(8 * block, 8), 8)
        for p, grad in enumerate((gx, gy)):
            total = window([grad[k, at, :] * chg[k, at, :] for k in range(3)])
            for k in range(3):
                sums[p, k, at, :] = total[k]
        return carry

    lax.fori_loop(0, BLOCKS, products, 0, unroll=6)
    scale = mean_scale()
    clear_rims(field)
    clear_rims(work)

    def right_side(block, carry):
        row = pl.multiple_of(8 * block, 8)
        at = pl.ds(row, 8)
        for k in range(3):
            xt, yt = (tall(sums, p, k, row) * scale for p in range(2))
            if k < 2:
                fresh[0, at, pl.ds(128 * k, 128)] = xt
                fresh[1, at, pl.ds(128 * k, 128)] = yt
            a, b, d = (matrix[i, k, at, :] for i in range(3))
            inv = inverse[k, at, :]
            rx = (b * yt - a * xt) * inv
            ry = (b * xt - d * yt) * inv
            rhs[0, k, at, :] = rx
            rhs[1, k, at, :] = ry
            work[0, k, at, :] = rx
            work[1, k, at, :] = ry
        return carry

    lax.fori_loop(1, BLOCKS - 1, right_side, 0, unroll=2)
    copies.append(pltpu.make_async_copy(fresh.at[:, inner], tensor.at[pl.ds(3, 2), 0], sems.at[1]))
    copies[1].start()

    step(work, field, rhs, matrix)
    step(field, work, rhs, matrix)

    def last(block, carry):
        new = sweep(work, rhs, matrix, block)
        at = pl.ds(pl.multiple_of(8 * block, 8), 8)
        for comp in range(2):
            for k in range(3):
                field[comp, k, at, :] = new[comp][k]
            for k in range(2):
                base = (2 * comp + k) * 8 * INNER
                sent[pl.ds(pl.multiple_of(base + 8 * block - 8, 8), 8), :] = new[comp][k] * inverse[k, at, :]
        return carry

    lax.fori_loop(1, BLOCKS - 1, last, 0, unroll=17)

    for comp in range(2):
        strip = [zero] * GROUP
        for block in range(INNER):
            g, place = divmod(block, GROUP)
            at = pl.ds(8 * block + 8, 8)
            tile = field[comp, 2, at, :] * inverse[2, at, :]
            tile = pltpu.roll(tile, FIELD_RIM + 16 * g, 1)
            strip[place] = jnp.where((lane >= 16 * g) & (lane < 16 * g + 16), tile, strip[place])
        for place in range(GROUP):
            sent[pl.ds(32 * INNER + STRIP * comp + 8 * place, 8), :] = strip[place]
    for copy in copies:
        copy.wait()


def second_kernel(rhs, matrix, inverse, field, far, near, out, moved, work_a, work_b, strips):
    lane = lanes()
    clear_rims(work_a)
    clear_rims(work_b)
    for comp in range(2):
        for block in range(INNER):
            g, place = divmod(block, GROUP)
            at = pl.ds(32 * INNER + STRIP * comp + 8 * place, 8)
            tile = pltpu.roll(far[at, :] + near[at, :], 128 - FIELD_RIM - 16 * g, 1)
            strips[comp, pl.ds(8 * block, 8), :] = jnp.where((lane < FIELD_RIM) | (lane >= 128 - FIELD_RIM), tile, 0.0)

    def right_side(block, carry):
        at = pl.ds(pl.multiple_of(8 * block, 8), 8)
        for k in range(3):
            pair = []
            for comp in range(2):
                if k < 2:
                    base = (2 * comp + k) * 8 * INNER
                    rows = pl.ds(pl.multiple_of(base + 8 * block - 8, 8), 8)
                    value = far[rows, :] + near[rows, :]
                else:
                    value = strips[comp, pl.ds(pl.multiple_of(8 * block - 8, 8), 8), :]
                pair.append(value * (inverse[k, at, :] * COUPLING))
            a, b, d = (matrix[i, k, at, :] for i in range(3))
            moved[0, k, at, :] = rhs[0, k, at, :] + (a * pair[0] - b * pair[1])
            moved[1, k, at, :] = rhs[1, k, at, :] + (d * pair[1] - b * pair[0])
        return carry

    lax.fori_loop(1, BLOCKS - 1, right_side, 0, unroll=17)

    step(field, work_a, moved, matrix)
    step(work_a, work_b, moved, matrix)
    step(work_b, work_a, moved, matrix)

    def last(block, carry):
        new = sweep(work_a, moved, matrix, block)
        at = pl.ds(pl.multiple_of(8 * block, 8), 8)
        for comp in range(2):
            for k in range(2):
                out[comp, 0, pl.ds(pl.multiple_of(8 * block - RIM, 8), 8), pl.ds(128 * k, 128)] = (
                    new[comp][k] * inverse[k, at, :]
                )
        return carry

    lax.fori_loop(2, BLOCKS - 2, last, 0, unroll=16)


def f32(*shape):
    return jax.ShapeDtypeStruct(shape, jnp.float32)


def vmem(*shape):
    return pltpu.VMEM(shape, jnp.float32)


def call(kernel, out_shape, args, mib=6, us=0, **rest):
    return pl.pallas_call(
        kernel,
        out_shape=out_shape,
        compiler_params=pltpu.CompilerParams(vmem_limit_bytes=mib << 20),
        cost_estimate=pl.CostEstimate(flops=us * 1000000, bytes_accessed=us * 3000000, transcendentals=0),
        **rest,
    )(*args)


def local(images, stiffness):
    grid = (3, EXT, 128)
    edge, strip = f32(2 * RIM, TILE), f32(2 * STRIP, 128)
    later = send(images, sec_of=earlier)
    img, root, to_o, to_e = call(prepare_kernel, (f32(TILE, TILE),) * 2 + (edge,) * 2, (images, stiffness), us=1)
    row_o = send(to_o, row_of=odd)
    row_e = send(to_e, row_of=even)

    strip_o, strip_e = call(strip_kernel, (strip, strip), (img, root, row_o, row_e))
    col_o = send(strip_o, col_of=odd)
    col_e = send(strip_e, col_of=even)

    rims = call(rims_kernel, f32(4 * RIM + 2 * STRIP, 128), (row_o, row_e, col_o, col_e))
    rims = send(rims, sec_of=earlier)
    ext, gx, gy, matrix, inverse, known = call(
        matrix_kernel,
        (f32(3, EXT + 16, 128), f32(*grid), f32(*grid), f32(3, *grid), f32(*grid), f32(3, EXT, TILE)),
        (img, root, row_o, row_e, col_o, col_e),
        mib=16,
        us=4,
        scratch_shapes=[vmem(*grid), vmem(3, *grid)],
    )
    sent_rows = 32 * INNER + 2 * STRIP
    everywhere = [pl.BlockSpec(memory_space=pltpu.VMEM)] * 3
    tensor, rhs, field, sent = call(
        first_kernel,
        (f32(5, 1, TILE, TILE), f32(2, *grid), f32(2, *grid), f32(sent_rows, 128)),
        (ext, gx, gy, matrix, inverse, known, later, rims),
        mib=20,
        us=5,
        out_specs=[pl.BlockSpec(memory_space=pl.ANY)] + everywhere,
        scratch_shapes=[vmem(*grid), vmem(2, *grid), vmem(2, *grid), vmem(2, EXT, TILE), pltpu.SemaphoreType.DMA((2,))],
    )

    far = send(sent, sec_of=odd)
    near = send(sent, sec_of=even)
    field = call(
        second_kernel,
        f32(2, 1, TILE, TILE),
        (rhs, matrix, inverse, field, far, near),
        mib=20,
        us=4,
        scratch_shapes=[vmem(2, *grid), vmem(2, *grid), vmem(2, *grid), vmem(2, 8 * INNER, 128)],
    )
    return tensor, field


def solution(mesh):
    in_specs = (P("sec", "row", "col"), P("sec", "row", "col"))
    out_specs = (P(None, "sec", "row", "col"), P(None, "sec", "row", "col"))
    return jax.shard_map(local, mesh=mesh, in_specs=in_specs, out_specs=out_specs, check_vma=False)
```

time: 86.1 us -> 51.9 us (0.60)
  the two profiles are of different devices: /device:TPU:122 before, /device:TPU:120 now
where the time goes in v2:
time: 51.9 us; the launch traced here: 51.1 us
  starting transfers between devices  16.7 us (32%)
  waiting for transfers between devices  16.6 us (32%)
  Pallas kernels  15.1 us (29%)
  local copies, waits for them, and re-layouts  1.89 us (4%)
  between operations  0.74 us (1%)
    ppermute x8, starting transfers between devices, send(): return lax.ppermute(value, AXES, pairs(sec_of, row_of, col_of))  16.7 us
    ppermute x8, waiting for transfers between devices, send(): return lax.ppermute(value, AXES, pairs(sec_of, row_of, col_of))  16.6 us
    pallas_call x6, Pallas kernels, call(): pl.pallas_call(kernel, out_shape=out_shape, compiler_params=pltpu.Compile...  15.1 us
    unnamed x4, local copies, waits for them, and re-layouts  1.89 us
  transfers between devices with their start and end apart: 8, of which 4 were waited for; matrix products, arithmetic and copies ran while one was open for 0% of the time, Pallas kernels for 13%

profile of v2, /device:TPU:120, one launch (start us, length us, event | category | flops | bytes accessed | tf_op | source)
XLA Modules:
  0.0 51.1 jit_solution(12276459506490145952)
XLA Ops:
  0.6 2.6 %collective-permute-start.4 = (f32[1,256,256]{2,1,0:T(8,128)}, f32[1,256,256]{2,1,0:T(8,128)S(1)}, u32[]{:S(2)}, u32[]{:S(2)}) collective-permute-start(f32[1,256,256]{2,1,0:T(8,128)} %image.1), channel_id=1, source_target_pairs={{64,0},{65,1},{66,2},{67,3},{68,4},{69,5},{70,6},{71,7},{72,8},{73... | collective-permute-start | bytes 786440 | tf_op jit(solution)/shard_map/ppermute | solution.py:49
  3.2 0.0 copy-start
  3.2 0.9 %copy-done = f32[1,256,256]{2,1,0:T(8,128)S(1)} copy-done((f32[1,256,256]{2,1,0:T(8,128)S(1)}, f32[1,256,256]{2,1,0:T(8,128)}, u32[]{:S(2)}) %copy-start) | copy-done | bytes 262168
  4.2 0.0 copy-start.1
  4.2 0.9 %copy-done.1 = f32[1,256,256]{2,1,0:T(8,128)S(1)} copy-done((f32[1,256,256]{2,1,0:T(8,128)S(1)}, f32[1,256,256]{2,1,0:T(8,128)}, u32[]{:S(2)}) %copy-start.1) | copy-done | bytes 262168
  5.1 0.1 shard_map.41
  5.2 0.7 %collective-permute-start = (f32[32,256]{1,0:T(8,128)S(1)}, f32[32,256]{1,0:T(8,128)S(1)}, u32[]{:S(2)}, u32[]{:S(2)}) collective-permute-start(f32[32,256]{1,0:T(8,128)S(1)} %get-tuple-element.20), channel_id=1, source_target_pairs={{16,32},{17,33},{18,34},{19,35},{20,36},{21,37},{22,38},{23,39},{2... | collective-permute-start | bytes 98312 | tf_op jit(solution)/shard_map/ppermute | solution.py:49
  5.9 4.3 %collective-permute-start.1 = (f32[32,256]{1,0:T(8,128)S(1)}, f32[32,256]{1,0:T(8,128)S(1)}, u32[]{:S(2)}, u32[]{:S(2)}) collective-permute-start(f32[32,256]{1,0:T(8,128)S(1)} %get-tuple-element.21), channel_id=1, source_target_pairs={{0,16},{1,17},{2,18},{3,19},{4,20},{5,21},{6,22},{7,23},{8,24},{9,... | collective-permute-start | bytes 98312 | tf_op jit(solution)/shard_map/ppermute | solution.py:49
  10.2 0.0 collective-permute-done.row_o
  10.2 1.9 %collective-permute-done.1.row_e = f32[32,256]{1,0:T(8,128)S(1)} collective-permute-done((f32[32,256]{1,0:T(8,128)S(1)}, f32[32,256]{1,0:T(8,128)S(1)}, u32[]{:S(2)}, u32[]{:S(2)}) %collective-permute-start.1) | collective-permute-done | bytes 32800 | tf_op jit(solution)/shard_map/ppermute | solution.py:49
  12.1 0.2 shard_map.42
  12.3 4.6 %collective-permute-start.2 = (f32[80,128]{1,0:T(8,128)S(1)}, f32[80,128]{1,0:T(8,128)S(1)}, u32[]{:S(2)}, u32[]{:S(2)}) collective-permute-start(f32[80,128]{1,0:T(8,128)S(1)} %get-tuple-element.22), channel_id=1, source_target_pairs={{1,2},{2,1},{3,4},{4,3},{5,6},{6,5},{7,8},{8,7},{9,10},{10,9},{11,... | collective-permute-start | bytes 122888 | tf_op jit(solution)/shard_map/ppermute | solution.py:49
  16.8 0.1 collective-permute-start.3
  16.9 3.3 %collective-permute-done.2.col_o = f32[80,128]{1,0:T(8,128)S(1)} collective-permute-done((f32[80,128]{1,0:T(8,128)S(1)}, f32[80,128]{1,0:T(8,128)S(1)}, u32[]{:S(2)}, u32[]{:S(2)}) %collective-permute-start.2) | collective-permute-done | bytes 40992 | tf_op jit(solution)/shard_map/ppermute | solution.py:49
  20.3 0.6 %collective-permute-done.3.col_e = f32[80,128]{1,0:T(8,128)S(1)} collective-permute-done((f32[80,128]{1,0:T(8,128)S(1)}, f32[80,128]{1,0:T(8,128)S(1)}, u32[]{:S(2)}, u32[]{:S(2)}) %collective-permute-start.3) | collective-permute-done | bytes 40992 | tf_op jit(solution)/shard_map/ppermute | solution.py:49
  20.9 1.9 %collective-permute-start.5 = (f32[144,128]{1,0:T(8,128)S(1)}, f32[144,128]{1,0:T(8,128)S(1)}, u32[]{:S(2)}, u32[]{:S(2)}) collective-permute-start(f32[144,128]{1,0:T(8,128)S(1)} %shard_map.44), channel_id=1, source_target_pairs={{64,0},{65,1},{66,2},{67,3},{68,4},{69,5},{70,6},{71,7},{72,8},{73... | collective-permute-start | bytes 221192 | tf_op jit(solution)/shard_map/ppermute | solution.py:49
  22.9 6.2 %shard_map.43 = (f32[3,304,128]{2,1,0:T(8,128)S(1)}, f32[3,288,128]{2,1,0:T(8,128)S(1)}, f32[3,288,128]{2,1,0:T(8,128)S(1)}, f32[3,3,288,128]{3,2,1,0:T(8,128)S(...) custom-call(f32[256,256]{1,0:T(8,128)S(1)} %get-tuple-element.18.img, f32[256,256]{1,0:T(8,128)S(1)} %get-tuple-element.19.root, ...), custom_call_target="tpu_custom_call" | custom-call | flops 4000000 | bytes 12000000 | tf_op jit(solution)/shard_map/pallas_call | solution.py:430
  29.1 0.0 collective-permute-done.5.rims
  29.1 0.0 collective-permute-done.4.later
  29.1 5.1 %shard_map.45 = (f32[5,1,256,256]{3,2,1,0:T(8,128)}, f32[2,3,288,128]{3,2,1,0:T(8,128)S(1)}, f32[2,3,288,128]{3,2,1,0:T(8,128)S(1)}, f32[1168,128]{1,0:T(8,128)S(1)}) custom-call(f32[3,304,128]{2,1,0:T(8,128)S(1)} %get-tuple-element.24.ext, f32[3,288,128]{2,1,0:T(8,128)S(1)} %get-tuple-element.25.gx, f32[3,288,128]{2,1,0:T(8,128)S(1)} %get-tuple-element.26.gy, ...), custom_call_target="tpu_custom_call" | custom-call | flops 5000000 | bytes 15000000 | tf_op jit(solution)/shard_map/pallas_call | solution.py:430
  34.2 0.6 %collective-permute-start.7 = (f32[1168,128]{1,0:T(8,128)S(1)}, f32[1168,128]{1,0:T(8,128)S(1)}, u32[]{:S(2)}, u32[]{:S(2)}) collective-permute-start(f32[1168,128]{1,0:T(8,128)S(1)} %get-tuple-element.33), channel_id=1, source_target_pairs={{0,64},{1,65},{2,66},{3,67},{4,68},{5,69},{6,70},{7,71},{8,72},{9,... | collective-permute-start | bytes 1794056 | tf_op jit(solution)/shard_map/ppermute | solution.py:49
  34.8 2.0 %collective-permute-start.6 = (f32[1168,128]{1,0:T(8,128)S(1)}, f32[1168,128]{1,0:T(8,128)S(1)}, u32[]{:S(2)}, u32[]{:S(2)}) collective-permute-start(f32[1168,128]{1,0:T(8,128)S(1)} %get-tuple-element.33), channel_id=1, source_target_pairs={{64,128},{65,129},{66,130},{67,131},{68,132},{69,133},{70,134},{71... | collective-permute-start | bytes 1794056 | tf_op jit(solution)/shard_map/ppermute | solution.py:49
  36.8 0.0 collective-permute-done.7.near
  36.8 10.7 %collective-permute-done.6.far = f32[1168,128]{1,0:T(8,128)S(1)} collective-permute-done((f32[1168,128]{1,0:T(8,128)S(1)}, f32[1168,128]{1,0:T(8,128)S(1)}, u32[]{:S(2)}, u32[]{:S(2)}) %collective-permute-start.6) | collective-permute-done | bytes 598048 | tf_op jit(solution)/shard_map/ppermute | solution.py:49
  47.6 3.6 %shard_map.46 = f32[2,1,256,256]{3,2,1,0:T(8,128)} custom-call(f32[2,3,288,128]{3,2,1,0:T(8,128)S(1)} %get-tuple-element.31.rhs, f32[3,3,288,128]{3,2,1,0:T(8,128)S(1)} %get-tuple-element.27.matrix, f32[3,288,128]{2,1,0:T(8,128)S(1)} %get-tuple-element.28.inverse, f32[2,3,288,128]{3,2,1,0:T(8,128)S(1)} %get-tuple-element.32.field, ...), custom_call_target="tpu_custom_call" | custom-call | flops 4000000 | bytes 12000000 | tf_op jit(solution)/shard_map/pallas_call | solution.py:430
  (1 shorter events, 0.0 us)
Async XLA Ops:
  0.6 28.5 %collective-permute-start.4 = (f32[1,256,256]{2,1,0:T(8,128)}, f32[1,256,256]{2,1,0:T(8,128)S(1)}, u32[]{:S(2)}, u32[]{:S(2)}) collective-permute-start(f32[1,256,256]{2,1,0:T(8,128)} %image.1), channel_id=1, source_target_pairs={{64,0},{65,1},{66,2},{67,3},{68,4},{69,5},{70,6},{71,7},{72,8},{73... | collective-permute-start | bytes 786440 | tf_op jit(solution)/shard_map/ppermute | solution.py:49
  3.2 1.0 %copy-start = (f32[1,256,256]{2,1,0:T(8,128)S(1)}, f32[1,256,256]{2,1,0:T(8,128)}, u32[]{:S(2)}) copy-start(f32[1,256,256]{2,1,0:T(8,128)} %stiff.1) | copy-start | bytes 786436
  4.2 0.9 %copy-start.1 = (f32[1,256,256]{2,1,0:T(8,128)S(1)}, f32[1,256,256]{2,1,0:T(8,128)}, u32[]{:S(2)}) copy-start(f32[1,256,256]{2,1,0:T(8,128)} %image.1) | copy-start | bytes 786436
  5.2 5.0 %collective-permute-start = (f32[32,256]{1,0:T(8,128)S(1)}, f32[32,256]{1,0:T(8,128)S(1)}, u32[]{:S(2)}, u32[]{:S(2)}) collective-permute-start(f32[32,256]{1,0:T(8,128)S(1)} %get-tuple-element.20), channel_id=1, source_target_pairs={{16,32},{17,33},{18,34},{19,35},{20,36},{21,37},{22,38},{23,39},{2... | collective-permute-start | bytes 98312 | tf_op jit(solution)/shard_map/ppermute | solution.py:49
  5.9 6.2 %collective-permute-start.1 = (f32[32,256]{1,0:T(8,128)S(1)}, f32[32,256]{1,0:T(8,128)S(1)}, u32[]{:S(2)}, u32[]{:S(2)}) collective-permute-start(f32[32,256]{1,0:T(8,128)S(1)} %get-tuple-element.21), channel_id=1, source_target_pairs={{0,16},{1,17},{2,18},{3,19},{4,20},{5,21},{6,22},{7,23},{8,24},{9,... | collective-permute-start | bytes 98312 | tf_op jit(solution)/shard_map/ppermute | solution.py:49
  12.3 8.0 %collective-permute-start.2 = (f32[80,128]{1,0:T(8,128)S(1)}, f32[80,128]{1,0:T(8,128)S(1)}, u32[]{:S(2)}, u32[]{:S(2)}) collective-permute-start(f32[80,128]{1,0:T(8,128)S(1)} %get-tuple-element.22), channel_id=1, source_target_pairs={{1,2},{2,1},{3,4},{4,3},{5,6},{6,5},{7,8},{8,7},{9,10},{10,9},{11,... | collective-permute-start | bytes 122888 | tf_op jit(solution)/shard_map/ppermute | solution.py:49
  16.8 4.1 %collective-permute-start.3 = (f32[80,128]{1,0:T(8,128)S(1)}, f32[80,128]{1,0:T(8,128)S(1)}, u32[]{:S(2)}, u32[]{:S(2)}) collective-permute-start(f32[80,128]{1,0:T(8,128)S(1)} %get-tuple-element.23), channel_id=1, source_target_pairs={{0,1},{1,0},{2,3},{3,2},{4,5},{5,4},{6,7},{7,6},{8,9},{9,8},{10,11... | collective-permute-start | bytes 122888 | tf_op jit(solution)/shard_map/ppermute | solution.py:49
  20.9 8.1 %collective-permute-start.5 = (f32[144,128]{1,0:T(8,128)S(1)}, f32[144,128]{1,0:T(8,128)S(1)}, u32[]{:S(2)}, u32[]{:S(2)}) collective-permute-start(f32[144,128]{1,0:T(8,128)S(1)} %shard_map.44), channel_id=1, source_target_pairs={{64,0},{65,1},{66,2},{67,3},{68,4},{69,5},{70,6},{71,7},{72,8},{73... | collective-permute-start | bytes 221192 | tf_op jit(solution)/shard_map/ppermute | solution.py:49
  34.2 2.6 %collective-permute-start.7 = (f32[1168,128]{1,0:T(8,128)S(1)}, f32[1168,128]{1,0:T(8,128)S(1)}, u32[]{:S(2)}, u32[]{:S(2)}) collective-permute-start(f32[1168,128]{1,0:T(8,128)S(1)} %get-tuple-element.33), channel_id=1, source_target_pairs={{0,64},{1,65},{2,66},{3,67},{4,68},{5,69},{6,70},{7,71},{8,72},{9,... | collective-permute-start | bytes 1794056 | tf_op jit(solution)/shard_map/ppermute | solution.py:49
  34.8 12.8 %collective-permute-start.6 = (f32[1168,128]{1,0:T(8,128)S(1)}, f32[1168,128]{1,0:T(8,128)S(1)}, u32[]{:S(2)}, u32[]{:S(2)}) collective-permute-start(f32[1168,128]{1,0:T(8,128)S(1)} %get-tuple-element.33), channel_id=1, source_target_pairs={{64,128},{65,129},{66,130},{67,131},{68,132},{69,133},{70,134},{71... | collective-permute-start | bytes 1794056 | tf_op jit(solution)/shard_map/ppermute | solution.py:49

commit v3 on v2

--- a/solution.py
+++ b/solution.py
@@ -16,41 +16,62 @@
 INNER = BLOCKS - 2
 GROUP = 5
 FIELD_RIM = 8
+CUTS = 4
 STRIP = GROUP * 8
-
-
-def even(i, count):
-    j = i ^ 1
-    return j if j < count else None
-
-
-def odd(i, count):
-    j = ((i + 1) ^ 1) - 1
-    return j if 0 <= j < count else None
-
-
-def same(i, count):
-    return i
-
-
-def pairs(sec_of, row_of, col_of):
-    secs, rows, cols = (lax.axis_size(name) for name in AXES)
+RIMS = 4 * RIM + 2 * STRIP
+
+
+def sizes():
+    return [lax.axis_size(name) for name in AXES]
+
+
+def even(i):
+    return i ^ 1
+
+
+def odd(i):
+    return ((i + 1) ^ 1) - 1
+
+
+def send(value, move):
+    secs, rows, cols = sizes()
     found = []
     for s in range(secs):
         for r in range(rows):
             for c in range(cols):
-                to = (sec_of(s, secs), row_of(r, rows), col_of(c, cols))
-                if None not in to:
-                    found.append(((s * rows + r) * cols + c, (to[0] * rows + to[1]) * cols + to[2]))
-    return found
-
-
-def send(value, sec_of=same, row_of=same, col_of=same):
-    return lax.ppermute(value, AXES, pairs(sec_of, row_of, col_of))
-
-
-def earlier(s, count):
-    return s - 1 if s > 0 else None
+                to = move(s, r, c, secs, rows, cols)
+                found.append(((s * rows + r) * cols + c, (to[0] * rows + to[1]) * cols + to[2]))
+    return lax.ppermute(value, AXES, found)
+
+
+def row_even(s, r, c, secs, rows, cols):
+    return s, even(r), c
+
+
+def row_odd(s, r, c, secs, rows, cols):
+    if 0 < r < rows - 1:
+        return s, odd(r), c
+    return s, r, even(c)
+
+
+def col_even(s, r, c, secs, rows, cols):
+    return s, r, even(c)
+
+
+def col_odd(s, r, c, secs, rows, cols):
+    if 0 < c < cols - 1:
+        return s, r, odd(c)
+    return s, even(r), c
+
+
+def sec_even(s, r, c, secs, rows, cols):
+    return even(s), r, c
+
+
+def sec_odd(s, r, c, secs, rows, cols):
+    if 0 < s < secs - 1:
+        return odd(s), r, c
+    return s, even(r), c
 
 
 def lanes():
@@ -82,42 +103,59 @@
     return lambda row, cols: ref[pl.ds(offset + row, 8), cols]
 
 
-def choose(flag, a, b):
-    return lambda row, cols: jnp.where(flag, a(row, cols), b(row, cols))
+def tile_of(ref):
+    return lambda row, cols: ref[0, pl.ds(row, 8), cols]
 
 
 def is_odd(axis):
     return lax.rem(lax.axis_index(axis), 2) == 1
 
 
-def prepare_kernel(image, stiff, img, root, out_o, out_e):
+def row_halo(from_o, from_e):
     flag = is_odd("row")
-    for n in range(TILE // 8):
-        rows = pl.ds(8 * n, 8)
-        img[rows, :] = image[0, rows, :]
-        root[rows, :] = jnp.sqrt(stiff[0, rows, :])
-    for m, ref in enumerate((img, root)):
+    r = lax.axis_index("row")
+    above, below = r > 0, r < lax.axis_size("row") - 1
+
+    def top(row, cols):
+        return jnp.where(above, jnp.where(flag, from_e(row, cols), from_o(row, cols)), 0.0)
+
+    def bottom(row, cols):
+        return jnp.where(below, jnp.where(flag, from_o(row, cols), from_e(row, cols)), 0.0)
+
+    return top, bottom
+
+
+def prepare_kernel(image, stiff, img, stf, out_o, out_e, sems):
+    flag = is_odd("row")
+    copies = []
+    for n in range(CUTS):
+        at = pl.ds(TILE // CUTS * n, TILE // CUTS)
+        copies.append(pltpu.make_async_copy(image.at[0, at], img.at[0, at], sems.at[0, n]))
+        copies.append(pltpu.make_async_copy(stiff.at[0, at], stf.at[0, at], sems.at[1, n]))
+    for copy in copies:
+        copy.start()
+    for copy in copies:
+        copy.wait()
+    for m, ref in enumerate((img, stf)):
         for n in range(RIM // 8):
-            first = ref[pl.ds(8 * n, 8), :]
-            last = ref[pl.ds(TILE - RIM + 8 * n, 8), :]
             rows = pl.ds(RIM * m + 8 * n, 8)
-            out_o[rows, :] = jnp.where(flag, last, first)
-            out_e[rows, :] = jnp.where(flag, first, last)
-
-
-def strip_kernel(img, root, row_o, row_e, out_o, out_e):
-    row_flag, col_flag = is_odd("row"), is_odd("col")
+            a, b = ref[0, pl.ds(8 * n, 8), :], ref[0, pl.ds(TILE - RIM + 8 * n, 8), :]
+            out_o[rows, :] = jnp.where(flag, b, a)
+            out_e[rows, :] = jnp.where(flag, a, b)
+
+
+def strip_kernel(image, stiff, row_o, row_e, out_o, out_e):
+    col_flag = is_odd("col")
     lane = lanes()
-    for n, main in enumerate((img, root)):
-        from_o, from_e = reader(row_o, RIM * n), reader(row_e, RIM * n)
-        top, bottom = choose(row_flag, from_e, from_o), choose(row_flag, from_o, from_e)
+    for n, main in enumerate((image, stiff)):
+        top, bottom = row_halo(reader(row_o, RIM * n), reader(row_e, RIM * n))
         left = [jnp.zeros((8, 128), jnp.float32)] * GROUP
         right = [jnp.zeros((8, 128), jnp.float32)] * GROUP
         for block in range(BLOCKS):
             g, place = divmod(block, GROUP)
             here = (lane >= 16 * g) & (lane < 16 * g + 16)
-            first = ext_block(reader(main), top, bottom, block, 0)
-            last = ext_block(reader(main), top, bottom, block, 1)
+            first = ext_block(tile_of(main), top, bottom, block, 0)
+            last = ext_block(tile_of(main), top, bottom, block, 1)
             first = pltpu.roll(first, 16 * g, 1) if g else first
             last = pltpu.roll(last, (16 + 16 * g) % 128, 1) if g != 7 else last
             left[place] = jnp.where(here, first, left[place])
@@ -128,7 +166,10 @@
             out_e[rows, :] = jnp.where(col_flag, left[place], right[place])
 
 
-def rims_kernel(row_o, row_e, col_o, col_e, out):
+def section_kernel(image, row_o, row_e, col_o, col_e, out):
+    for k in range(2):
+        for n in range(TILE // 8):
+            out[pl.ds(RIMS + TILE * k + 8 * n, 8), :] = image[0, pl.ds(8 * n, 8), pl.ds(128 * k, 128)]
     for m, ref in enumerate((row_o, row_e)):
         for k in range(2):
             for n in range(RIM // 8):
@@ -138,8 +179,12 @@
             out[pl.ds(4 * RIM + STRIP * m + 8 * n, 8), :] = ref[pl.ds(8 * n, 8), :]
 
 
-def side_block(from_o, from_e, flag, block):
+def side_block(from_o, from_e, block):
     lane = lanes()
+    c = lax.axis_index("col")
+    flag = is_odd("col")
+    right_ok = (lane < 16) & (c < lax.axis_size("col") - 1)
+    left_ok = (lane >= 112) & (c > 0)
     g, place = divmod(block, GROUP)
     cols = pl.ds(0, 128)
     a, b = from_o(8 * place, cols), from_e(8 * place, cols)
@@ -147,7 +192,7 @@
     left = jnp.where(flag, b, a)
     right = pltpu.roll(right, 128 - 16 * g, 1) if g else right
     left = pltpu.roll(left, (112 - 16 * g) % 128, 1) if g != 7 else left
-    return jnp.where(lane < 16, right, jnp.where(lane >= 112, left, 0.0))
+    return jnp.where(right_ok, right, jnp.where(left_ok, left, 0.0))
 
 
 def window(tiles):
@@ -167,26 +212,27 @@
     return jnp.where(keep, 1.0 / float((2 * RADIUS + 1) ** 2), 0.0)
 
 
-def matrix_kernel(img, root, row_o, row_e, col_o, col_e, ext, gx_out, gy_out, matrix, inverse, tensor, wide, sums):
+def matrix_kernel(image, stiff, row_o, row_e, col_o, col_e, ext, gx_out, gy_out, matrix, inverse, tensor, wide, sums):
     lane = lanes()
     sub = lax.broadcasted_iota(jnp.int32, (8, 128), 0)
     zero = jnp.zeros((8, 128), jnp.float32)
-    row_flag, col_flag = is_odd("row"), is_odd("col")
     r, c = lax.axis_index("row"), lax.axis_index("col")
     rows, cols = lax.axis_size("row"), lax.axis_size("col")
 
     for k in range(3):
         ext[k, pl.ds(0, 8), :] = zero
         ext[k, pl.ds(EXT + 8, 8), :] = zero
-    for n, (main, dst, shift) in enumerate(((img, ext, 8), (root, wide, 0))):
-        from_o, from_e = reader(row_o, RIM * n), reader(row_e, RIM * n)
-        top, bottom = choose(row_flag, from_e, from_o), choose(row_flag, from_o, from_e)
+    for n, (main, dst, shift) in enumerate(((image, ext, 8), (stiff, wide, 0))):
+        top, bottom = row_halo(reader(row_o, RIM * n), reader(row_e, RIM * n))
         side_o, side_e = reader(col_o, STRIP * n), reader(col_e, STRIP * n)
         for block in range(BLOCKS):
             at = pl.ds(8 * block + shift, 8)
-            for k in range(2):
-                dst[k, at, :] = ext_block(reader(main), top, bottom, block, k)
-            dst[2, at, :] = side_block(side_o, side_e, col_flag, block)
+            for k in range(3):
+                if k < 2:
+                    value = ext_block(tile_of(main), top, bottom, block, k)
+                else:
+                    value = side_block(side_o, side_e, block)
+                dst[k, at, :] = jnp.sqrt(value) if n else value
 
     low = jnp.where(r == 0, RIM, 0)
     high = jnp.where(r == rows - 1, RIM + TILE, EXT)
@@ -281,30 +327,48 @@
 
 
 def first_kernel(
-    ext, gx, gy, matrix, inverse, known, later, rims,
+    ext, gx, gy, matrix, inverse, known, far, near,
     tensor, rhs, field, sent,
     chg, sums, work, fresh, sems,
 ):
     lane = lanes()
     zero = jnp.zeros((8, 128), jnp.float32)
-    row_flag, col_flag = is_odd("row"), is_odd("col")
+    s, secs = lax.axis_index("sec"), lax.axis_size("sec")
     inner = pl.ds(RIM, TILE)
     copies = [pltpu.make_async_copy(known.at[:, inner], tensor.at[pl.ds(0, 3), 0], sems.at[0])]
     copies[0].start()
 
+    use_far, use_near = lax.rem(s, 2) == 1, s < secs - 1
+
+    def pick(a, b):
+        return jnp.where(use_near, jnp.where(use_far, a, b), 0.0)
+
     def rim_rows(base):
-        return lambda row, cols: rims[pl.ds(base + RIM * (cols.start // 128) + row, 8), :]
-
-    from_o, from_e = rim_rows(0), rim_rows(2 * RIM)
-    top, bottom = choose(row_flag, from_e, from_o), choose(row_flag, from_o, from_e)
-    side_o, side_e = reader(rims, 4 * RIM), reader(rims, 4 * RIM + STRIP)
-    main = lambda row, cols: later[0, pl.ds(row, 8), cols]
+        def read(row, cols):
+            at = pl.ds(base + RIM * (cols.start // 128) + row, 8)
+            return pick(far[at, :], near[at, :])
+
+        return read
+
+    def rim_cols(base):
+        def read(row, cols):
+            at = pl.ds(base + row, 8)
+            return pick(far[at, :], near[at, :])
+
+        return read
+
+    def main(row, cols):
+        at = pl.ds(RIMS + TILE * (cols.start // 128) + row, 8)
+        return pick(far[at, :], near[at, :])
+
+    top, bottom = row_halo(rim_rows(0), rim_rows(2 * RIM))
+    side_o, side_e = rim_cols(4 * RIM), rim_cols(4 * RIM + STRIP)
     for block in range(BLOCKS):
         at = pl.ds(8 * block, 8)
         old = pl.ds(8 * block + 8, 8)
         for k in range(2):
             chg[k, at, :] = ext_block(main, top, bottom, block, k) - ext[k, old, :]
-        chg[2, at, :] = side_block(side_o, side_e, col_flag, block) - ext[2, old, :]
+        chg[2, at, :] = side_block(side_o, side_e, block) - ext[2, old, :]
 
     def products(block, carry):
         at = pl.ds(pl.multiple_of(8 * block, 8), 8)
@@ -373,13 +437,19 @@
 
 def second_kernel(rhs, matrix, inverse, field, far, near, out, moved, work_a, work_b, strips):
     lane = lanes()
+    s = lax.axis_index("sec")
+    inside = (s > 0) & (s < lax.axis_size("sec") - 1)
+
+    def both(at):
+        return jnp.where(inside, far[at, :], 0.0) + near[at, :]
+
     clear_rims(work_a)
     clear_rims(work_b)
     for comp in range(2):
         for block in range(INNER):
             g, place = divmod(block, GROUP)
             at = pl.ds(32 * INNER + STRIP * comp + 8 * place, 8)
-            tile = pltpu.roll(far[at, :] + near[at, :], 128 - FIELD_RIM - 16 * g, 1)
+            tile = pltpu.roll(both(at), 128 - FIELD_RIM - 16 * g, 1)
             strips[comp, pl.ds(8 * block, 8), :] = jnp.where((lane < FIELD_RIM) | (lane >= 128 - FIELD_RIM), tile, 0.0)
 
     def right_side(block, carry):
@@ -390,7 +460,7 @@
                 if k < 2:
                     base = (2 * comp + k) * 8 * INNER
                     rows = pl.ds(pl.multiple_of(base + 8 * block - 8, 8), 8)
-                    value = far[rows, :] + near[rows, :]
+                    value = both(rows)
                 else:
                     value = strips[comp, pl.ds(pl.multiple_of(8 * block - 8, 8), 8), :]
                 pair.append(value * (inverse[k, at, :] * COUPLING))
@@ -439,21 +509,29 @@
 def local(images, stiffness):
     grid = (3, EXT, 128)
     edge, strip = f32(2 * RIM, TILE), f32(2 * STRIP, 128)
-    later = send(images, sec_of=earlier)
-    img, root, to_o, to_e = call(prepare_kernel, (f32(TILE, TILE),) * 2 + (edge,) * 2, (images, stiffness), us=1)
-    row_o = send(to_o, row_of=odd)
-    row_e = send(to_e, row_of=even)
-
-    strip_o, strip_e = call(strip_kernel, (strip, strip), (img, root, row_o, row_e))
-    col_o = send(strip_o, col_of=odd)
-    col_e = send(strip_e, col_of=even)
-
-    rims = call(rims_kernel, f32(4 * RIM + 2 * STRIP, 128), (row_o, row_e, col_o, col_e))
-    rims = send(rims, sec_of=earlier)
+    in_hbm = pl.BlockSpec(memory_space=pltpu.HBM)
+    tile = f32(1, TILE, TILE)
+    images, stiffness, to_o, to_e = call(
+        prepare_kernel,
+        (tile, tile, edge, edge),
+        [pltpu.with_memory_space_constraint(x, pltpu.HBM) for x in (images, stiffness)],
+        in_specs=[in_hbm, in_hbm],
+        scratch_shapes=[pltpu.SemaphoreType.DMA((2, CUTS))],
+    )
+    row_o = send(to_o, row_odd)
+    row_e = send(to_e, row_even)
+
+    strip_o, strip_e = call(strip_kernel, (strip, strip), (images, stiffness, row_o, row_e))
+    col_o = send(strip_o, col_odd)
+    col_e = send(strip_e, col_even)
+
+    section = call(section_kernel, f32(RIMS + 2 * TILE, 128), (images, row_o, row_e, col_o, col_e))
+    later_far = send(section, sec_odd)
+    later_near = send(section, sec_even)
     ext, gx, gy, matrix, inverse, known = call(
         matrix_kernel,
         (f32(3, EXT + 16, 128), f32(*grid), f32(*grid), f32(3, *grid), f32(*grid), f32(3, EXT, TILE)),
-        (img, root, row_o, row_e, col_o, col_e),
+        (images, stiffness, row_o, row_e, col_o, col_e),
         mib=16,
         us=4,
         scratch_shapes=[vmem(*grid), vmem(3, *grid)],
@@ -463,15 +541,15 @@
     tensor, rhs, field, sent = call(
         first_kernel,
         (f32(5, 1, TILE, TILE), f32(2, *grid), f32(2, *grid), f32(sent_rows, 128)),
-        (ext, gx, gy, matrix, inverse, known, later, rims),
+        (ext, gx, gy, matrix, inverse, known, later_far, later_near),
         mib=20,
         us=5,
         out_specs=[pl.BlockSpec(memory_space=pl.ANY)] + everywhere,
         scratch_shapes=[vmem(*grid), vmem(2, *grid), vmem(2, *grid), vmem(2, EXT, TILE), pltpu.SemaphoreType.DMA((2,))],
     )
 
-    far = send(sent, sec_of=odd)
-    near = send(sent, sec_of=even)
+    far = send(sent, sec_odd)
+    near = send(sent, sec_even)
     field = call(
         second_kernel,
         f32(2, 1, TILE, TILE),

time: 51.9 us -> 43.9 us (0.85)
  the two profiles are of different devices: /device:TPU:120 before, /device:TPU:99 now
where the time goes in v3:
time: 43.9 us; the launch traced here: 43.8 us
  Pallas kernels  16.2 us (37%)
  starting transfers between devices  13.8 us (31%)
  waiting for transfers between devices  13.1 us (30%)
  between operations  0.7 us (2%)
    pallas_call x6, Pallas kernels, call(): pl.pallas_call(kernel, out_shape=out_shape, compiler_params=pltpu.Compile...  16.2 us
    ppermute x8, starting transfers between devices, send(): return lax.ppermute(value, AXES, found)  13.8 us
    ppermute x8, waiting for transfers between devices, send(): return lax.ppermute(value, AXES, found)  13.1 us
  transfers between devices with their start and end apart: 8, of which 5 were waited for; matrix products, arithmetic and copies ran while one was open for 0% of the time, Pallas kernels for 14%

profile of v3, /device:TPU:99, one launch (start us, length us, event | category | flops | bytes accessed | tf_op | source)
XLA Modules:
  0.0 43.8 jit_solution(3427180940531243700)
XLA Ops:
  0.6 1.1 %shard_map.41 = (f32[1,256,256]{2,1,0:T(8,128)S(1)}, f32[1,256,256]{2,1,0:T(8,128)S(1)}, f32[32,256]{1,0:T(8,128)S(1)}, f32[32,256]{1,0:T(8,128)S(1)}) custom-call(f32[1,256,256]{2,1,0:T(8,128)} %image.1, f32[1,256,256]{2,1,0:T(8,128)} %stiff.1), custom_call_target="tpu_custom_call" | custom-call | tf_op jit(solution)/shard_map/pallas_call | solution.py:500
  1.8 1.3 %collective-permute-start = (f32[32,256]{1,0:T(8,128)S(1)}, f32[32,256]{1,0:T(8,128)S(1)}, u32[]{:S(2)}, u32[]{:S(2)}) collective-permute-start(f32[32,256]{1,0:T(8,128)S(1)} %get-tuple-element.20), channel_id=1, source_target_pairs={{0,1},{1,0},{2,3},{3,2},{4,5},{5,4},{6,7},{7,6},{8,9},{9,8},{10,11... | collective-permute-start | bytes 98312 | tf_op jit(solution)/shard_map/ppermute | solution.py:44
  3.1 0.3 collective-permute-start.1
  3.4 1.2 %collective-permute-done.row_o = f32[32,256]{1,0:T(8,128)S(1)} collective-permute-done((f32[32,256]{1,0:T(8,128)S(1)}, f32[32,256]{1,0:T(8,128)S(1)}, u32[]{:S(2)}, u32[]{:S(2)}) %collective-permute-start) | collective-permute-done | bytes 32800 | tf_op jit(solution)/shard_map/ppermute | solution.py:44
  4.6 1.4 %collective-permute-done.1.row_e = f32[32,256]{1,0:T(8,128)S(1)} collective-permute-done((f32[32,256]{1,0:T(8,128)S(1)}, f32[32,256]{1,0:T(8,128)S(1)}, u32[]{:S(2)}, u32[]{:S(2)}) %collective-permute-start.1) | collective-permute-done | bytes 32800 | tf_op jit(solution)/shard_map/ppermute | solution.py:44
  6.1 0.2 shard_map.42
  6.3 0.9 %collective-permute-start.2 = (f32[80,128]{1,0:T(8,128)S(1)}, f32[80,128]{1,0:T(8,128)S(1)}, u32[]{:S(2)}, u32[]{:S(2)}) collective-permute-start(f32[80,128]{1,0:T(8,128)S(1)} %get-tuple-element.22), channel_id=1, source_target_pairs={{0,16},{1,2},{2,1},{3,4},{4,3},{5,6},{6,5},{7,8},{8,7},{9,10},{10,... | collective-permute-start | bytes 122888 | tf_op jit(solution)/shard_map/ppermute | solution.py:44
  7.2 3.2 %collective-permute-start.3 = (f32[80,128]{1,0:T(8,128)S(1)}, f32[80,128]{1,0:T(8,128)S(1)}, u32[]{:S(2)}, u32[]{:S(2)}) collective-permute-start(f32[80,128]{1,0:T(8,128)S(1)} %get-tuple-element.23), channel_id=1, source_target_pairs={{0,1},{1,0},{2,3},{3,2},{4,5},{5,4},{6,7},{7,6},{8,9},{9,8},{10,11... | collective-permute-start | bytes 122888 | tf_op jit(solution)/shard_map/ppermute | solution.py:44
  10.4 0.0 collective-permute-done.2.col_o
  10.4 1.4 %collective-permute-done.3.col_e = f32[80,128]{1,0:T(8,128)S(1)} collective-permute-done((f32[80,128]{1,0:T(8,128)S(1)}, f32[80,128]{1,0:T(8,128)S(1)}, u32[]{:S(2)}, u32[]{:S(2)}) %collective-permute-start.3) | collective-permute-done | bytes 40992 | tf_op jit(solution)/shard_map/ppermute | solution.py:44
  11.8 3.1 %collective-permute-start.5 = (f32[656,128]{1,0:T(8,128)S(1)}, f32[656,128]{1,0:T(8,128)S(1)}, u32[]{:S(2)}, u32[]{:S(2)}) collective-permute-start(f32[656,128]{1,0:T(8,128)S(1)} %shard_map.44), channel_id=1, source_target_pairs={{0,64},{1,65},{2,66},{3,67},{4,68},{5,69},{6,70},{7,71},{8,72},{9,... | collective-permute-start | bytes 1007624 | tf_op jit(solution)/shard_map/ppermute | solution.py:44
  14.9 2.9 %collective-permute-start.4 = (f32[656,128]{1,0:T(8,128)S(1)}, f32[656,128]{1,0:T(8,128)S(1)}, u32[]{:S(2)}, u32[]{:S(2)}) collective-permute-start(f32[656,128]{1,0:T(8,128)S(1)} %shard_map.44), channel_id=1, source_target_pairs={{0,16},{1,17},{2,18},{3,19},{4,20},{5,21},{6,22},{7,23},{8,24},{9,... | collective-permute-start | bytes 1007624 | tf_op jit(solution)/shard_map/ppermute | solution.py:44
  17.8 6.2 %shard_map.43 = (f32[3,304,128]{2,1,0:T(8,128)S(1)}, f32[3,288,128]{2,1,0:T(8,128)S(1)}, f32[3,288,128]{2,1,0:T(8,128)S(1)}, f32[3,3,288,128]{3,2,1,0:T(8,128)S(...) custom-call(f32[1,256,256]{2,1,0:T(8,128)S(1)} %get-tuple-element.18.image, ...), custom_call_target="tpu_custom_call" | custom-call | flops 4000000 | bytes 12000000 | tf_op jit(solution)/shard_map/pallas_call | solution.py:500
  24.1 0.0 collective-permute-done.5.near
  24.1 0.0 collective-permute-done.4.far
  24.1 5.0 %shard_map.45 = (f32[5,1,256,256]{3,2,1,0:T(8,128)}, f32[2,3,288,128]{3,2,1,0:T(8,128)S(1)}, f32[2,3,288,128]{3,2,1,0:T(8,128)S(1)}, f32[1168,128]{1,0:T(8,128)S(1)}) custom-call(f32[3,304,128]{2,1,0:T(8,128)S(1)} %get-tuple-element.24.ext, f32[3,288,128]{2,1,0:T(8,128)S(1)} %get-tuple-element.25.gx, f32[3,288,128]{2,1,0:T(8,128)S(1)} %get-tuple-element.26.gy, ...), custom_call_target="tpu_custom_call" | custom-call | flops 5000000 | bytes 15000000 | tf_op jit(solution)/shard_map/pallas_call | solution.py:500
  29.1 0.1 collective-permute-start.7
  29.2 1.9 %collective-permute-start.6 = (f32[1168,128]{1,0:T(8,128)S(1)}, f32[1168,128]{1,0:T(8,128)S(1)}, u32[]{:S(2)}, u32[]{:S(2)}) collective-permute-start(f32[1168,128]{1,0:T(8,128)S(1)} %get-tuple-element.33), channel_id=1, source_target_pairs={{0,16},{1,17},{2,18},{3,19},{4,20},{5,21},{6,22},{7,23},{8,24},{9,... | collective-permute-start | bytes 1794056 | tf_op jit(solution)/shard_map/ppermute | solution.py:44
  31.1 0.1 collective-permute-done.7.near
  31.2 9.0 %collective-permute-done.6.far = f32[1168,128]{1,0:T(8,128)S(1)} collective-permute-done((f32[1168,128]{1,0:T(8,128)S(1)}, f32[1168,128]{1,0:T(8,128)S(1)}, u32[]{:S(2)}, u32[]{:S(2)}) %collective-permute-start.6) | collective-permute-done | bytes 598048 | tf_op jit(solution)/shard_map/ppermute | solution.py:44
  40.2 3.6 %shard_map.46 = f32[2,1,256,256]{3,2,1,0:T(8,128)} custom-call(f32[2,3,288,128]{3,2,1,0:T(8,128)S(1)} %get-tuple-element.31.rhs, f32[3,3,288,128]{3,2,1,0:T(8,128)S(1)} %get-tuple-element.27.matrix, f32[3,288,128]{2,1,0:T(8,128)S(1)} %get-tuple-element.28.inverse, f32[2,3,288,128]{3,2,1,0:T(8,128)S(1)} %get-tuple-element.32.field, ...), custom_call_target="tpu_custom_call" | custom-call | flops 4000000 | bytes 12000000 | tf_op jit(solution)/shard_map/pallas_call | solution.py:500
  (1 shorter events, 0.0 us)
Async XLA Ops:
  1.8 2.9 %collective-permute-start = (f32[32,256]{1,0:T(8,128)S(1)}, f32[32,256]{1,0:T(8,128)S(1)}, u32[]{:S(2)}, u32[]{:S(2)}) collective-permute-start(f32[32,256]{1,0:T(8,128)S(1)} %get-tuple-element.20), channel_id=1, source_target_pairs={{0,1},{1,0},{2,3},{3,2},{4,5},{5,4},{6,7},{7,6},{8,9},{9,8},{10,11... | collective-permute-start | bytes 98312 | tf_op jit(solution)/shard_map/ppermute | solution.py:44
  3.1 3.0 %collective-permute-start.1 = (f32[32,256]{1,0:T(8,128)S(1)}, f32[32,256]{1,0:T(8,128)S(1)}, u32[]{:S(2)}, u32[]{:S(2)}) collective-permute-start(f32[32,256]{1,0:T(8,128)S(1)} %get-tuple-element.21), channel_id=1, source_target_pairs={{0,16},{1,17},{2,18},{3,19},{4,20},{5,21},{6,22},{7,23},{8,24},{9,... | collective-permute-start | bytes 98312 | tf_op jit(solution)/shard_map/ppermute | solution.py:44
  6.3 4.1 %collective-permute-start.2 = (f32[80,128]{1,0:T(8,128)S(1)}, f32[80,128]{1,0:T(8,128)S(1)}, u32[]{:S(2)}, u32[]{:S(2)}) collective-permute-start(f32[80,128]{1,0:T(8,128)S(1)} %get-tuple-element.22), channel_id=1, source_target_pairs={{0,16},{1,2},{2,1},{3,4},{4,3},{5,6},{6,5},{7,8},{8,7},{9,10},{10,... | collective-permute-start | bytes 122888 | tf_op jit(solution)/shard_map/ppermute | solution.py:44
  7.2 4.6 %collective-permute-start.3 = (f32[80,128]{1,0:T(8,128)S(1)}, f32[80,128]{1,0:T(8,128)S(1)}, u32[]{:S(2)}, u32[]{:S(2)}) collective-permute-start(f32[80,128]{1,0:T(8,128)S(1)} %get-tuple-element.23), channel_id=1, source_target_pairs={{0,1},{1,0},{2,3},{3,2},{4,5},{5,4},{6,7},{7,6},{8,9},{9,8},{10,11... | collective-permute-start | bytes 122888 | tf_op jit(solution)/shard_map/ppermute | solution.py:44
  11.8 12.3 %collective-permute-start.5 = (f32[656,128]{1,0:T(8,128)S(1)}, f32[656,128]{1,0:T(8,128)S(1)}, u32[]{:S(2)}, u32[]{:S(2)}) collective-permute-start(f32[656,128]{1,0:T(8,128)S(1)} %shard_map.44), channel_id=1, source_target_pairs={{0,64},{1,65},{2,66},{3,67},{4,68},{5,69},{6,70},{7,71},{8,72},{9,... | collective-permute-start | bytes 1007624 | tf_op jit(solution)/shard_map/ppermute | solution.py:44
  14.9 9.2 %collective-permute-start.4 = (f32[656,128]{1,0:T(8,128)S(1)}, f32[656,128]{1,0:T(8,128)S(1)}, u32[]{:S(2)}, u32[]{:S(2)}) collective-permute-start(f32[656,128]{1,0:T(8,128)S(1)} %shard_map.44), channel_id=1, source_target_pairs={{0,16},{1,17},{2,18},{3,19},{4,20},{5,21},{6,22},{7,23},{8,24},{9,... | collective-permute-start | bytes 1007624 | tf_op jit(solution)/shard_map/ppermute | solution.py:44
  29.1 2.1 %collective-permute-start.7 = (f32[1168,128]{1,0:T(8,128)S(1)}, f32[1168,128]{1,0:T(8,128)S(1)}, u32[]{:S(2)}, u32[]{:S(2)}) collective-permute-start(f32[1168,128]{1,0:T(8,128)S(1)} %get-tuple-element.33), channel_id=1, source_target_pairs={{0,64},{1,65},{2,66},{3,67},{4,68},{5,69},{6,70},{7,71},{8,72},{9,... | collective-permute-start | bytes 1794056 | tf_op jit(solution)/shard_map/ppermute | solution.py:44
  29.2 11.0 %collective-permute-start.6 = (f32[1168,128]{1,0:T(8,128)S(1)}, f32[1168,128]{1,0:T(8,128)S(1)}, u32[]{:S(2)}, u32[]{:S(2)}) collective-permute-start(f32[1168,128]{1,0:T(8,128)S(1)} %get-tuple-element.33), channel_id=1, source_target_pairs={{0,16},{1,17},{2,18},{3,19},{4,20},{5,21},{6,22},{7,23},{8,24},{9,... | collective-permute-start | bytes 1794056 | tf_op jit(solution)/shard_map/ppermute | solution.py:44

commit v4 on v3

--- a/solution.py
+++ b/solution.py
@@ -1,3 +1,5 @@
+import functools
+
 import jax
 import jax.numpy as jnp
 from jax import lax
@@ -16,6 +18,9 @@
 INNER = BLOCKS - 2
 GROUP = 5
 FIELD_RIM = 8
+HALF = INNER // 2
+FOLD = 3
+SENT = 32 * HALF + 16 * FOLD
 CUTS = 4
 STRIP = GROUP * 8
 RIMS = 4 * RIM + 2 * STRIP
@@ -166,10 +171,7 @@
             out_e[rows, :] = jnp.where(col_flag, left[place], right[place])
 
 
-def section_kernel(image, row_o, row_e, col_o, col_e, out):
-    for k in range(2):
-        for n in range(TILE // 8):
-            out[pl.ds(RIMS + TILE * k + 8 * n, 8), :] = image[0, pl.ds(8 * n, 8), pl.ds(128 * k, 128)]
+def rims_kernel(row_o, row_e, col_o, col_e, out):
     for m, ref in enumerate((row_o, row_e)):
         for k in range(2):
             for n in range(RIM // 8):
@@ -195,9 +197,29 @@
     return jnp.where(right_ok, right, jnp.where(left_ok, left, 0.0))
 
 
-def window(tiles):
-    three = [a + (b + c) for a, b, c in zip(tiles, from_left(tiles, 1), from_right(tiles, 1))]
-    return [a + (b + c) for a, b, c in zip(three, from_left(three, 3), from_right(three, 3))]
+def band_kernel(start, band):
+    wide = 3 * 128
+    for n in range(wide // 8):
+        a = lax.broadcasted_iota(jnp.int32, (8, wide), 0) + 8 * n
+        b = lax.broadcasted_iota(jnp.int32, (8, wide), 1)
+        apart = jnp.abs(a - b)
+        near = (apart <= RADIUS) | (apart >= wide - RADIUS)
+        band[pl.ds(8 * n, 8), :] = jnp.where(near, 1.0, 0.0)
+
+
+def spread(prods, band, sums, count):
+    ones = band[...].astype(jnp.bfloat16)
+    rest = prods[...]
+    total = None
+    for part in range(3):
+        piece = rest.astype(jnp.bfloat16)
+        if part < 2:
+            rest = rest - piece.astype(jnp.float32)
+        found = jnp.dot(piece, ones, preferred_element_type=jnp.float32)
+        total = found if total is None else total + found
+    for p in range(count):
+        for k in range(3):
+            sums[p, k] = total[EXT * p : EXT * (p + 1), 128 * k : 128 * (k + 1)]
 
 
 def tall(ref, p, k, row):
@@ -212,7 +234,11 @@
     return jnp.where(keep, 1.0 / float((2 * RADIUS + 1) ** 2), 0.0)
 
 
-def matrix_kernel(image, stiff, row_o, row_e, col_o, col_e, ext, gx_out, gy_out, matrix, inverse, tensor, wide, sums):
+def matrix_kernel(
+    image, stiff, row_o, row_e, col_o, col_e, band,
+    ext, gx_out, gy_out, matrix, inverse, tensor,
+    wide, sums, prods,
+):
     lane = lanes()
     sub = lax.broadcasted_iota(jnp.int32, (8, 128), 0)
     zero = jnp.zeros((8, 128), jnp.float32)
@@ -254,12 +280,13 @@
             gx_out[k, at, :] = gx[k]
             gy_out[k, at, :] = gy[k]
         for p, (a, b) in enumerate(((gx, gx), (gx, gy), (gy, gy))):
-            total = window([u * v for u, v in zip(a, b)])
+            rows_at = pl.ds(pl.multiple_of(EXT * p + row, 8), 8)
             for k in range(3):
-                sums[p, k, at, :] = total[k]
+                prods[rows_at, pl.ds(128 * k, 128)] = a[k] * b[k]
         return carry
 
-    lax.fori_loop(0, BLOCKS, gradient, 0, unroll=6)
+    lax.fori_loop(0, BLOCKS, gradient, 0, unroll=12)
+    spread(prods, band, sums, 3)
     scale = mean_scale()
 
     def system(block, carry):
@@ -284,7 +311,7 @@
             inverse[k, at, :] = jnp.where(q > 0.0, 1.0 / q, 0.0)
         return carry
 
-    lax.fori_loop(1, BLOCKS - 1, system, 0, unroll=2)
+    lax.fori_loop(1, BLOCKS - 1, system, 0, unroll=INNER)
 
 
 def clear_rims(ref):
@@ -314,7 +341,7 @@
     return first, second
 
 
-def step(src, dst, rhs, matrix):
+def step(src, dst, rhs, matrix, low=1, high=BLOCKS - 2):
     def body(block, carry):
         new = sweep(src, rhs, matrix, block)
         at = pl.ds(pl.multiple_of(8 * block, 8), 8)
@@ -323,13 +350,13 @@
                 dst[comp, k, at, :] = new[comp][k]
         return carry
 
-    lax.fori_loop(1, BLOCKS - 1, body, 0, unroll=17)
+    lax.fori_loop(low, high + 1, body, 0, unroll=(high + 1 - low) // 2)
 
 
 def first_kernel(
-    ext, gx, gy, matrix, inverse, known, far, near,
-    tensor, rhs, field, sent,
-    chg, sums, work, fresh, sems,
+    ext, gx, gy, matrix, inverse, known, later_far, later_near, far, near, band,
+    tensor, rhs, field, sent_a, sent_b,
+    chg, sums, prods, work, fresh, sems,
 ):
     lane = lanes()
     zero = jnp.zeros((8, 128), jnp.float32)
@@ -358,8 +385,8 @@
         return read
 
     def main(row, cols):
-        at = pl.ds(RIMS + TILE * (cols.start // 128) + row, 8)
-        return pick(far[at, :], near[at, :])
+        at = pl.ds(row, 8)
+        return pick(later_far[0, at, cols], later_near[0, at, cols])
 
     top, bottom = row_halo(rim_rows(0), rim_rows(2 * RIM))
     side_o, side_e = rim_cols(4 * RIM), rim_cols(4 * RIM + STRIP)
@@ -371,14 +398,16 @@
         chg[2, at, :] = side_block(side_o, side_e, block) - ext[2, old, :]
 
     def products(block, carry):
-        at = pl.ds(pl.multiple_of(8 * block, 8), 8)
+        row = pl.multiple_of(8 * block, 8)
+        at = pl.ds(row, 8)
         for p, grad in enumerate((gx, gy)):
-            total = window([grad[k, at, :] * chg[k, at, :] for k in range(3)])
+            rows_at = pl.ds(pl.multiple_of(EXT * p + row, 8), 8)
             for k in range(3):
-                sums[p, k, at, :] = total[k]
+                prods[rows_at, pl.ds(128 * k, 128)] = grad[k, at, :] * chg[k, at, :]
         return carry
 
     lax.fori_loop(0, BLOCKS, products, 0, unroll=6)
+    spread(prods, band, sums, 2)
     scale = mean_scale()
     clear_rims(field)
     clear_rims(work)
@@ -401,76 +430,83 @@
             work[1, k, at, :] = ry
         return carry
 
-    lax.fori_loop(1, BLOCKS - 1, right_side, 0, unroll=2)
+    lax.fori_loop(1, BLOCKS - 1, right_side, 0, unroll=17)
     copies.append(pltpu.make_async_copy(fresh.at[:, inner], tensor.at[pl.ds(3, 2), 0], sems.at[1]))
     copies[1].start()
 
     step(work, field, rhs, matrix)
     step(field, work, rhs, matrix)
 
-    def last(block, carry):
-        new = sweep(work, rhs, matrix, block)
-        at = pl.ds(pl.multiple_of(8 * block, 8), 8)
+    for half, sent in enumerate((sent_a, sent_b)):
+        start = 1 + HALF * half
+
+        def last(block, carry):
+            new = sweep(work, rhs, matrix, block)
+            at = pl.ds(pl.multiple_of(8 * block, 8), 8)
+            for comp in range(2):
+                for k in range(3):
+                    field[comp, k, at, :] = new[comp][k]
+                for k in range(2):
+                    to = pl.multiple_of(8 * ((2 * comp + k) * HALF + block - start), 8)
+                    sent[pl.ds(to, 8), :] = new[comp][k] * inverse[k, at, :]
+            return carry
+
+        lax.fori_loop(start, start + HALF, last, 0, unroll=HALF)
+
         for comp in range(2):
-            for k in range(3):
-                field[comp, k, at, :] = new[comp][k]
-            for k in range(2):
-                base = (2 * comp + k) * 8 * INNER
-                sent[pl.ds(pl.multiple_of(base + 8 * block - 8, 8), 8), :] = new[comp][k] * inverse[k, at, :]
-        return carry
-
-    lax.fori_loop(1, BLOCKS - 1, last, 0, unroll=17)
-
-    for comp in range(2):
-        strip = [zero] * GROUP
-        for block in range(INNER):
-            g, place = divmod(block, GROUP)
-            at = pl.ds(8 * block + 8, 8)
-            tile = field[comp, 2, at, :] * inverse[2, at, :]
-            tile = pltpu.roll(tile, FIELD_RIM + 16 * g, 1)
-            strip[place] = jnp.where((lane >= 16 * g) & (lane < 16 * g + 16), tile, strip[place])
-        for place in range(GROUP):
-            sent[pl.ds(32 * INNER + STRIP * comp + 8 * place, 8), :] = strip[place]
+            strip = [zero] * FOLD
+            for n in range(HALF):
+                g, place = divmod(n, FOLD)
+                at = pl.ds(8 * (start + n), 8)
+                tile = pltpu.roll(field[comp, 2, at, :] * inverse[2, at, :], FIELD_RIM + 16 * g, 1)
+                strip[place] = jnp.where((lane >= 16 * g) & (lane < 16 * g + 16), tile, strip[place])
+            for place in range(FOLD):
+                sent[pl.ds(32 * HALF + 8 * (FOLD * comp + place), 8), :] = strip[place]
     for copy in copies:
         copy.wait()
 
 
-def second_kernel(rhs, matrix, inverse, field, far, near, out, moved, work_a, work_b, strips):
+def beside_terms(half, received, matrix, inverse, strips, store, ok=None):
     lane = lanes()
-    s = lax.axis_index("sec")
-    inside = (s > 0) & (s < lax.axis_size("sec") - 1)
-
-    def both(at):
-        return jnp.where(inside, far[at, :], 0.0) + near[at, :]
-
-    clear_rims(work_a)
-    clear_rims(work_b)
+    start = 1 + HALF * half
+
+    def read(at):
+        return received[at, :] if ok is None else jnp.where(ok, received[at, :], 0.0)
+
     for comp in range(2):
-        for block in range(INNER):
-            g, place = divmod(block, GROUP)
-            at = pl.ds(32 * INNER + STRIP * comp + 8 * place, 8)
-            tile = pltpu.roll(both(at), 128 - FIELD_RIM - 16 * g, 1)
-            strips[comp, pl.ds(8 * block, 8), :] = jnp.where((lane < FIELD_RIM) | (lane >= 128 - FIELD_RIM), tile, 0.0)
-
-    def right_side(block, carry):
-        at = pl.ds(pl.multiple_of(8 * block, 8), 8)
+        for n in range(HALF):
+            g, place = divmod(n, FOLD)
+            tile = read(pl.ds(32 * HALF + 8 * (FOLD * comp + place), 8))
+            tile = pltpu.roll(tile, 128 - FIELD_RIM - 16 * g, 1)
+            strips[comp, pl.ds(8 * n, 8), :] = jnp.where((lane < FIELD_RIM) | (lane >= 128 - FIELD_RIM), tile, 0.0)
+
+    def body(n, carry):
+        at = pl.ds(pl.multiple_of(8 * (start + n), 8), 8)
         for k in range(3):
             pair = []
             for comp in range(2):
                 if k < 2:
-                    base = (2 * comp + k) * 8 * INNER
-                    rows = pl.ds(pl.multiple_of(base + 8 * block - 8, 8), 8)
-                    value = both(rows)
+                    value = read(pl.ds(pl.multiple_of(8 * ((2 * comp + k) * HALF + n), 8), 8))
                 else:
-                    value = strips[comp, pl.ds(pl.multiple_of(8 * block - 8, 8), 8), :]
+                    value = strips[comp, pl.ds(pl.multiple_of(8 * n, 8), 8), :]
                 pair.append(value * (inverse[k, at, :] * COUPLING))
             a, b, d = (matrix[i, k, at, :] for i in range(3))
-            moved[0, k, at, :] = rhs[0, k, at, :] + (a * pair[0] - b * pair[1])
-            moved[1, k, at, :] = rhs[1, k, at, :] + (d * pair[1] - b * pair[0])
+            store(k, at, a * pair[0] - b * pair[1], d * pair[1] - b * pair[0])
         return carry
 
-    lax.fori_loop(1, BLOCKS - 1, right_side, 0, unroll=17)
-
+    lax.fori_loop(0, HALF, body, 0, unroll=HALF)
+
+
+def carry_kernel(rhs, matrix, inverse, field, near_a, near_b, out, moved, work_a, work_b, strips):
+    clear_rims(work_a)
+    clear_rims(work_b)
+
+    def store(k, at, x, y):
+        moved[0, k, at, :] = rhs[0, k, at, :] + x
+        moved[1, k, at, :] = rhs[1, k, at, :] + y
+
+    for half, near in enumerate((near_a, near_b)):
+        beside_terms(half, near, matrix, inverse, strips, store)
     step(field, work_a, moved, matrix)
     step(work_a, work_b, moved, matrix)
     step(work_b, work_a, moved, matrix)
@@ -480,12 +516,64 @@
         at = pl.ds(pl.multiple_of(8 * block, 8), 8)
         for comp in range(2):
             for k in range(2):
-                out[comp, 0, pl.ds(pl.multiple_of(8 * block - RIM, 8), 8), pl.ds(128 * k, 128)] = (
-                    new[comp][k] * inverse[k, at, :]
-                )
+                out[comp, k, at, :] = new[comp][k]
         return carry
 
     lax.fori_loop(2, BLOCKS - 2, last, 0, unroll=16)
+
+
+def second_kernel(half, matrix, inverse, carried, far, *rest):
+    if half == 0:
+        out, seam, moved, work_a, work_b, strips, result, sems = rest
+    else:
+        seam, _, out, moved, work_a, work_b, strips, result, sems = rest
+    s = lax.axis_index("sec")
+    inside = (s > 0) & (s < lax.axis_size("sec") - 1)
+    low, high = (1, HALF + 1) if half == 0 else (HALF, 2 * HALF)
+    zero = jnp.zeros((8, 128), jnp.float32)
+    for comp in range(2):
+        for k in range(3):
+            for ref in (moved, work_a, work_b):
+                ref[comp, k, pl.ds(8 * low - 8, 8), :] = zero
+                ref[comp, k, pl.ds(8 * high + 8, 8), :] = zero
+            moved[comp, k, pl.ds(8 * (high if half == 0 else low), 8), :] = zero
+
+    def store(k, at, x, y):
+        moved[0, k, at, :] = x
+        moved[1, k, at, :] = y
+
+    beside_terms(half, far, matrix, inverse, strips, store, inside)
+    step(moved, work_a, moved, matrix, low, high)
+    step(work_a, work_b, moved, matrix, low, high)
+
+    first, count = (2, HALF - 2) if half == 0 else (HALF, HALF)
+    moves = []
+
+    def final(block, new):
+        at = pl.ds(8 * block, 8)
+        for comp in range(2):
+            for k in range(2):
+                value = new[comp][k] + carried[comp, k, at, :]
+                if half == 1 and block <= HALF + 1:
+                    value = value + seam[comp, k, pl.ds(8 * (block - HALF), 8), :]
+                result[comp, pl.ds(8 * block - RIM, 8), pl.ds(128 * k, 128)] = value * inverse[k, at, :]
+
+    for block in range(max(low, 2), min(high, BLOCKS - 3) + 1):
+        new = sweep(work_b, moved, matrix, block)
+        if block < first + count:
+            final(block, new)
+        else:
+            for comp in range(2):
+                for k in range(2):
+                    seam[comp, k, pl.ds(8 * (block - HALF), 8), :] = new[comp][k]
+        if block + 1 == first + count or (block + 1 - first) % 8 == 0 and block < first + count:
+            done = len(moves) // 2
+            at = pl.ds(8 * (first + 8 * done) - RIM, 8 * (block + 1 - first - 8 * done))
+            for c in range(2):
+                moves.append(pltpu.make_async_copy(result.at[c, at], out.at[c, 0, at], sems.at[c, done]))
+                moves[-1].start()
+    for move in moves:
+        move.wait()
 
 
 def f32(*shape):
@@ -509,6 +597,8 @@
 def local(images, stiffness):
     grid = (3, EXT, 128)
     edge, strip = f32(2 * RIM, TILE), f32(2 * STRIP, 128)
+    later_far = send(images, sec_odd)
+    later_near = send(images, sec_even)
     in_hbm = pl.BlockSpec(memory_space=pltpu.HBM)
     tile = f32(1, TILE, TILE)
     images, stiffness, to_o, to_e = call(
@@ -525,38 +615,77 @@
     col_o = send(strip_o, col_odd)
     col_e = send(strip_e, col_even)
 
-    section = call(section_kernel, f32(RIMS + 2 * TILE, 128), (images, row_o, row_e, col_o, col_e))
-    later_far = send(section, sec_odd)
-    later_near = send(section, sec_even)
+    band = call(band_kernel, f32(3 * 128, 3 * 128), (to_o,), us=1)
+
+    rims = call(rims_kernel, f32(RIMS, 128), (row_o, row_e, col_o, col_e))
+    rims_far = send(rims, sec_odd)
+    rims_near = send(rims, sec_even)
     ext, gx, gy, matrix, inverse, known = call(
         matrix_kernel,
         (f32(3, EXT + 16, 128), f32(*grid), f32(*grid), f32(3, *grid), f32(*grid), f32(3, EXT, TILE)),
-        (images, stiffness, row_o, row_e, col_o, col_e),
-        mib=16,
+        (images, stiffness, row_o, row_e, col_o, col_e, band),
+        mib=20,
         us=4,
-        scratch_shapes=[vmem(*grid), vmem(3, *grid)],
+        scratch_shapes=[vmem(*grid), vmem(3, *grid), vmem(3 * EXT, 3 * 128)],
     )
-    sent_rows = 32 * INNER + 2 * STRIP
-    everywhere = [pl.BlockSpec(memory_space=pltpu.VMEM)] * 3
-    tensor, rhs, field, sent = call(
+    everywhere = [pl.BlockSpec(memory_space=pltpu.VMEM)] * 4
+    tensor, rhs, field, sent_a, sent_b = call(
         first_kernel,
-        (f32(5, 1, TILE, TILE), f32(2, *grid), f32(2, *grid), f32(sent_rows, 128)),
-        (ext, gx, gy, matrix, inverse, known, later_far, later_near),
+        (f32(5, 1, TILE, TILE), f32(2, *grid), f32(2, *grid), f32(SENT, 128), f32(SENT, 128)),
+        (ext, gx, gy, matrix, inverse, known, later_far, later_near, rims_far, rims_near, band),
         mib=20,
         us=5,
         out_specs=[pl.BlockSpec(memory_space=pl.ANY)] + everywhere,
-        scratch_shapes=[vmem(*grid), vmem(2, *grid), vmem(2, *grid), vmem(2, EXT, TILE), pltpu.SemaphoreType.DMA((2,))],
+        scratch_shapes=[
+            vmem(*grid),
+            vmem(2, *grid),
+            vmem(2 * EXT, 3 * 128),
+            vmem(2, *grid),
+            vmem(2, EXT, TILE),
+            pltpu.SemaphoreType.DMA((2,)),
+        ],
     )
 
-    far = send(sent, sec_odd)
-    near = send(sent, sec_even)
+    near_a, near_b = send(sent_a, sec_even), send(sent_b, sec_even)
+    far_a, far_b = send(sent_a, sec_odd), send(sent_b, sec_odd)
+    carried = call(
+        carry_kernel,
+        f32(2, 2, EXT, 128),
+        (rhs, matrix, inverse, field, near_a, near_b),
+        mib=16,
+        us=3,
+        scratch_shapes=[vmem(2, *grid), vmem(2, *grid), vmem(2, *grid), vmem(2, 8 * HALF, 128)],
+    )
+    whole = pl.BlockSpec(memory_space=pltpu.VMEM)
+    anywhere = pl.BlockSpec(memory_space=pl.ANY)
+    final = f32(2, 1, TILE, TILE)
+    scratch = [
+        vmem(2, *grid),
+        vmem(2, *grid),
+        vmem(2, *grid),
+        vmem(2, 8 * HALF, 128),
+        vmem(2, TILE, TILE),
+        pltpu.SemaphoreType.DMA((2, CUTS)),
+    ]
+    field, seam = call(
+        functools.partial(second_kernel, 0),
+        (final, f32(2, 2, 16, 128)),
+        (matrix, inverse, carried, far_a),
+        mib=16,
+        us=2,
+        out_specs=[anywhere, whole],
+        scratch_shapes=scratch,
+    )
     field = call(
-        second_kernel,
-        f32(2, 1, TILE, TILE),
-        (rhs, matrix, inverse, field, far, near),
-        mib=20,
-        us=4,
-        scratch_shapes=[vmem(2, *grid), vmem(2, *grid), vmem(2, *grid), vmem(2, 8 * INNER, 128)],
+        functools.partial(second_kernel, 1),
+        final,
+        (matrix, inverse, carried, far_b, seam, field),
+        mib=16,
+        us=2,
+        in_specs=[whole] * 5 + [anywhere],
+        out_specs=anywhere,
+        input_output_aliases={5: 0},
+        scratch_shapes=scratch,
     )
     return tensor, field
 

time: 43.9 us -> 39.9 us (0.909)
  the two profiles are of different devices: /device:TPU:99 before, /device:TPU:120 now
where the time goes in v4:
time: 39.9 us; the launch traced here: 39.4 us
  Pallas kernels  14.8 us (37%)
  waiting for transfers between devices  12.6 us (32%)
  starting transfers between devices  11.1 us (28%)
  between operations  0.88 us (2%)
    pallas_call x9, Pallas kernels, call(): pl.pallas_call(kernel, out_shape=out_shape, compiler_params=pltpu.Compile...  14.8 us
    ppermute x12, waiting for transfers between devices, send(): return lax.ppermute(value, AXES, found)  12.6 us
    ppermute x12, starting transfers between devices, send(): return lax.ppermute(value, AXES, found)  11.1 us
  transfers between devices with their start and end apart: 12, of which 7 were waited for; matrix products, arithmetic and copies ran while one was open for 0% of the time, Pallas kernels for 22%

profile of v4, /device:TPU:120, one launch (start us, length us, event | category | flops | bytes accessed | tf_op | source)
XLA Modules:
  0.0 39.4 jit_solution(9280547433583984131)
XLA Ops:
  0.6 0.1 collective-permute-start.5
  0.7 1.3 %collective-permute-start.4 = (f32[1,256,256]{2,1,0:T(8,128)}, f32[1,256,256]{2,1,0:T(8,128)S(1)}, u32[]{:S(2)}, u32[]{:S(2)}) collective-permute-start(f32[1,256,256]{2,1,0:T(8,128)} %image.1), channel_id=1, source_target_pairs={{0,16},{1,17},{2,18},{3,19},{4,20},{5,21},{6,22},{7,23},{8,24},{9,... | collective-permute-start | bytes 786440 | tf_op jit(solution)/shard_map/ppermute | solution.py:49
  2.1 1.1 %shard_map.41 = (f32[1,256,256]{2,1,0:T(8,128)S(1)}, f32[1,256,256]{2,1,0:T(8,128)S(1)}, f32[32,256]{1,0:T(8,128)S(1)}, f32[32,256]{1,0:T(8,128)S(1)}) custom-call(f32[1,256,256]{2,1,0:T(8,128)} %image.1, f32[1,256,256]{2,1,0:T(8,128)} %stiff.1), custom_call_target="tpu_custom_call" | custom-call | tf_op jit(solution)/shard_map/pallas_call | solution.py:588
  3.2 1.6 %collective-permute-start.1 = (f32[32,256]{1,0:T(8,128)S(1)}, f32[32,256]{1,0:T(8,128)S(1)}, u32[]{:S(2)}, u32[]{:S(2)}) collective-permute-start(f32[32,256]{1,0:T(8,128)S(1)} %get-tuple-element.24), channel_id=1, source_target_pairs={{0,16},{1,17},{2,18},{3,19},{4,20},{5,21},{6,22},{7,23},{8,24},{9,... | collective-permute-start | bytes 98312 | tf_op jit(solution)/shard_map/ppermute | solution.py:49
  4.8 0.0 collective-permute-start
  4.8 2.8 %collective-permute-done.1.row_e = f32[32,256]{1,0:T(8,128)S(1)} collective-permute-done((f32[32,256]{1,0:T(8,128)S(1)}, f32[32,256]{1,0:T(8,128)S(1)}, u32[]{:S(2)}, u32[]{:S(2)}) %collective-permute-start.1) | collective-permute-done | bytes 32800 | tf_op jit(solution)/shard_map/ppermute | solution.py:49
  7.5 1.2 %collective-permute-done.row_o = f32[32,256]{1,0:T(8,128)S(1)} collective-permute-done((f32[32,256]{1,0:T(8,128)S(1)}, f32[32,256]{1,0:T(8,128)S(1)}, u32[]{:S(2)}, u32[]{:S(2)}) %collective-permute-start) | collective-permute-done | bytes 32800 | tf_op jit(solution)/shard_map/ppermute | solution.py:49
  8.7 0.2 shard_map.42
  8.9 3.3 %collective-permute-start.2 = (f32[80,128]{1,0:T(8,128)S(1)}, f32[80,128]{1,0:T(8,128)S(1)}, u32[]{:S(2)}, u32[]{:S(2)}) collective-permute-start(f32[80,128]{1,0:T(8,128)S(1)} %get-tuple-element.25), channel_id=1, source_target_pairs={{0,16},{1,2},{2,1},{3,4},{4,3},{5,6},{6,5},{7,8},{8,7},{9,10},{10,... | collective-permute-start | bytes 122888 | tf_op jit(solution)/shard_map/ppermute | solution.py:49
  12.2 0.0 collective-permute-start.3
  12.2 2.9 %collective-permute-done.2.col_o = f32[80,128]{1,0:T(8,128)S(1)} collective-permute-done((f32[80,128]{1,0:T(8,128)S(1)}, f32[80,128]{1,0:T(8,128)S(1)}, u32[]{:S(2)}, u32[]{:S(2)}) %collective-permute-start.2) | collective-permute-done | bytes 40992 | tf_op jit(solution)/shard_map/ppermute | solution.py:49
  15.1 1.1 %collective-permute-done.3.col_e = f32[80,128]{1,0:T(8,128)S(1)} collective-permute-done((f32[80,128]{1,0:T(8,128)S(1)}, f32[80,128]{1,0:T(8,128)S(1)}, u32[]{:S(2)}, u32[]{:S(2)}) %collective-permute-start.3) | collective-permute-done | bytes 40992 | tf_op jit(solution)/shard_map/ppermute | solution.py:49
  16.2 0.0 collective-permute-start.7
  16.2 1.0 %collective-permute-start.6 = (f32[144,128]{1,0:T(8,128)S(1)}, f32[144,128]{1,0:T(8,128)S(1)}, u32[]{:S(2)}, u32[]{:S(2)}) collective-permute-start(f32[144,128]{1,0:T(8,128)S(1)} %shard_map.45), channel_id=1, source_target_pairs={{0,16},{1,17},{2,18},{3,19},{4,20},{5,21},{6,22},{7,23},{8,24},{9,... | collective-permute-start | bytes 221192 | tf_op jit(solution)/shard_map/ppermute | solution.py:49
  17.2 0.1 shard_map.43.band
  17.3 2.8 %shard_map.44 = (f32[3,304,128]{2,1,0:T(8,128)S(1)}, f32[3,288,128]{2,1,0:T(8,128)S(1)}, f32[3,288,128]{2,1,0:T(8,128)S(1)}, f32[3,3,288,128]{3,2,1,0:T(8,128)S(...) custom-call(f32[1,256,256]{2,1,0:T(8,128)S(1)} %get-tuple-element.21.image, ...), custom_call_target="tpu_custom_call" | custom-call | flops 4000000 | bytes 12000000 | tf_op jit(solution)/shard_map/pallas_call | solution.py:588
  20.1 0.0 collective-permute-done.7.near
  20.1 1.5 %collective-permute-done.6.far = f32[144,128]{1,0:T(8,128)S(1)} collective-permute-done((f32[144,128]{1,0:T(8,128)S(1)}, f32[144,128]{1,0:T(8,128)S(1)}, u32[]{:S(2)}, u32[]{:S(2)}) %collective-permute-start.6) | collective-permute-done | bytes 73760 | tf_op jit(solution)/shard_map/ppermute | solution.py:49
  21.6 0.0 collective-permute-done.5.later_near
  21.6 0.0 collective-permute-done.4.later_far
  21.6 4.1 %shard_map.46 = (f32[5,1,256,256]{3,2,1,0:T(8,128)}, f32[2,3,288,128]{3,2,1,0:T(8,128)S(1)}, f32[2,3,288,128]{3,2,1,0:T(8,128)S(1)}, f32[592,128]{1,0:T(8,128)S(1)}, f32[592,128]{1,0:T(8,128)S(1)}) custom-call(f32[3,304,128]{2,1,0:T(8,128)S(1)} %get-tuple-element.27.ext, f32[3,288,128]{2,1,0:T(8,128)S(1)} %get-tuple-element.28.gx, ...), custom_call_target="tpu_custom_call" | custom-call | flops 5000000 | bytes 15000000 | tf_op jit(solution)/shard_map/pallas_call | solution.py:588
  25.7 0.1 collective-permute-start.8
  25.8 0.5 %collective-permute-start.9 = (f32[592,128]{1,0:T(8,128)S(1)}, f32[592,128]{1,0:T(8,128)S(1)}, u32[]{:S(2)}, u32[]{:S(2)}) collective-permute-start(f32[592,128]{1,0:T(8,128)S(1)} %get-tuple-element.37), channel_id=1, source_target_pairs={{0,64},{1,65},{2,66},{3,67},{4,68},{5,69},{6,70},{7,71},{8,72},{9,... | collective-permute-start | bytes 909320 | tf_op jit(solution)/shard_map/ppermute | solution.py:49
  26.3 0.9 %collective-permute-start.11 = (f32[592,128]{1,0:T(8,128)S(1)}, f32[592,128]{1,0:T(8,128)S(1)}, u32[]{:S(2)}, u32[]{:S(2)}) collective-permute-start(f32[592,128]{1,0:T(8,128)S(1)} %get-tuple-element.36), channel_id=1, source_target_pairs={{0,16},{1,17},{2,18},{3,19},{4,20},{5,21},{6,22},{7,23},{8,24},{9,... | collective-permute-start | bytes 909320 | tf_op jit(solution)/shard_map/ppermute | solution.py:49
  27.2 2.3 %collective-permute-start.10 = (f32[592,128]{1,0:T(8,128)S(1)}, f32[592,128]{1,0:T(8,128)S(1)}, u32[]{:S(2)}, u32[]{:S(2)}) collective-permute-start(f32[592,128]{1,0:T(8,128)S(1)} %get-tuple-element.37), channel_id=1, source_target_pairs={{0,16},{1,17},{2,18},{3,19},{4,20},{5,21},{6,22},{7,23},{8,24},{9,... | collective-permute-start | bytes 909320 | tf_op jit(solution)/shard_map/ppermute | solution.py:49
  29.6 0.0 collective-permute-done.8.near_a
  29.6 0.0 collective-permute-done.9.near_b
  29.6 2.6 %shard_map.47.carried = f32[2,2,288,128]{3,2,1,0:T(8,128)S(1)} custom-call(f32[2,3,288,128]{3,2,1,0:T(8,128)S(1)} %get-tuple-element.34.rhs, f32[3,3,288,128]{3,2,1,0:T(8,128)S(1)} %get-tuple-element.30.matrix, f32[3,288,128]{2,1,0:T(8,128)S(1)} %get-tuple-element.31.inverse, f32[2,3,288,128]{3,2,1,0:T(8,128)S(1)} %get-tuple-element.35.field, ...), custom_call_target="tpu_custom_call" | custom-call | flops 3000000 | bytes 9000000 | tf_op jit(solution)/shard_map/pallas_call | solution.py:588
  32.2 1.8 %collective-permute-done.11.far = f32[592,128]{1,0:T(8,128)S(1)} collective-permute-done((f32[592,128]{1,0:T(8,128)S(1)}, f32[592,128]{1,0:T(8,128)S(1)}, u32[]{:S(2)}, u32[]{:S(2)}) %collective-permute-start.11) | collective-permute-done | bytes 303136 | tf_op jit(solution)/shard_map/ppermute | solution.py:49
  34.1 1.9 %shard_map.48 = (f32[2,1,256,256]{3,2,1,0:T(8,128)}, f32[2,2,16,128]{3,2,1,0:T(8,128)S(1)}) custom-call(f32[3,3,288,128]{3,2,1,0:T(8,128)S(1)} %get-tuple-element.30.matrix, f32[3,288,128]{2,1,0:T(8,128)S(1)} %get-tuple-element.31.inverse, f32[2,2,288,128]{3,2,1,0:T(8,128)S(1)} %shard_map.47.carried, f32[592,128]{1,0:T(8,128)S(1)} %collective-permute-done.11.far), custom_call_target="tpu_custom_call" | custom-call | flops 2000000 | bytes 6000000 | tf_op jit(solution)/shard_map/pallas_call | solution.py:588
  35.9 1.4 %collective-permute-done.10.far = f32[592,128]{1,0:T(8,128)S(1)} collective-permute-done((f32[592,128]{1,0:T(8,128)S(1)}, f32[592,128]{1,0:T(8,128)S(1)}, u32[]{:S(2)}, u32[]{:S(2)}) %collective-permute-start.10) | collective-permute-done | bytes 303136 | tf_op jit(solution)/shard_map/ppermute | solution.py:49
  37.3 1.9 %shard_map.49 = f32[2,1,256,256]{3,2,1,0:T(8,128)} custom-call(f32[3,3,288,128]{3,2,1,0:T(8,128)S(1)} %get-tuple-element.30.matrix, f32[3,288,128]{2,1,0:T(8,128)S(1)} %get-tuple-element.31.inverse, f32[2,2,288,128]{3,2,1,0:T(8,128)S(1)} %shard_map.47.carried, f32[592,128]{1,0:T(8,128)S(1)} %collective-permute-done.10.far, ...), custom_call_target="tpu_custom_call", output_to_operand_aliasing={{}: (5, {})} | custom-call | flops 2000000 | bytes 6000000 | tf_op jit(solution)/shard_map/pallas_call | solution.py:588
  (1 shorter events, 0.0 us)
Async XLA Ops:
  0.6 21.0 %collective-permute-start.5 = (f32[1,256,256]{2,1,0:T(8,128)}, f32[1,256,256]{2,1,0:T(8,128)S(1)}, u32[]{:S(2)}, u32[]{:S(2)}) collective-permute-start(f32[1,256,256]{2,1,0:T(8,128)} %image.1), channel_id=1, source_target_pairs={{0,64},{1,65},{2,66},{3,67},{4,68},{5,69},{6,70},{7,71},{8,72},{9,... | collective-permute-start | bytes 786440 | tf_op jit(solution)/shard_map/ppermute | solution.py:49
  0.7 20.9 %collective-permute-start.4 = (f32[1,256,256]{2,1,0:T(8,128)}, f32[1,256,256]{2,1,0:T(8,128)S(1)}, u32[]{:S(2)}, u32[]{:S(2)}) collective-permute-start(f32[1,256,256]{2,1,0:T(8,128)} %image.1), channel_id=1, source_target_pairs={{0,16},{1,17},{2,18},{3,19},{4,20},{5,21},{6,22},{7,23},{8,24},{9,... | collective-permute-start | bytes 786440 | tf_op jit(solution)/shard_map/ppermute | solution.py:49
  3.2 4.3 %collective-permute-start.1 = (f32[32,256]{1,0:T(8,128)S(1)}, f32[32,256]{1,0:T(8,128)S(1)}, u32[]{:S(2)}, u32[]{:S(2)}) collective-permute-start(f32[32,256]{1,0:T(8,128)S(1)} %get-tuple-element.24), channel_id=1, source_target_pairs={{0,16},{1,17},{2,18},{3,19},{4,20},{5,21},{6,22},{7,23},{8,24},{9,... | collective-permute-start | bytes 98312 | tf_op jit(solution)/shard_map/ppermute | solution.py:49
  4.8 3.9 %collective-permute-start = (f32[32,256]{1,0:T(8,128)S(1)}, f32[32,256]{1,0:T(8,128)S(1)}, u32[]{:S(2)}, u32[]{:S(2)}) collective-permute-start(f32[32,256]{1,0:T(8,128)S(1)} %get-tuple-element.23.start), channel_id=1, source_target_pairs={{0,1},{1,0},{2,3},{3,2},{4,5},{5,4},{6,7},{7,6},{8,9},{9,8},{10,11... | collective-permute-start | bytes 98312 | tf_op jit(solution)/shard_map/ppermute | solution.py:49
  8.9 6.2 %collective-permute-start.2 = (f32[80,128]{1,0:T(8,128)S(1)}, f32[80,128]{1,0:T(8,128)S(1)}, u32[]{:S(2)}, u32[]{:S(2)}) collective-permute-start(f32[80,128]{1,0:T(8,128)S(1)} %get-tuple-element.25), channel_id=1, source_target_pairs={{0,16},{1,2},{2,1},{3,4},{4,3},{5,6},{6,5},{7,8},{8,7},{9,10},{10,... | collective-permute-start | bytes 122888 | tf_op jit(solution)/shard_map/ppermute | solution.py:49
  12.2 4.0 %collective-permute-start.3 = (f32[80,128]{1,0:T(8,128)S(1)}, f32[80,128]{1,0:T(8,128)S(1)}, u32[]{:S(2)}, u32[]{:S(2)}) collective-permute-start(f32[80,128]{1,0:T(8,128)S(1)} %get-tuple-element.26), channel_id=1, source_target_pairs={{0,1},{1,0},{2,3},{3,2},{4,5},{5,4},{6,7},{7,6},{8,9},{9,8},{10,11... | collective-permute-start | bytes 122888 | tf_op jit(solution)/shard_map/ppermute | solution.py:49
  16.2 3.9 %collective-permute-start.7 = (f32[144,128]{1,0:T(8,128)S(1)}, f32[144,128]{1,0:T(8,128)S(1)}, u32[]{:S(2)}, u32[]{:S(2)}) collective-permute-start(f32[144,128]{1,0:T(8,128)S(1)} %shard_map.45), channel_id=1, source_target_pairs={{0,64},{1,65},{2,66},{3,67},{4,68},{5,69},{6,70},{7,71},{8,72},{9,... | collective-permute-start | bytes 221192 | tf_op jit(solution)/shard_map/ppermute | solution.py:49
  16.2 5.4 %collective-permute-start.6 = (f32[144,128]{1,0:T(8,128)S(1)}, f32[144,128]{1,0:T(8,128)S(1)}, u32[]{:S(2)}, u32[]{:S(2)}) collective-permute-start(f32[144,128]{1,0:T(8,128)S(1)} %shard_map.45), channel_id=1, source_target_pairs={{0,16},{1,17},{2,18},{3,19},{4,20},{5,21},{6,22},{7,23},{8,24},{9,... | collective-permute-start | bytes 221192 | tf_op jit(solution)/shard_map/ppermute | solution.py:49
  25.7 3.9 %collective-permute-start.8 = (f32[592,128]{1,0:T(8,128)S(1)}, f32[592,128]{1,0:T(8,128)S(1)}, u32[]{:S(2)}, u32[]{:S(2)}) collective-permute-start(f32[592,128]{1,0:T(8,128)S(1)} %get-tuple-element.36), channel_id=1, source_target_pairs={{0,64},{1,65},{2,66},{3,67},{4,68},{5,69},{6,70},{7,71},{8,72},{9,... | collective-permute-start | bytes 909320 | tf_op jit(solution)/shard_map/ppermute | solution.py:49
  25.8 3.8 %collective-permute-start.9 = (f32[592,128]{1,0:T(8,128)S(1)}, f32[592,128]{1,0:T(8,128)S(1)}, u32[]{:S(2)}, u32[]{:S(2)}) collective-permute-start(f32[592,128]{1,0:T(8,128)S(1)} %get-tuple-element.37), channel_id=1, source_target_pairs={{0,64},{1,65},{2,66},{3,67},{4,68},{5,69},{6,70},{7,71},{8,72},{9,... | collective-permute-start | bytes 909320 | tf_op jit(solution)/shard_map/ppermute | solution.py:49
  26.3 7.7 %collective-permute-start.11 = (f32[592,128]{1,0:T(8,128)S(1)}, f32[592,128]{1,0:T(8,128)S(1)}, u32[]{:S(2)}, u32[]{:S(2)}) collective-permute-start(f32[592,128]{1,0:T(8,128)S(1)} %get-tuple-element.36), channel_id=1, source_target_pairs={{0,16},{1,17},{2,18},{3,19},{4,20},{5,21},{6,22},{7,23},{8,24},{9,... | collective-permute-start | bytes 909320 | tf_op jit(solution)/shard_map/ppermute | solution.py:49
  27.2 10.1 %collective-permute-start.10 = (f32[592,128]{1,0:T(8,128)S(1)}, f32[592,128]{1,0:T(8,128)S(1)}, u32[]{:S(2)}, u32[]{:S(2)}) collective-permute-start(f32[592,128]{1,0:T(8,128)S(1)} %get-tuple-element.37), channel_id=1, source_target_pairs={{0,16},{1,17},{2,18},{3,19},{4,20},{5,21},{6,22},{7,23},{8,24},{9,... | collective-permute-start | bytes 909320 | tf_op jit(solution)/shard_map/ppermute | solution.py:49

commit v5 on v4

--- a/solution.py
+++ b/solution.py
@@ -18,9 +18,10 @@
 INNER = BLOCKS - 2
 GROUP = 5
 FIELD_RIM = 8
-HALF = INNER // 2
+COUNTS = (22, INNER - 22)
+STARTS = (1, 1 + COUNTS[0])
 FOLD = 3
-SENT = 32 * HALF + 16 * FOLD
+SENT = [32 * count + 16 * FOLD for count in COUNTS]
 CUTS = 4
 STRIP = GROUP * 8
 RIMS = 4 * RIM + 2 * STRIP
@@ -130,8 +131,24 @@
     return top, bottom
 
 
-def prepare_kernel(image, stiff, img, stf, out_o, out_e, sems):
+def edges_kernel(image, stiff, out_o, out_e, first, last, sems):
     flag = is_odd("row")
+    copies = []
+    for m, ref in enumerate((image, stiff)):
+        for n, (dst, at) in enumerate(((first, 0), (last, TILE - RIM))):
+            copies.append(pltpu.make_async_copy(ref.at[0, pl.ds(at, RIM)], dst.at[pl.ds(RIM * m, RIM)], sems.at[m, n]))
+    for copy in copies:
+        copy.start()
+    for copy in copies:
+        copy.wait()
+    for n in range(2 * RIM // 8):
+        rows = pl.ds(8 * n, 8)
+        a, b = first[rows, :], last[rows, :]
+        out_o[rows, :] = jnp.where(flag, b, a)
+        out_e[rows, :] = jnp.where(flag, a, b)
+
+
+def load_kernel(image, stiff, after, img, stf, sems):
     copies = []
     for n in range(CUTS):
         at = pl.ds(TILE // CUTS * n, TILE // CUTS)
@@ -141,12 +158,6 @@
         copy.start()
     for copy in copies:
         copy.wait()
-    for m, ref in enumerate((img, stf)):
-        for n in range(RIM // 8):
-            rows = pl.ds(RIM * m + 8 * n, 8)
-            a, b = ref[0, pl.ds(8 * n, 8), :], ref[0, pl.ds(TILE - RIM + 8 * n, 8), :]
-            out_o[rows, :] = jnp.where(flag, b, a)
-            out_e[rows, :] = jnp.where(flag, a, b)
 
 
 def strip_kernel(image, stiff, row_o, row_e, out_o, out_e):
@@ -341,7 +352,7 @@
     return first, second
 
 
-def step(src, dst, rhs, matrix, low=1, high=BLOCKS - 2):
+def step(src, dst, rhs, matrix, low=1, high=BLOCKS - 2, unroll=INNER // 2):
     def body(block, carry):
         new = sweep(src, rhs, matrix, block)
         at = pl.ds(pl.multiple_of(8 * block, 8), 8)
@@ -350,12 +361,12 @@
                 dst[comp, k, at, :] = new[comp][k]
         return carry
 
-    lax.fori_loop(low, high + 1, body, 0, unroll=(high + 1 - low) // 2)
+    lax.fori_loop(low, high + 1, body, 0, unroll=unroll)
 
 
 def first_kernel(
     ext, gx, gy, matrix, inverse, known, later_far, later_near, far, near, band,
-    tensor, rhs, field, sent_a, sent_b,
+    tensor, rhs, field, sent_a, sent_b, sent,
     chg, sums, prods, work, fresh, sems,
 ):
     lane = lanes()
@@ -437,8 +448,8 @@
     step(work, field, rhs, matrix)
     step(field, work, rhs, matrix)
 
-    for half, sent in enumerate((sent_a, sent_b)):
-        start = 1 + HALF * half
+    for half, part in enumerate((sent_a, sent_b)):
+        start, count, base = STARTS[half], COUNTS[half], SENT[0] * half
 
         def last(block, carry):
             new = sweep(work, rhs, matrix, block)
@@ -447,36 +458,39 @@
                 for k in range(3):
                     field[comp, k, at, :] = new[comp][k]
                 for k in range(2):
-                    to = pl.multiple_of(8 * ((2 * comp + k) * HALF + block - start), 8)
-                    sent[pl.ds(to, 8), :] = new[comp][k] * inverse[k, at, :]
+                    to = pl.multiple_of(8 * ((2 * comp + k) * count + block - start), 8)
+                    value = new[comp][k] * inverse[k, at, :]
+                    part[pl.ds(to, 8), :] = value
+                    sent[pl.ds(pl.multiple_of(base + to, 8), 8), :] = value
             return carry
 
-        lax.fori_loop(start, start + HALF, last, 0, unroll=HALF)
+        lax.fori_loop(start, start + count, last, 0, unroll=count)
 
         for comp in range(2):
             strip = [zero] * FOLD
-            for n in range(HALF):
+            for n in range(count):
                 g, place = divmod(n, FOLD)
                 at = pl.ds(8 * (start + n), 8)
                 tile = pltpu.roll(field[comp, 2, at, :] * inverse[2, at, :], FIELD_RIM + 16 * g, 1)
                 strip[place] = jnp.where((lane >= 16 * g) & (lane < 16 * g + 16), tile, strip[place])
             for place in range(FOLD):
-                sent[pl.ds(32 * HALF + 8 * (FOLD * comp + place), 8), :] = strip[place]
+                for ref, at in ((part, 0), (sent, base)):
+                    ref[pl.ds(at + 32 * count + 8 * (FOLD * comp + place), 8), :] = strip[place]
     for copy in copies:
         copy.wait()
 
 
-def beside_terms(half, received, matrix, inverse, strips, store, ok=None):
+def beside_terms(half, received, matrix, inverse, strips, store, base=0, ok=None):
     lane = lanes()
-    start = 1 + HALF * half
+    start, count = STARTS[half], COUNTS[half]
 
     def read(at):
         return received[at, :] if ok is None else jnp.where(ok, received[at, :], 0.0)
 
     for comp in range(2):
-        for n in range(HALF):
+        for n in range(count):
             g, place = divmod(n, FOLD)
-            tile = read(pl.ds(32 * HALF + 8 * (FOLD * comp + place), 8))
+            tile = read(pl.ds(base + 32 * count + 8 * (FOLD * comp + place), 8))
             tile = pltpu.roll(tile, 128 - FIELD_RIM - 16 * g, 1)
             strips[comp, pl.ds(8 * n, 8), :] = jnp.where((lane < FIELD_RIM) | (lane >= 128 - FIELD_RIM), tile, 0.0)
 
@@ -486,7 +500,7 @@
             pair = []
             for comp in range(2):
                 if k < 2:
-                    value = read(pl.ds(pl.multiple_of(8 * ((2 * comp + k) * HALF + n), 8), 8))
+                    value = read(pl.ds(pl.multiple_of(base + 8 * ((2 * comp + k) * count + n), 8), 8))
                 else:
                     value = strips[comp, pl.ds(pl.multiple_of(8 * n, 8), 8), :]
                 pair.append(value * (inverse[k, at, :] * COUPLING))
@@ -494,10 +508,10 @@
             store(k, at, a * pair[0] - b * pair[1], d * pair[1] - b * pair[0])
         return carry
 
-    lax.fori_loop(0, HALF, body, 0, unroll=HALF)
-
-
-def carry_kernel(rhs, matrix, inverse, field, near_a, near_b, out, moved, work_a, work_b, strips):
+    lax.fori_loop(0, count, body, 0, unroll=count)
+
+
+def carry_kernel(rhs, matrix, inverse, field, near, out, moved, work_a, work_b, strips):
     clear_rims(work_a)
     clear_rims(work_b)
 
@@ -505,8 +519,8 @@
         moved[0, k, at, :] = rhs[0, k, at, :] + x
         moved[1, k, at, :] = rhs[1, k, at, :] + y
 
-    for half, near in enumerate((near_a, near_b)):
-        beside_terms(half, near, matrix, inverse, strips, store)
+    for half in range(2):
+        beside_terms(half, near, matrix, inverse, strips, store, SENT[0] * half)
     step(field, work_a, moved, matrix)
     step(work_a, work_b, moved, matrix)
     step(work_b, work_a, moved, matrix)
@@ -529,7 +543,8 @@
         seam, _, out, moved, work_a, work_b, strips, result, sems = rest
     s = lax.axis_index("sec")
     inside = (s > 0) & (s < lax.axis_size("sec") - 1)
-    low, high = (1, HALF + 1) if half == 0 else (HALF, 2 * HALF)
+    edge = COUNTS[0]
+    low, high = (1, edge + 1) if half == 0 else (edge, INNER)
     zero = jnp.zeros((8, 128), jnp.float32)
     for comp in range(2):
         for k in range(3):
@@ -542,11 +557,11 @@
         moved[0, k, at, :] = x
         moved[1, k, at, :] = y
 
-    beside_terms(half, far, matrix, inverse, strips, store, inside)
-    step(moved, work_a, moved, matrix, low, high)
-    step(work_a, work_b, moved, matrix, low, high)
-
-    first, count = (2, HALF - 2) if half == 0 else (HALF, HALF)
+    beside_terms(half, far, matrix, inverse, strips, store, ok=inside)
+    step(moved, work_a, moved, matrix, low, high, high + 1 - low)
+    step(work_a, work_b, moved, matrix, low, high, high + 1 - low)
+
+    first, count = (2, edge - 2) if half == 0 else (edge, INNER - edge)
     moves = []
 
     def final(block, new):
@@ -554,8 +569,8 @@
         for comp in range(2):
             for k in range(2):
                 value = new[comp][k] + carried[comp, k, at, :]
-                if half == 1 and block <= HALF + 1:
-                    value = value + seam[comp, k, pl.ds(8 * (block - HALF), 8), :]
+                if half == 1 and block <= edge + 1:
+                    value = value + seam[comp, k, pl.ds(8 * (block - edge), 8), :]
                 result[comp, pl.ds(8 * block - RIM, 8), pl.ds(128 * k, 128)] = value * inverse[k, at, :]
 
     for block in range(max(low, 2), min(high, BLOCKS - 3) + 1):
@@ -565,7 +580,7 @@
         else:
             for comp in range(2):
                 for k in range(2):
-                    seam[comp, k, pl.ds(8 * (block - HALF), 8), :] = new[comp][k]
+                    seam[comp, k, pl.ds(8 * (block - edge), 8), :] = new[comp][k]
         if block + 1 == first + count or (block + 1 - first) % 8 == 0 and block < first + count:
             done = len(moves) // 2
             at = pl.ds(8 * (first + 8 * done) - RIM, 8 * (block + 1 - first - 8 * done))
@@ -601,11 +616,21 @@
     later_near = send(images, sec_even)
     in_hbm = pl.BlockSpec(memory_space=pltpu.HBM)
     tile = f32(1, TILE, TILE)
-    images, stiffness, to_o, to_e = call(
-        prepare_kernel,
-        (tile, tile, edge, edge),
-        [pltpu.with_memory_space_constraint(x, pltpu.HBM) for x in (images, stiffness)],
+    held = [pltpu.with_memory_space_constraint(x, pltpu.HBM) for x in (images, stiffness)]
+    to_o, to_e = call(
+        edges_kernel,
+        (edge, edge),
+        held,
+        us=1,
         in_specs=[in_hbm, in_hbm],
+        scratch_shapes=[vmem(2 * RIM, TILE), vmem(2 * RIM, TILE), pltpu.SemaphoreType.DMA((2, 2))],
+    )
+    images, stiffness = call(
+        load_kernel,
+        (tile, tile),
+        (*held, to_o),
+        us=1,
+        in_specs=[in_hbm, in_hbm, pl.BlockSpec(memory_space=pltpu.VMEM)],
         scratch_shapes=[pltpu.SemaphoreType.DMA((2, CUTS))],
     )
     row_o = send(to_o, row_odd)
@@ -628,10 +653,10 @@
         us=4,
         scratch_shapes=[vmem(*grid), vmem(3, *grid), vmem(3 * EXT, 3 * 128)],
     )
-    everywhere = [pl.BlockSpec(memory_space=pltpu.VMEM)] * 4
-    tensor, rhs, field, sent_a, sent_b = call(
+    everywhere = [pl.BlockSpec(memory_space=pltpu.VMEM)] * 5
+    tensor, rhs, field, sent_a, sent_b, sent = call(
         first_kernel,
-        (f32(5, 1, TILE, TILE), f32(2, *grid), f32(2, *grid), f32(SENT, 128), f32(SENT, 128)),
+        (f32(5, 1, TILE, TILE), f32(2, *grid), f32(2, *grid), *[f32(rows, 128) for rows in SENT], f32(sum(SENT), 128)),
         (ext, gx, gy, matrix, inverse, known, later_far, later_near, rims_far, rims_near, band),
         mib=20,
         us=5,
@@ -646,15 +671,15 @@
         ],
     )
 
-    near_a, near_b = send(sent_a, sec_even), send(sent_b, sec_even)
+    near = send(sent, sec_even)
     far_a, far_b = send(sent_a, sec_odd), send(sent_b, sec_odd)
     carried = call(
         carry_kernel,
         f32(2, 2, EXT, 128),
-        (rhs, matrix, inverse, field, near_a, near_b),
+        (rhs, matrix, inverse, field, near),
         mib=16,
         us=3,
-        scratch_shapes=[vmem(2, *grid), vmem(2, *grid), vmem(2, *grid), vmem(2, 8 * HALF, 128)],
+        scratch_shapes=[vmem(2, *grid), vmem(2, *grid), vmem(2, *grid), vmem(2, 8 * max(COUNTS), 128)],
     )
     whole = pl.BlockSpec(memory_space=pltpu.VMEM)
     anywhere = pl.BlockSpec(memory_space=pl.ANY)
@@ -663,7 +688,7 @@
         vmem(2, *grid),
         vmem(2, *grid),
         vmem(2, *grid),
-        vmem(2, 8 * HALF, 128),
+        vmem(2, 8 * max(COUNTS), 128),
         vmem(2, TILE, TILE),
         pltpu.SemaphoreType.DMA((2, CUTS)),
     ]

time: 39.9 us -> 39.1 us (0.980)
  waiting for transfers between devices: 12.6 us -> 11.7 us
    ppermute x12 -> x11, waiting for transfers between devices: 12.6 us -> 11.7 us  [send(): return lax.ppermute(value, AXES, found)]
    ppermute x12 -> x11, starting transfers between devices: 11.1 us -> 10.9 us  [send(): return lax.ppermute(value, AXES, found)]
    pallas_call x9 -> x10, Pallas kernels: 14.8 us -> 14.9 us  [call(): pl.pallas_call(kernel, out_shape=out_shape, compiler_params=pltpu.Compile...]
  transfers between devices with their start and end apart: 12 -> 11, of which waited for: 7 -> 7; matrix products, arithmetic and copies ran while one was open for 0% -> 0% of each run, Pallas kernels for 22% -> 25%
where the time goes in v5:
time: 39.1 us; the launch traced here: 38.4 us
  Pallas kernels  14.9 us (38%)
  waiting for transfers between devices  11.7 us (30%)
  starting transfers between devices  10.9 us (28%)
  between operations  0.89 us (2%)
    pallas_call x10, Pallas kernels, call(): pl.pallas_call(kernel, out_shape=out_shape, compiler_params=pltpu.Compile...  14.9 us
    ppermute x11, waiting for transfers between devices, send(): return lax.ppermute(value, AXES, found)  11.7 us
    ppermute x11, starting transfers between devices, send(): return lax.ppermute(value, AXES, found)  10.9 us
  transfers between devices with their start and end apart: 11, of which 7 were waited for; matrix products, arithmetic and copies ran while one was open for 0% of the time, Pallas kernels for 25%

profile of v5, /device:TPU:120, one launch (start us, length us, event | category | flops | bytes accessed | tf_op | source)
XLA Modules:
  0.0 38.4 jit_solution(13706551715068289238)
XLA Ops:
  0.6 0.1 collective-permute-start.5
  0.7 1.3 %collective-permute-start.4 = (f32[1,256,256]{2,1,0:T(8,128)}, f32[1,256,256]{2,1,0:T(8,128)S(1)}, u32[]{:S(2)}, u32[]{:S(2)}) collective-permute-start(f32[1,256,256]{2,1,0:T(8,128)} %image.3), channel_id=1, source_target_pairs={{0,16},{1,17},{2,18},{3,19},{4,20},{5,21},{6,22},{7,23},{8,24},{9,... | collective-permute-start | bytes 786440 | tf_op jit(solution)/shard_map/ppermute | solution.py:50
  2.1 0.8 %shard_map.41 = (f32[32,256]{1,0:T(8,128)S(1)}, f32[32,256]{1,0:T(8,128)S(1)}) custom-call(f32[1,256,256]{2,1,0:T(8,128)} %image.3, f32[1,256,256]{2,1,0:T(8,128)} %stiff.3), custom_call_target="tpu_custom_call" | custom-call | flops 1000000 | bytes 3000000 | tf_op jit(solution)/shard_map/pallas_call | solution.py:603
  2.9 1.6 %collective-permute-start.1 = (f32[32,256]{1,0:T(8,128)S(1)}, f32[32,256]{1,0:T(8,128)S(1)}, u32[]{:S(2)}, u32[]{:S(2)}) collective-permute-start(f32[32,256]{1,0:T(8,128)S(1)} %get-tuple-element.25), channel_id=1, source_target_pairs={{0,16},{1,17},{2,18},{3,19},{4,20},{5,21},{6,22},{7,23},{8,24},{9,... | collective-permute-start | bytes 98312 | tf_op jit(solution)/shard_map/ppermute | solution.py:50
  4.5 0.0 collective-permute-start
  4.5 1.1 %shard_map.42 = (f32[1,256,256]{2,1,0:T(8,128)S(1)}, f32[1,256,256]{2,1,0:T(8,128)S(1)}) custom-call(f32[1,256,256]{2,1,0:T(8,128)} %image.3, f32[1,256,256]{2,1,0:T(8,128)} %stiff.3, f32[32,256]{1,0:T(8,128)S(1)} %get-tuple-element.22.after.start), custom_call_target="tpu_custom_call" | custom-call | flops 1000000 | bytes 3000000 | tf_op jit(solution)/shard_map/pallas_call | solution.py:603
  5.6 1.7 %collective-permute-done.1.row_e = f32[32,256]{1,0:T(8,128)S(1)} collective-permute-done((f32[32,256]{1,0:T(8,128)S(1)}, f32[32,256]{1,0:T(8,128)S(1)}, u32[]{:S(2)}, u32[]{:S(2)}) %collective-permute-start.1) | collective-permute-done | bytes 32800 | tf_op jit(solution)/shard_map/ppermute | solution.py:50
  7.3 1.1 %collective-permute-done.row_o = f32[32,256]{1,0:T(8,128)S(1)} collective-permute-done((f32[32,256]{1,0:T(8,128)S(1)}, f32[32,256]{1,0:T(8,128)S(1)}, u32[]{:S(2)}, u32[]{:S(2)}) %collective-permute-start) | collective-permute-done | bytes 32800 | tf_op jit(solution)/shard_map/ppermute | solution.py:50
  8.4 0.2 shard_map.43
  8.6 3.6 %collective-permute-start.2 = (f32[80,128]{1,0:T(8,128)S(1)}, f32[80,128]{1,0:T(8,128)S(1)}, u32[]{:S(2)}, u32[]{:S(2)}) collective-permute-start(f32[80,128]{1,0:T(8,128)S(1)} %get-tuple-element.26), channel_id=1, source_target_pairs={{0,16},{1,2},{2,1},{3,4},{4,3},{5,6},{6,5},{7,8},{8,7},{9,10},{10,... | collective-permute-start | bytes 122888 | tf_op jit(solution)/shard_map/ppermute | solution.py:50
  12.2 0.0 collective-permute-start.3
  12.2 2.6 %collective-permute-done.2.col_o = f32[80,128]{1,0:T(8,128)S(1)} collective-permute-done((f32[80,128]{1,0:T(8,128)S(1)}, f32[80,128]{1,0:T(8,128)S(1)}, u32[]{:S(2)}, u32[]{:S(2)}) %collective-permute-start.2) | collective-permute-done | bytes 40992 | tf_op jit(solution)/shard_map/ppermute | solution.py:50
  14.8 1.4 %collective-permute-done.3.col_e = f32[80,128]{1,0:T(8,128)S(1)} collective-permute-done((f32[80,128]{1,0:T(8,128)S(1)}, f32[80,128]{1,0:T(8,128)S(1)}, u32[]{:S(2)}, u32[]{:S(2)}) %collective-permute-start.3) | collective-permute-done | bytes 40992 | tf_op jit(solution)/shard_map/ppermute | solution.py:50
  16.2 0.0 collective-permute-start.7
  16.2 0.8 %collective-permute-start.6 = (f32[144,128]{1,0:T(8,128)S(1)}, f32[144,128]{1,0:T(8,128)S(1)}, u32[]{:S(2)}, u32[]{:S(2)}) collective-permute-start(f32[144,128]{1,0:T(8,128)S(1)} %shard_map.46), channel_id=1, source_target_pairs={{0,16},{1,17},{2,18},{3,19},{4,20},{5,21},{6,22},{7,23},{8,24},{9,... | collective-permute-start | bytes 221192 | tf_op jit(solution)/shard_map/ppermute | solution.py:50
  17.1 0.1 shard_map.44.band
  17.1 2.9 %shard_map.45 = (f32[3,304,128]{2,1,0:T(8,128)S(1)}, f32[3,288,128]{2,1,0:T(8,128)S(1)}, f32[3,288,128]{2,1,0:T(8,128)S(1)}, f32[3,3,288,128]{3,2,1,0:T(8,128)S(...) custom-call(f32[1,256,256]{2,1,0:T(8,128)S(1)} %get-tuple-element.23.image, ...), custom_call_target="tpu_custom_call" | custom-call | flops 4000000 | bytes 12000000 | tf_op jit(solution)/shard_map/pallas_call | solution.py:603
  20.0 0.0 collective-permute-done.7.near
  20.0 1.6 %collective-permute-done.6.far = f32[144,128]{1,0:T(8,128)S(1)} collective-permute-done((f32[144,128]{1,0:T(8,128)S(1)}, f32[144,128]{1,0:T(8,128)S(1)}, u32[]{:S(2)}, u32[]{:S(2)}) %collective-permute-start.6) | collective-permute-done | bytes 73760 | tf_op jit(solution)/shard_map/ppermute | solution.py:50
  21.6 0.0 collective-permute-done.5.later_near
  21.6 0.0 collective-permute-done.4.later_far
  21.6 4.1 %shard_map.47 = (f32[5,1,256,256]{3,2,1,0:T(8,128)}, f32[2,3,288,128]{3,2,1,0:T(8,128)S(1)}, f32[2,3,288,128]{3,2,1,0:T(8,128)S(1)}, f32[752,128]{1,0:T(8,128)S(...) custom-call(f32[3,304,128]{2,1,0:T(8,128)S(1)} %get-tuple-element.28.ext, f32[3,288,128]{2,1,0:T(8,128)S(1)} %get-tuple-element.29.gx, ...), custom_call_target="tpu_custom_call" | custom-call | flops 5000000 | bytes 15000000 | tf_op jit(solution)/shard_map/pallas_call | solution.py:603
  25.7 0.1 collective-permute-start.8
  25.8 1.0 %collective-permute-start.10 = (f32[752,128]{1,0:T(8,128)S(1)}, f32[752,128]{1,0:T(8,128)S(1)}, u32[]{:S(2)}, u32[]{:S(2)}) collective-permute-start(f32[752,128]{1,0:T(8,128)S(1)} %get-tuple-element.39), channel_id=1, source_target_pairs={{0,16},{1,17},{2,18},{3,19},{4,20},{5,21},{6,22},{7,23},{8,24},{9,... | collective-permute-start | bytes 1155080 | tf_op jit(solution)/shard_map/ppermute | solution.py:50
  26.8 2.3 %collective-permute-start.9 = (f32[432,128]{1,0:T(8,128)S(1)}, f32[432,128]{1,0:T(8,128)S(1)}, u32[]{:S(2)}, u32[]{:S(2)}) collective-permute-start(f32[432,128]{1,0:T(8,128)S(1)} %get-tuple-element.38), channel_id=1, source_target_pairs={{0,16},{1,17},{2,18},{3,19},{4,20},{5,21},{6,22},{7,23},{8,24},{9,... | collective-permute-start | bytes 663560 | tf_op jit(solution)/shard_map/ppermute | solution.py:50
  29.2 0.0 collective-permute-done.8.near
  29.2 2.6 %shard_map.48.carried = f32[2,2,288,128]{3,2,1,0:T(8,128)S(1)} custom-call(f32[2,3,288,128]{3,2,1,0:T(8,128)S(1)} %get-tuple-element.35.rhs, f32[3,3,288,128]{3,2,1,0:T(8,128)S(1)} %get-tuple-element.31.matrix, f32[3,288,128]{2,1,0:T(8,128)S(1)} %get-tuple-element.32.inverse, f32[2,3,288,128]{3,2,1,0:T(8,128)S(1)} %get-tuple-element.36.field, ...), custom_call_target="tpu_custom_call" | custom-call | flops 3000000 | bytes 9000000 | tf_op jit(solution)/shard_map/pallas_call | solution.py:603
  31.8 2.7 %collective-permute-done.10.far = f32[752,128]{1,0:T(8,128)S(1)} collective-permute-done((f32[752,128]{1,0:T(8,128)S(1)}, f32[752,128]{1,0:T(8,128)S(1)}, u32[]{:S(2)}, u32[]{:S(2)}) %collective-permute-start.10) | collective-permute-done | bytes 385056 | tf_op jit(solution)/shard_map/ppermute | solution.py:50
  34.5 1.8 %shard_map.49 = (f32[2,1,256,256]{3,2,1,0:T(8,128)}, f32[2,2,16,128]{3,2,1,0:T(8,128)S(1)}) custom-call(f32[3,3,288,128]{3,2,1,0:T(8,128)S(1)} %get-tuple-element.31.matrix, f32[3,288,128]{2,1,0:T(8,128)S(1)} %get-tuple-element.32.inverse, f32[2,2,288,128]{3,2,1,0:T(8,128)S(1)} %shard_map.48.carried, f32[752,128]{1,0:T(8,128)S(1)} %collective-permute-done.10.far), custom_call_target="tpu_custom_call" | custom-call | flops 2000000 | bytes 6000000 | tf_op jit(solution)/shard_map/pallas_call | solution.py:603
  36.3 0.6 %collective-permute-done.9.far = f32[432,128]{1,0:T(8,128)S(1)} collective-permute-done((f32[432,128]{1,0:T(8,128)S(1)}, f32[432,128]{1,0:T(8,128)S(1)}, u32[]{:S(2)}, u32[]{:S(2)}) %collective-permute-start.9) | collective-permute-done | bytes 221216 | tf_op jit(solution)/shard_map/ppermute | solution.py:50
  36.9 1.3 %shard_map.50 = f32[2,1,256,256]{3,2,1,0:T(8,128)} custom-call(f32[3,3,288,128]{3,2,1,0:T(8,128)S(1)} %get-tuple-element.31.matrix, f32[3,288,128]{2,1,0:T(8,128)S(1)} %get-tuple-element.32.inverse, f32[2,2,288,128]{3,2,1,0:T(8,128)S(1)} %shard_map.48.carried, f32[432,128]{1,0:T(8,128)S(1)} %collective-permute-done.9.far, ...), custom_call_target="tpu_custom_call", output_to_operand_aliasing={{}: (5, {})} | custom-call | flops 2000000 | bytes 6000000 | tf_op jit(solution)/shard_map/pallas_call | solution.py:603
  (1 shorter events, 0.0 us)
Async XLA Ops:
  0.6 21.0 %collective-permute-start.5 = (f32[1,256,256]{2,1,0:T(8,128)}, f32[1,256,256]{2,1,0:T(8,128)S(1)}, u32[]{:S(2)}, u32[]{:S(2)}) collective-permute-start(f32[1,256,256]{2,1,0:T(8,128)} %image.3), channel_id=1, source_target_pairs={{0,64},{1,65},{2,66},{3,67},{4,68},{5,69},{6,70},{7,71},{8,72},{9,... | collective-permute-start | bytes 786440 | tf_op jit(solution)/shard_map/ppermute | solution.py:50
  0.7 20.9 %collective-permute-start.4 = (f32[1,256,256]{2,1,0:T(8,128)}, f32[1,256,256]{2,1,0:T(8,128)S(1)}, u32[]{:S(2)}, u32[]{:S(2)}) collective-permute-start(f32[1,256,256]{2,1,0:T(8,128)} %image.3), channel_id=1, source_target_pairs={{0,16},{1,17},{2,18},{3,19},{4,20},{5,21},{6,22},{7,23},{8,24},{9,... | collective-permute-start | bytes 786440 | tf_op jit(solution)/shard_map/ppermute | solution.py:50
  2.9 4.4 %collective-permute-start.1 = (f32[32,256]{1,0:T(8,128)S(1)}, f32[32,256]{1,0:T(8,128)S(1)}, u32[]{:S(2)}, u32[]{:S(2)}) collective-permute-start(f32[32,256]{1,0:T(8,128)S(1)} %get-tuple-element.25), channel_id=1, source_target_pairs={{0,16},{1,17},{2,18},{3,19},{4,20},{5,21},{6,22},{7,23},{8,24},{9,... | collective-permute-start | bytes 98312 | tf_op jit(solution)/shard_map/ppermute | solution.py:50
  4.5 3.9 %collective-permute-start = (f32[32,256]{1,0:T(8,128)S(1)}, f32[32,256]{1,0:T(8,128)S(1)}, u32[]{:S(2)}, u32[]{:S(2)}) collective-permute-start(f32[32,256]{1,0:T(8,128)S(1)} %get-tuple-element.22.after.start), channel_id=1, source_target_pairs={{0,1},{1,0},{2,3},{3,2},{4,5},{5,4},{6,7},{7,6},{8,9},{9,8},{10,11... | collective-permute-start | bytes 98312 | tf_op jit(solution)/shard_map/ppermute | solution.py:50
  8.6 6.2 %collective-permute-start.2 = (f32[80,128]{1,0:T(8,128)S(1)}, f32[80,128]{1,0:T(8,128)S(1)}, u32[]{:S(2)}, u32[]{:S(2)}) collective-permute-start(f32[80,128]{1,0:T(8,128)S(1)} %get-tuple-element.26), channel_id=1, source_target_pairs={{0,16},{1,2},{2,1},{3,4},{4,3},{5,6},{6,5},{7,8},{8,7},{9,10},{10,... | collective-permute-start | bytes 122888 | tf_op jit(solution)/shard_map/ppermute | solution.py:50
  12.2 4.0 %collective-permute-start.3 = (f32[80,128]{1,0:T(8,128)S(1)}, f32[80,128]{1,0:T(8,128)S(1)}, u32[]{:S(2)}, u32[]{:S(2)}) collective-permute-start(f32[80,128]{1,0:T(8,128)S(1)} %get-tuple-element.27), channel_id=1, source_target_pairs={{0,1},{1,0},{2,3},{3,2},{4,5},{5,4},{6,7},{7,6},{8,9},{9,8},{10,11... | collective-permute-start | bytes 122888 | tf_op jit(solution)/shard_map/ppermute | solution.py:50
  16.2 3.8 %collective-permute-start.7 = (f32[144,128]{1,0:T(8,128)S(1)}, f32[144,128]{1,0:T(8,128)S(1)}, u32[]{:S(2)}, u32[]{:S(2)}) collective-permute-start(f32[144,128]{1,0:T(8,128)S(1)} %shard_map.46), channel_id=1, source_target_pairs={{0,64},{1,65},{2,66},{3,67},{4,68},{5,69},{6,70},{7,71},{8,72},{9,... | collective-permute-start | bytes 221192 | tf_op jit(solution)/shard_map/ppermute | solution.py:50
  16.2 5.4 %collective-permute-start.6 = (f32[144,128]{1,0:T(8,128)S(1)}, f32[144,128]{1,0:T(8,128)S(1)}, u32[]{:S(2)}, u32[]{:S(2)}) collective-permute-start(f32[144,128]{1,0:T(8,128)S(1)} %shard_map.46), channel_id=1, source_target_pairs={{0,16},{1,17},{2,18},{3,19},{4,20},{5,21},{6,22},{7,23},{8,24},{9,... | collective-permute-start | bytes 221192 | tf_op jit(solution)/shard_map/ppermute | solution.py:50
  25.7 3.4 %collective-permute-start.8 = (f32[1184,128]{1,0:T(8,128)S(1)}, f32[1184,128]{1,0:T(8,128)S(1)}, u32[]{:S(2)}, u32[]{:S(2)}) collective-permute-start(f32[1184,128]{1,0:T(8,128)S(1)} %get-tuple-element.37), channel_id=1, source_target_pairs={{0,64},{1,65},{2,66},{3,67},{4,68},{5,69},{6,70},{7,71},{8,72},{9,... | collective-permute-start | bytes 1818632 | tf_op jit(solution)/shard_map/ppermute | solution.py:50
  25.8 8.7 %collective-permute-start.10 = (f32[752,128]{1,0:T(8,128)S(1)}, f32[752,128]{1,0:T(8,128)S(1)}, u32[]{:S(2)}, u32[]{:S(2)}) collective-permute-start(f32[752,128]{1,0:T(8,128)S(1)} %get-tuple-element.39), channel_id=1, source_target_pairs={{0,16},{1,17},{2,18},{3,19},{4,20},{5,21},{6,22},{7,23},{8,24},{9,... | collective-permute-start | bytes 1155080 | tf_op jit(solution)/shard_map/ppermute | solution.py:50
  26.8 10.1 %collective-permute-start.9 = (f32[432,128]{1,0:T(8,128)S(1)}, f32[432,128]{1,0:T(8,128)S(1)}, u32[]{:S(2)}, u32[]{:S(2)}) collective-permute-start(f32[432,128]{1,0:T(8,128)S(1)} %get-tuple-element.38), channel_id=1, source_target_pairs={{0,16},{1,17},{2,18},{3,19},{4,20},{5,21},{6,22},{7,23},{8,24},{9,... | collective-permute-start | bytes 663560 | tf_op jit(solution)/shard_map/ppermute | solution.py:50

commit v6 on v5

--- a/solution.py
+++ b/solution.py
@@ -18,7 +18,7 @@
 INNER = BLOCKS - 2
 GROUP = 5
 FIELD_RIM = 8
-COUNTS = (22, INNER - 22)
+COUNTS = (24, INNER - 24)
 STARTS = (1, 1 + COUNTS[0])
 FOLD = 3
 SENT = [32 * count + 16 * FOLD for count in COUNTS]
@@ -365,17 +365,11 @@
 
 
 def first_kernel(
-    ext, gx, gy, matrix, inverse, known, later_far, later_near, far, near, band,
-    tensor, rhs, field, sent_a, sent_b, sent,
-    chg, sums, prods, work, fresh, sems,
+    ext, gx, gy, matrix, inverse, later_far, later_near, far, near, band,
+    fresh, rhs, field, work, done, sent,
+    chg, sums, prods,
 ):
-    lane = lanes()
-    zero = jnp.zeros((8, 128), jnp.float32)
     s, secs = lax.axis_index("sec"), lax.axis_size("sec")
-    inner = pl.ds(RIM, TILE)
-    copies = [pltpu.make_async_copy(known.at[:, inner], tensor.at[pl.ds(0, 3), 0], sems.at[0])]
-    copies[0].start()
-
     use_far, use_near = lax.rem(s, 2) == 1, s < secs - 1
 
     def pick(a, b):
@@ -441,46 +435,60 @@
             work[1, k, at, :] = ry
         return carry
 
-    lax.fori_loop(1, BLOCKS - 1, right_side, 0, unroll=17)
-    copies.append(pltpu.make_async_copy(fresh.at[:, inner], tensor.at[pl.ds(3, 2), 0], sems.at[1]))
-    copies[1].start()
-
-    step(work, field, rhs, matrix)
-    step(field, work, rhs, matrix)
-
-    for half, part in enumerate((sent_a, sent_b)):
-        start, count, base = STARTS[half], COUNTS[half], SENT[0] * half
-
-        def last(block, carry):
-            new = sweep(work, rhs, matrix, block)
-            at = pl.ds(pl.multiple_of(8 * block, 8), 8)
-            for comp in range(2):
-                for k in range(3):
-                    field[comp, k, at, :] = new[comp][k]
-                for k in range(2):
-                    to = pl.multiple_of(8 * ((2 * comp + k) * count + block - start), 8)
-                    value = new[comp][k] * inverse[k, at, :]
-                    part[pl.ds(to, 8), :] = value
-                    sent[pl.ds(pl.multiple_of(base + to, 8), 8), :] = value
-            return carry
-
-        lax.fori_loop(start, start + count, last, 0, unroll=count)
-
+    lax.fori_loop(1, BLOCKS - 1, right_side, 0, unroll=INNER)
+    edge = COUNTS[0]
+    step(work, field, rhs, matrix, 1, edge + 4, edge // 2 + 2)
+    step(field, work, rhs, matrix, 1, edge + 2, edge // 2 + 1)
+    send_part(0, work, done, sent, rhs, matrix, inverse)
+
+
+def send_part(half, src, dst, sent, rhs, matrix, inverse):
+    lane = lanes()
+    start, count = STARTS[half], COUNTS[half]
+
+    def last(block, carry):
+        new = sweep(src, rhs, matrix, block)
+        at = pl.ds(pl.multiple_of(8 * block, 8), 8)
         for comp in range(2):
-            strip = [zero] * FOLD
-            for n in range(count):
-                g, place = divmod(n, FOLD)
-                at = pl.ds(8 * (start + n), 8)
-                tile = pltpu.roll(field[comp, 2, at, :] * inverse[2, at, :], FIELD_RIM + 16 * g, 1)
-                strip[place] = jnp.where((lane >= 16 * g) & (lane < 16 * g + 16), tile, strip[place])
-            for place in range(FOLD):
-                for ref, at in ((part, 0), (sent, base)):
-                    ref[pl.ds(at + 32 * count + 8 * (FOLD * comp + place), 8), :] = strip[place]
-    for copy in copies:
-        copy.wait()
-
-
-def beside_terms(half, received, matrix, inverse, strips, store, base=0, ok=None):
+            for k in range(3):
+                dst[comp, k, at, :] = new[comp][k]
+            for k in range(2):
+                to = pl.multiple_of(8 * ((2 * comp + k) * count + block - start), 8)
+                sent[pl.ds(to, 8), :] = new[comp][k] * inverse[k, at, :]
+        return carry
+
+    lax.fori_loop(start, start + count, last, 0, unroll=count)
+
+    for comp in range(2):
+        strip = [jnp.zeros((8, 128), jnp.float32)] * FOLD
+        for n in range(count):
+            g, place = divmod(n, FOLD)
+            at = pl.ds(8 * (start + n), 8)
+            tile = pltpu.roll(dst[comp, 2, at, :] * inverse[2, at, :], FIELD_RIM + 16 * g, 1)
+            strip[place] = jnp.where((lane >= 16 * g) & (lane < 16 * g + 16), tile, strip[place])
+        for place in range(FOLD):
+            sent[pl.ds(32 * count + 8 * (FOLD * comp + place), 8), :] = strip[place]
+
+
+def tail_kernel(rhs, matrix, inverse, once, twice, done, after, field, sent, second, third):
+    edge = COUNTS[0]
+    for ref in (second, third, field):
+        clear_rims(ref)
+    for comp in range(2):
+        for k in range(3):
+            for dst, src, low in ((second, twice, edge + 2), (third, once, edge)):
+                for block in range(low, low + 3):
+                    at = pl.ds(8 * block, 8)
+                    dst[comp, k, at, :] = src[comp, k, at, :]
+            for block in range(1, edge + 1):
+                at = pl.ds(8 * block, 8)
+                field[comp, k, at, :] = done[comp, k, at, :]
+    step(once, second, rhs, matrix, edge + 5, INNER, INNER - edge - 4)
+    step(second, third, rhs, matrix, edge + 3, INNER, INNER - edge - 2)
+    send_part(1, third, field, sent, rhs, matrix, inverse)
+
+
+def beside_terms(half, received, matrix, inverse, strips, store, ok=None):
     lane = lanes()
     start, count = STARTS[half], COUNTS[half]
 
@@ -490,7 +498,7 @@
     for comp in range(2):
         for n in range(count):
             g, place = divmod(n, FOLD)
-            tile = read(pl.ds(base + 32 * count + 8 * (FOLD * comp + place), 8))
+            tile = read(pl.ds(32 * count + 8 * (FOLD * comp + place), 8))
             tile = pltpu.roll(tile, 128 - FIELD_RIM - 16 * g, 1)
             strips[comp, pl.ds(8 * n, 8), :] = jnp.where((lane < FIELD_RIM) | (lane >= 128 - FIELD_RIM), tile, 0.0)
 
@@ -500,7 +508,7 @@
             pair = []
             for comp in range(2):
                 if k < 2:
-                    value = read(pl.ds(pl.multiple_of(base + 8 * ((2 * comp + k) * count + n), 8), 8))
+                    value = read(pl.ds(pl.multiple_of(8 * ((2 * comp + k) * count + n), 8), 8))
                 else:
                     value = strips[comp, pl.ds(pl.multiple_of(8 * n, 8), 8), :]
                 pair.append(value * (inverse[k, at, :] * COUPLING))
@@ -511,7 +519,19 @@
     lax.fori_loop(0, count, body, 0, unroll=count)
 
 
-def carry_kernel(rhs, matrix, inverse, field, near, out, moved, work_a, work_b, strips):
+def carry_kernel(
+    rhs, matrix, inverse, field, near_a, near_b, known, fresh,
+    out, tensor,
+    moved, work_a, work_b, strips, sems,
+):
+    inner = pl.ds(RIM, TILE)
+    copies = [
+        pltpu.make_async_copy(src.at[p, inner], tensor.at[base + p, 0], sems.at[base + p])
+        for src, base, count in ((known, 0, 3), (fresh, 3, 2))
+        for p in range(count)
+    ]
+    for copy in copies:
+        copy.start()
     clear_rims(work_a)
     clear_rims(work_b)
 
@@ -519,8 +539,8 @@
         moved[0, k, at, :] = rhs[0, k, at, :] + x
         moved[1, k, at, :] = rhs[1, k, at, :] + y
 
-    for half in range(2):
-        beside_terms(half, near, matrix, inverse, strips, store, SENT[0] * half)
+    for half, near in enumerate((near_a, near_b)):
+        beside_terms(half, near, matrix, inverse, strips, store)
     step(field, work_a, moved, matrix)
     step(work_a, work_b, moved, matrix)
     step(work_b, work_a, moved, matrix)
@@ -534,6 +554,8 @@
         return carry
 
     lax.fori_loop(2, BLOCKS - 2, last, 0, unroll=16)
+    for copy in copies:
+        copy.wait()
 
 
 def second_kernel(half, matrix, inverse, carried, far, *rest):
@@ -557,7 +579,7 @@
         moved[0, k, at, :] = x
         moved[1, k, at, :] = y
 
-    beside_terms(half, far, matrix, inverse, strips, store, ok=inside)
+    beside_terms(half, far, matrix, inverse, strips, store, inside)
     step(moved, work_a, moved, matrix, low, high, high + 1 - low)
     step(work_a, work_b, moved, matrix, low, high, high + 1 - low)
 
@@ -653,36 +675,44 @@
         us=4,
         scratch_shapes=[vmem(*grid), vmem(3, *grid), vmem(3 * EXT, 3 * 128)],
     )
-    everywhere = [pl.BlockSpec(memory_space=pltpu.VMEM)] * 5
-    tensor, rhs, field, sent_a, sent_b, sent = call(
+    fresh, rhs, twice, once, done, sent_a = call(
         first_kernel,
-        (f32(5, 1, TILE, TILE), f32(2, *grid), f32(2, *grid), *[f32(rows, 128) for rows in SENT], f32(sum(SENT), 128)),
-        (ext, gx, gy, matrix, inverse, known, later_far, later_near, rims_far, rims_near, band),
+        (f32(2, EXT, TILE), *[f32(2, *grid)] * 4, f32(SENT[0], 128)),
+        (ext, gx, gy, matrix, inverse, later_far, later_near, rims_far, rims_near, band),
         mib=20,
         us=5,
-        out_specs=[pl.BlockSpec(memory_space=pl.ANY)] + everywhere,
+        scratch_shapes=[vmem(*grid), vmem(2, *grid), vmem(2 * EXT, 3 * 128)],
+    )
+
+    far_a = send(sent_a, sec_odd)
+    near_a = send(sent_a, sec_even)
+    field, sent_b = call(
+        tail_kernel,
+        (f32(2, *grid), f32(SENT[1], 128)),
+        (rhs, matrix, inverse, once, twice, done, near_a),
+        mib=16,
+        us=1,
+        scratch_shapes=[vmem(2, *grid), vmem(2, *grid)],
+    )
+    far_b = send(sent_b, sec_odd)
+    near_b = send(sent_b, sec_even)
+    whole = pl.BlockSpec(memory_space=pltpu.VMEM)
+    anywhere = pl.BlockSpec(memory_space=pl.ANY)
+    carried, tensor = call(
+        carry_kernel,
+        (f32(2, 2, EXT, 128), f32(5, 1, TILE, TILE)),
+        (rhs, matrix, inverse, field, near_a, near_b, known, fresh),
+        mib=16,
+        us=3,
+        out_specs=[whole, anywhere],
         scratch_shapes=[
-            vmem(*grid),
             vmem(2, *grid),
-            vmem(2 * EXT, 3 * 128),
             vmem(2, *grid),
-            vmem(2, EXT, TILE),
-            pltpu.SemaphoreType.DMA((2,)),
+            vmem(2, *grid),
+            vmem(2, 8 * max(COUNTS), 128),
+            pltpu.SemaphoreType.DMA((5,)),
         ],
     )
-
-    near = send(sent, sec_even)
-    far_a, far_b = send(sent_a, sec_odd), send(sent_b, sec_odd)
-    carried = call(
-        carry_kernel,
-        f32(2, 2, EXT, 128),
-        (rhs, matrix, inverse, field, near),
-        mib=16,
-        us=3,
-        scratch_shapes=[vmem(2, *grid), vmem(2, *grid), vmem(2, *grid), vmem(2, 8 * max(COUNTS), 128)],
-    )
-    whole = pl.BlockSpec(memory_space=pltpu.VMEM)
-    anywhere = pl.BlockSpec(memory_space=pl.ANY)
     final = f32(2, 1, TILE, TILE)
     scratch = [
         vmem(2, *grid),

time: 39.1 us -> 38.2 us (0.977)
  Pallas kernels: 14.9 us -> 14.5 us
  starting transfers between devices: 10.9 us -> 10.5 us
    pallas_call x10 -> x11, Pallas kernels: 14.9 us -> 14.5 us  [call(): pl.pallas_call(kernel, out_shape=out_shape, compiler_params=pltpu.Compile...]
    ppermute x11 -> x12, starting transfers between devices: 10.9 us -> 10.5 us  [send(): return lax.ppermute(value, AXES, found)]
    ppermute x11 -> x12, waiting for transfers between devices: 11.7 us -> 11.6 us  [send(): return lax.ppermute(value, AXES, found)]
  transfers between devices with their start and end apart: 11 -> 12, of which waited for: 7 -> 8; matrix products, arithmetic and copies ran while one was open for 0% -> 0% of each run, Pallas kernels for 25% -> 27%
where the time goes in v6:
time: 38.2 us; the launch traced here: 37.5 us
  Pallas kernels  14.5 us (38%)
  waiting for transfers between devices  11.6 us (30%)
  starting transfers between devices  10.5 us (27%)
  between operations  0.88 us (2%)
    pallas_call x11, Pallas kernels, call(): pl.pallas_call(kernel, out_shape=out_shape, compiler_params=pltpu.Compile...  14.5 us
    ppermute x12, waiting for transfers between devices, send(): return lax.ppermute(value, AXES, found)  11.6 us
    ppermute x12, starting transfers between devices, send(): return lax.ppermute(value, AXES, found)  10.5 us
  transfers between devices with their start and end apart: 12, of which 8 were waited for; matrix products, arithmetic and copies ran while one was open for 0% of the time, Pallas kernels for 27%

profile of v6, /device:TPU:120, one launch (start us, length us, event | category | flops | bytes accessed | tf_op | source)
XLA Modules:
  0.0 37.5 jit_solution(5970687176900992525)
XLA Ops:
  0.6 0.1 collective-permute-start.5
  0.7 1.3 %collective-permute-start.4 = (f32[1,256,256]{2,1,0:T(8,128)}, f32[1,256,256]{2,1,0:T(8,128)S(1)}, u32[]{:S(2)}, u32[]{:S(2)}) collective-permute-start(f32[1,256,256]{2,1,0:T(8,128)} %image.3), channel_id=1, source_target_pairs={{0,16},{1,17},{2,18},{3,19},{4,20},{5,21},{6,22},{7,23},{8,24},{9,... | collective-permute-start | bytes 786440 | tf_op jit(solution)/shard_map/ppermute | solution.py:50
  2.1 0.8 %shard_map.41 = (f32[32,256]{1,0:T(8,128)S(1)}, f32[32,256]{1,0:T(8,128)S(1)}) custom-call(f32[1,256,256]{2,1,0:T(8,128)} %image.3, f32[1,256,256]{2,1,0:T(8,128)} %stiff.3), custom_call_target="tpu_custom_call" | custom-call | flops 1000000 | bytes 3000000 | tf_op jit(solution)/shard_map/pallas_call | solution.py:625
  2.9 1.6 %collective-permute-start.1 = (f32[32,256]{1,0:T(8,128)S(1)}, f32[32,256]{1,0:T(8,128)S(1)}, u32[]{:S(2)}, u32[]{:S(2)}) collective-permute-start(f32[32,256]{1,0:T(8,128)S(1)} %get-tuple-element.29), channel_id=1, source_target_pairs={{0,16},{1,17},{2,18},{3,19},{4,20},{5,21},{6,22},{7,23},{8,24},{9,... | collective-permute-start | bytes 98312 | tf_op jit(solution)/shard_map/ppermute | solution.py:50
  4.5 0.0 collective-permute-start
  4.5 1.1 %shard_map.42 = (f32[1,256,256]{2,1,0:T(8,128)S(1)}, f32[1,256,256]{2,1,0:T(8,128)S(1)}) custom-call(f32[1,256,256]{2,1,0:T(8,128)} %image.3, f32[1,256,256]{2,1,0:T(8,128)} %stiff.3, f32[32,256]{1,0:T(8,128)S(1)} %get-tuple-element.26.after.start), custom_call_target="tpu_custom_call" | custom-call | flops 1000000 | bytes 3000000 | tf_op jit(solution)/shard_map/pallas_call | solution.py:625
  5.6 1.7 %collective-permute-done.1.row_e = f32[32,256]{1,0:T(8,128)S(1)} collective-permute-done((f32[32,256]{1,0:T(8,128)S(1)}, f32[32,256]{1,0:T(8,128)S(1)}, u32[]{:S(2)}, u32[]{:S(2)}) %collective-permute-start.1) | collective-permute-done | bytes 32800 | tf_op jit(solution)/shard_map/ppermute | solution.py:50
  7.3 1.1 %collective-permute-done.row_o = f32[32,256]{1,0:T(8,128)S(1)} collective-permute-done((f32[32,256]{1,0:T(8,128)S(1)}, f32[32,256]{1,0:T(8,128)S(1)}, u32[]{:S(2)}, u32[]{:S(2)}) %collective-permute-start) | collective-permute-done | bytes 32800 | tf_op jit(solution)/shard_map/ppermute | solution.py:50
  8.4 0.2 shard_map.43
  8.6 3.6 %collective-permute-start.2 = (f32[80,128]{1,0:T(8,128)S(1)}, f32[80,128]{1,0:T(8,128)S(1)}, u32[]{:S(2)}, u32[]{:S(2)}) collective-permute-start(f32[80,128]{1,0:T(8,128)S(1)} %get-tuple-element.30), channel_id=1, source_target_pairs={{0,16},{1,2},{2,1},{3,4},{4,3},{5,6},{6,5},{7,8},{8,7},{9,10},{10,... | collective-permute-start | bytes 122888 | tf_op jit(solution)/shard_map/ppermute | solution.py:50
  12.2 0.0 collective-permute-start.3
  12.2 2.6 %collective-permute-done.2.col_o = f32[80,128]{1,0:T(8,128)S(1)} collective-permute-done((f32[80,128]{1,0:T(8,128)S(1)}, f32[80,128]{1,0:T(8,128)S(1)}, u32[]{:S(2)}, u32[]{:S(2)}) %collective-permute-start.2) | collective-permute-done | bytes 40992 | tf_op jit(solution)/shard_map/ppermute | solution.py:50
  14.8 1.4 %collective-permute-done.3.col_e = f32[80,128]{1,0:T(8,128)S(1)} collective-permute-done((f32[80,128]{1,0:T(8,128)S(1)}, f32[80,128]{1,0:T(8,128)S(1)}, u32[]{:S(2)}, u32[]{:S(2)}) %collective-permute-start.3) | collective-permute-done | bytes 40992 | tf_op jit(solution)/shard_map/ppermute | solution.py:50
  16.2 0.0 collective-permute-start.7
  16.2 0.8 %collective-permute-start.6 = (f32[144,128]{1,0:T(8,128)S(1)}, f32[144,128]{1,0:T(8,128)S(1)}, u32[]{:S(2)}, u32[]{:S(2)}) collective-permute-start(f32[144,128]{1,0:T(8,128)S(1)} %shard_map.46), channel_id=1, source_target_pairs={{0,16},{1,17},{2,18},{3,19},{4,20},{5,21},{6,22},{7,23},{8,24},{9,... | collective-permute-start | bytes 221192 | tf_op jit(solution)/shard_map/ppermute | solution.py:50
  17.1 0.1 shard_map.44.band
  17.1 2.8 %shard_map.45 = (f32[3,304,128]{2,1,0:T(8,128)S(1)}, f32[3,288,128]{2,1,0:T(8,128)S(1)}, f32[3,288,128]{2,1,0:T(8,128)S(1)}, f32[3,3,288,128]{3,2,1,0:T(8,128)S(...) custom-call(f32[1,256,256]{2,1,0:T(8,128)S(1)} %get-tuple-element.27.image, ...), custom_call_target="tpu_custom_call" | custom-call | flops 4000000 | bytes 12000000 | tf_op jit(solution)/shard_map/pallas_call | solution.py:625
  20.0 0.0 collective-permute-done.7.near
  20.0 1.6 %collective-permute-done.6.far = f32[144,128]{1,0:T(8,128)S(1)} collective-permute-done((f32[144,128]{1,0:T(8,128)S(1)}, f32[144,128]{1,0:T(8,128)S(1)}, u32[]{:S(2)}, u32[]{:S(2)}) %collective-permute-start.6) | collective-permute-done | bytes 73760 | tf_op jit(solution)/shard_map/ppermute | solution.py:50
  21.6 0.0 collective-permute-done.5.later_near
  21.6 0.0 collective-permute-done.4.later_far
  21.6 3.3 %shard_map.47 = (f32[2,288,256]{2,1,0:T(8,128)S(1)}, f32[2,3,288,128]{3,2,1,0:T(8,128)S(1)}, f32[2,3,288,128]{3,2,1,0:T(8,128)S(1)}, f32[2,3,288,128]{3,2,1,0:T(...) custom-call(f32[3,304,128]{2,1,0:T(8,128)S(1)} %get-tuple-element.32.ext, ...), custom_call_target="tpu_custom_call" | custom-call | flops 5000000 | bytes 15000000 | tf_op jit(solution)/shard_map/pallas_call | solution.py:625
  24.9 0.1 collective-permute-start.8
  25.0 1.0 %collective-permute-start.11 = (f32[816,128]{1,0:T(8,128)S(1)}, f32[816,128]{1,0:T(8,128)S(1)}, u32[]{:S(2)}, u32[]{:S(2)}) collective-permute-start(f32[816,128]{1,0:T(8,128)S(1)} %get-tuple-element.41), channel_id=1, source_target_pairs={{0,16},{1,17},{2,18},{3,19},{4,20},{5,21},{6,22},{7,23},{8,24},{9,... | collective-permute-start | bytes 1253384 | tf_op jit(solution)/shard_map/ppermute | solution.py:50
  26.0 0.7 %collective-permute-done.8.after.near_a = f32[816,128]{1,0:T(8,128)S(1)} collective-permute-done((f32[816,128]{1,0:T(8,128)S(1)}, f32[816,128]{1,0:T(8,128)S(1)}, u32[]{:S(2)}, u32[]{:S(2)}) %collective-permute-start.8) | collective-permute-done | bytes 417824 | tf_op jit(solution)/shard_map/ppermute | solution.py:50
  26.8 0.5 %shard_map.48 = (f32[2,3,288,128]{3,2,1,0:T(8,128)S(1)}, f32[368,128]{1,0:T(8,128)S(1)}) custom-call(f32[2,3,288,128]{3,2,1,0:T(8,128)S(1)} %get-tuple-element.37.rhs, f32[3,3,288,128]{3,2,1,0:T(8,128)S(1)} %get-tuple-element.35.matrix, f32[3,288,128]{2,1,0:T(8,128)S(1)} %get-tuple-element.36.inverse, f32[2,3,288,128]{3,2,1,0:T(8,128)S(1)} %get-tuple-element.38.once, ...), custom_call_target="tpu_custom_call" | custom-call | flops 1000000 | bytes 3000000 | tf_op jit(solution)/shard_map/pallas_call | solution.py:625
  27.2 0.2 collective-permute-start.9
  27.5 1.7 %collective-permute-start.10 = (f32[368,128]{1,0:T(8,128)S(1)}, f32[368,128]{1,0:T(8,128)S(1)}, u32[]{:S(2)}, u32[]{:S(2)}) collective-permute-start(f32[368,128]{1,0:T(8,128)S(1)} %get-tuple-element.43), channel_id=1, source_target_pairs={{0,16},{1,17},{2,18},{3,19},{4,20},{5,21},{6,22},{7,23},{8,24},{9,... | collective-permute-start | bytes 565256 | tf_op jit(solution)/shard_map/ppermute | solution.py:50
  29.2 0.0 collective-permute-done.9.near_b
  29.2 2.7 %shard_map.49 = (f32[2,2,288,128]{3,2,1,0:T(8,128)S(1)}, f32[5,1,256,256]{3,2,1,0:T(8,128)}) custom-call(f32[2,3,288,128]{3,2,1,0:T(8,128)S(1)} %get-tuple-element.37.rhs, f32[3,3,288,128]{3,2,1,0:T(8,128)S(1)} %get-tuple-element.35.matrix, f32[3,288,128]{2,1,0:T(8,128)S(1)} %get-tuple-element.36.inverse, f32[2,3,288,128]{3,2,1,0:T(8,128)S(1)} %get-tuple-element.42.field, ...), custom_call_target="tpu_custom_call" | custom-call | flops 3000000 | bytes 9000000 | tf_op jit(solution)/shard_map/pallas_call | solution.py:625
  31.9 2.2 %collective-permute-done.11.far = f32[816,128]{1,0:T(8,128)S(1)} collective-permute-done((f32[816,128]{1,0:T(8,128)S(1)}, f32[816,128]{1,0:T(8,128)S(1)}, u32[]{:S(2)}, u32[]{:S(2)}) %collective-permute-start.11) | collective-permute-done | bytes 417824 | tf_op jit(solution)/shard_map/ppermute | solution.py:50
  34.1 1.8 %shard_map.50 = (f32[2,1,256,256]{3,2,1,0:T(8,128)}, f32[2,2,16,128]{3,2,1,0:T(8,128)S(1)}) custom-call(f32[3,3,288,128]{3,2,1,0:T(8,128)S(1)} %get-tuple-element.35.matrix, f32[3,288,128]{2,1,0:T(8,128)S(1)} %get-tuple-element.36.inverse, f32[2,2,288,128]{3,2,1,0:T(8,128)S(1)} %get-tuple-element.47.carried, f32[816,128]{1,0:T(8,128)S(1)} %collective-permute-done.11.far), custom_call_target="tpu_custom_call" | custom-call | flops 2000000 | bytes 6000000 | tf_op jit(solution)/shard_map/pallas_call | solution.py:625
  35.9 0.2 collective-permute-done.10.far
  36.1 1.2 %shard_map.51 = f32[2,1,256,256]{3,2,1,0:T(8,128)} custom-call(f32[3,3,288,128]{3,2,1,0:T(8,128)S(1)} %get-tuple-element.35.matrix, f32[3,288,128]{2,1,0:T(8,128)S(1)} %get-tuple-element.36.inverse, f32[2,2,288,128]{3,2,1,0:T(8,128)S(1)} %get-tuple-element.47.carried, f32[368,128]{1,0:T(8,128)S(1)} %collective-permute-done.10.far, ...), custom_call_target="tpu_custom_call", output_to_operand_aliasing={{}: (5, {})} | custom-call | flops 2000000 | bytes 6000000 | tf_op jit(solution)/shard_map/pallas_call | solution.py:625
  (1 shorter events, 0.0 us)
Async XLA Ops:
  0.6 21.0 %collective-permute-start.5 = (f32[1,256,256]{2,1,0:T(8,128)}, f32[1,256,256]{2,1,0:T(8,128)S(1)}, u32[]{:S(2)}, u32[]{:S(2)}) collective-permute-start(f32[1,256,256]{2,1,0:T(8,128)} %image.3), channel_id=1, source_target_pairs={{0,64},{1,65},{2,66},{3,67},{4,68},{5,69},{6,70},{7,71},{8,72},{9,... | collective-permute-start | bytes 786440 | tf_op jit(solution)/shard_map/ppermute | solution.py:50
  0.7 20.9 %collective-permute-start.4 = (f32[1,256,256]{2,1,0:T(8,128)}, f32[1,256,256]{2,1,0:T(8,128)S(1)}, u32[]{:S(2)}, u32[]{:S(2)}) collective-permute-start(f32[1,256,256]{2,1,0:T(8,128)} %image.3), channel_id=1, source_target_pairs={{0,16},{1,17},{2,18},{3,19},{4,20},{5,21},{6,22},{7,23},{8,24},{9,... | collective-permute-start | bytes 786440 | tf_op jit(solution)/shard_map/ppermute | solution.py:50
  2.9 4.4 %collective-permute-start.1 = (f32[32,256]{1,0:T(8,128)S(1)}, f32[32,256]{1,0:T(8,128)S(1)}, u32[]{:S(2)}, u32[]{:S(2)}) collective-permute-start(f32[32,256]{1,0:T(8,128)S(1)} %get-tuple-element.29), channel_id=1, source_target_pairs={{0,16},{1,17},{2,18},{3,19},{4,20},{5,21},{6,22},{7,23},{8,24},{9,... | collective-permute-start | bytes 98312 | tf_op jit(solution)/shard_map/ppermute | solution.py:50
  4.5 3.9 %collective-permute-start = (f32[32,256]{1,0:T(8,128)S(1)}, f32[32,256]{1,0:T(8,128)S(1)}, u32[]{:S(2)}, u32[]{:S(2)}) collective-permute-start(f32[32,256]{1,0:T(8,128)S(1)} %get-tuple-element.26.after.start), channel_id=1, source_target_pairs={{0,1},{1,0},{2,3},{3,2},{4,5},{5,4},{6,7},{7,6},{8,9},{9,8},{10,11... | collective-permute-start | bytes 98312 | tf_op jit(solution)/shard_map/ppermute | solution.py:50
  8.6 6.2 %collective-permute-start.2 = (f32[80,128]{1,0:T(8,128)S(1)}, f32[80,128]{1,0:T(8,128)S(1)}, u32[]{:S(2)}, u32[]{:S(2)}) collective-permute-start(f32[80,128]{1,0:T(8,128)S(1)} %get-tuple-element.30), channel_id=1, source_target_pairs={{0,16},{1,2},{2,1},{3,4},{4,3},{5,6},{6,5},{7,8},{8,7},{9,10},{10,... | collective-permute-start | bytes 122888 | tf_op jit(solution)/shard_map/ppermute | solution.py:50
  12.2 4.0 %collective-permute-start.3 = (f32[80,128]{1,0:T(8,128)S(1)}, f32[80,128]{1,0:T(8,128)S(1)}, u32[]{:S(2)}, u32[]{:S(2)}) collective-permute-start(f32[80,128]{1,0:T(8,128)S(1)} %get-tuple-element.31), channel_id=1, source_target_pairs={{0,1},{1,0},{2,3},{3,2},{4,5},{5,4},{6,7},{7,6},{8,9},{9,8},{10,11... | collective-permute-start | bytes 122888 | tf_op jit(solution)/shard_map/ppermute | solution.py:50
  16.2 3.8 %collective-permute-start.7 = (f32[144,128]{1,0:T(8,128)S(1)}, f32[144,128]{1,0:T(8,128)S(1)}, u32[]{:S(2)}, u32[]{:S(2)}) collective-permute-start(f32[144,128]{1,0:T(8,128)S(1)} %shard_map.46), channel_id=1, source_target_pairs={{0,64},{1,65},{2,66},{3,67},{4,68},{5,69},{6,70},{7,71},{8,72},{9,... | collective-permute-start | bytes 221192 | tf_op jit(solution)/shard_map/ppermute | solution.py:50
  16.2 5.4 %collective-permute-start.6 = (f32[144,128]{1,0:T(8,128)S(1)}, f32[144,128]{1,0:T(8,128)S(1)}, u32[]{:S(2)}, u32[]{:S(2)}) collective-permute-start(f32[144,128]{1,0:T(8,128)S(1)} %shard_map.46), channel_id=1, source_target_pairs={{0,16},{1,17},{2,18},{3,19},{4,20},{5,21},{6,22},{7,23},{8,24},{9,... | collective-permute-start | bytes 221192 | tf_op jit(solution)/shard_map/ppermute | solution.py:50
  24.9 1.8 %collective-permute-start.8 = (f32[816,128]{1,0:T(8,128)S(1)}, f32[816,128]{1,0:T(8,128)S(1)}, u32[]{:S(2)}, u32[]{:S(2)}) collective-permute-start(f32[816,128]{1,0:T(8,128)S(1)} %get-tuple-element.41), channel_id=1, source_target_pairs={{0,64},{1,65},{2,66},{3,67},{4,68},{5,69},{6,70},{7,71},{8,72},{9,... | collective-permute-start | bytes 1253384 | tf_op jit(solution)/shard_map/ppermute | solution.py:50
  25.0 9.1 %collective-permute-start.11 = (f32[816,128]{1,0:T(8,128)S(1)}, f32[816,128]{1,0:T(8,128)S(1)}, u32[]{:S(2)}, u32[]{:S(2)}) collective-permute-start(f32[816,128]{1,0:T(8,128)S(1)} %get-tuple-element.41), channel_id=1, source_target_pairs={{0,16},{1,17},{2,18},{3,19},{4,20},{5,21},{6,22},{7,23},{8,24},{9,... | collective-permute-start | bytes 1253384 | tf_op jit(solution)/shard_map/ppermute | solution.py:50
  27.2 2.0 %collective-permute-start.9 = (f32[368,128]{1,0:T(8,128)S(1)}, f32[368,128]{1,0:T(8,128)S(1)}, u32[]{:S(2)}, u32[]{:S(2)}) collective-permute-start(f32[368,128]{1,0:T(8,128)S(1)} %get-tuple-element.43), channel_id=1, source_target_pairs={{0,64},{1,65},{2,66},{3,67},{4,68},{5,69},{6,70},{7,71},{8,72},{9,... | collective-permute-start | bytes 565256 | tf_op jit(solution)/shard_map/ppermute | solution.py:50
  27.5 8.6 %collective-permute-start.10 = (f32[368,128]{1,0:T(8,128)S(1)}, f32[368,128]{1,0:T(8,128)S(1)}, u32[]{:S(2)}, u32[]{:S(2)}) collective-permute-start(f32[368,128]{1,0:T(8,128)S(1)} %get-tuple-element.43), channel_id=1, source_target_pairs={{0,16},{1,17},{2,18},{3,19},{4,20},{5,21},{6,22},{7,23},{8,24},{9,... | collective-permute-start | bytes 565256 | tf_op jit(solution)/shard_map/ppermute | solution.py:50

commit v7 on v6

--- a/solution.py
+++ b/solution.py
@@ -18,7 +18,7 @@
 INNER = BLOCKS - 2
 GROUP = 5
 FIELD_RIM = 8
-COUNTS = (24, INNER - 24)
+COUNTS = (20, INNER - 20)
 STARTS = (1, 1 + COUNTS[0])
 FOLD = 3
 SENT = [32 * count + 16 * FOLD for count in COUNTS]
@@ -296,7 +296,7 @@
                 prods[rows_at, pl.ds(128 * k, 128)] = a[k] * b[k]
         return carry
 
-    lax.fori_loop(0, BLOCKS, gradient, 0, unroll=12)
+    lax.fori_loop(0, BLOCKS, gradient, 0, unroll=18)
     spread(prods, band, sums, 3)
     scale = mean_scale()
 
@@ -411,7 +411,7 @@
                 prods[rows_at, pl.ds(128 * k, 128)] = grad[k, at, :] * chg[k, at, :]
         return carry
 
-    lax.fori_loop(0, BLOCKS, products, 0, unroll=6)
+    lax.fori_loop(0, BLOCKS, products, 0, unroll=12)
     spread(prods, band, sums, 2)
     scale = mean_scale()
     clear_rims(field)

time: 38.2 us -> 38.1 us (level)
  transfers between devices with their start and end apart: 12 -> 12, of which waited for: 8 -> 8; matrix products, arithmetic and copies ran while one was open for 0% -> 0% of each run, Pallas kernels for 27% -> 26%
where the time goes in v7:
time: 38.1 us; the launch traced here: 37.5 us
  Pallas kernels  14.4 us (38%)
  waiting for transfers between devices  11.6 us (30%)
  starting transfers between devices  10.5 us (28%)
  between operations  0.88 us (2%)
    pallas_call x11, Pallas kernels, call(): pl.pallas_call(kernel, out_shape=out_shape, compiler_params=pltpu.Compile...  14.4 us
    ppermute x12, waiting for transfers between devices, send(): return lax.ppermute(value, AXES, found)  11.6 us
    ppermute x12, starting transfers between devices, send(): return lax.ppermute(value, AXES, found)  10.5 us
  transfers between devices with their start and end apart: 12, of which 8 were waited for; matrix products, arithmetic and copies ran while one was open for 0% of the time, Pallas kernels for 26%

profile of v7, /device:TPU:120, one launch (start us, length us, event | category | flops | bytes accessed | tf_op | source)
XLA Modules:
  0.0 37.5 jit_solution(15917081093548649913)
XLA Ops:
  0.6 0.1 collective-permute-start.5
  0.7 1.3 %collective-permute-start.4 = (f32[1,256,256]{2,1,0:T(8,128)}, f32[1,256,256]{2,1,0:T(8,128)S(1)}, u32[]{:S(2)}, u32[]{:S(2)}) collective-permute-start(f32[1,256,256]{2,1,0:T(8,128)} %image.3), channel_id=1, source_target_pairs={{0,16},{1,17},{2,18},{3,19},{4,20},{5,21},{6,22},{7,23},{8,24},{9,... | collective-permute-start | bytes 786440 | tf_op jit(solution)/shard_map/ppermute | solution.py:50
  2.1 0.8 %shard_map.41 = (f32[32,256]{1,0:T(8,128)S(1)}, f32[32,256]{1,0:T(8,128)S(1)}) custom-call(f32[1,256,256]{2,1,0:T(8,128)} %image.3, f32[1,256,256]{2,1,0:T(8,128)} %stiff.3), custom_call_target="tpu_custom_call" | custom-call | flops 1000000 | bytes 3000000 | tf_op jit(solution)/shard_map/pallas_call | solution.py:625
  2.9 1.6 %collective-permute-start.1 = (f32[32,256]{1,0:T(8,128)S(1)}, f32[32,256]{1,0:T(8,128)S(1)}, u32[]{:S(2)}, u32[]{:S(2)}) collective-permute-start(f32[32,256]{1,0:T(8,128)S(1)} %get-tuple-element.29), channel_id=1, source_target_pairs={{0,16},{1,17},{2,18},{3,19},{4,20},{5,21},{6,22},{7,23},{8,24},{9,... | collective-permute-start | bytes 98312 | tf_op jit(solution)/shard_map/ppermute | solution.py:50
  4.5 0.0 collective-permute-start
  4.5 1.1 %shard_map.42 = (f32[1,256,256]{2,1,0:T(8,128)S(1)}, f32[1,256,256]{2,1,0:T(8,128)S(1)}) custom-call(f32[1,256,256]{2,1,0:T(8,128)} %image.3, f32[1,256,256]{2,1,0:T(8,128)} %stiff.3, f32[32,256]{1,0:T(8,128)S(1)} %get-tuple-element.26.after.start), custom_call_target="tpu_custom_call" | custom-call | flops 1000000 | bytes 3000000 | tf_op jit(solution)/shard_map/pallas_call | solution.py:625
  5.6 1.7 %collective-permute-done.1.row_e = f32[32,256]{1,0:T(8,128)S(1)} collective-permute-done((f32[32,256]{1,0:T(8,128)S(1)}, f32[32,256]{1,0:T(8,128)S(1)}, u32[]{:S(2)}, u32[]{:S(2)}) %collective-permute-start.1) | collective-permute-done | bytes 32800 | tf_op jit(solution)/shard_map/ppermute | solution.py:50
  7.3 1.1 %collective-permute-done.row_o = f32[32,256]{1,0:T(8,128)S(1)} collective-permute-done((f32[32,256]{1,0:T(8,128)S(1)}, f32[32,256]{1,0:T(8,128)S(1)}, u32[]{:S(2)}, u32[]{:S(2)}) %collective-permute-start) | collective-permute-done | bytes 32800 | tf_op jit(solution)/shard_map/ppermute | solution.py:50
  8.4 0.2 shard_map.43
  8.6 3.6 %collective-permute-start.2 = (f32[80,128]{1,0:T(8,128)S(1)}, f32[80,128]{1,0:T(8,128)S(1)}, u32[]{:S(2)}, u32[]{:S(2)}) collective-permute-start(f32[80,128]{1,0:T(8,128)S(1)} %get-tuple-element.30), channel_id=1, source_target_pairs={{0,16},{1,2},{2,1},{3,4},{4,3},{5,6},{6,5},{7,8},{8,7},{9,10},{10,... | collective-permute-start | bytes 122888 | tf_op jit(solution)/shard_map/ppermute | solution.py:50
  12.2 0.0 collective-permute-start.3
  12.2 2.6 %collective-permute-done.2.col_o = f32[80,128]{1,0:T(8,128)S(1)} collective-permute-done((f32[80,128]{1,0:T(8,128)S(1)}, f32[80,128]{1,0:T(8,128)S(1)}, u32[]{:S(2)}, u32[]{:S(2)}) %collective-permute-start.2) | collective-permute-done | bytes 40992 | tf_op jit(solution)/shard_map/ppermute | solution.py:50
  14.8 1.4 %collective-permute-done.3.col_e = f32[80,128]{1,0:T(8,128)S(1)} collective-permute-done((f32[80,128]{1,0:T(8,128)S(1)}, f32[80,128]{1,0:T(8,128)S(1)}, u32[]{:S(2)}, u32[]{:S(2)}) %collective-permute-start.3) | collective-permute-done | bytes 40992 | tf_op jit(solution)/shard_map/ppermute | solution.py:50
  16.2 0.0 collective-permute-start.7
  16.2 0.8 %collective-permute-start.6 = (f32[144,128]{1,0:T(8,128)S(1)}, f32[144,128]{1,0:T(8,128)S(1)}, u32[]{:S(2)}, u32[]{:S(2)}) collective-permute-start(f32[144,128]{1,0:T(8,128)S(1)} %shard_map.46), channel_id=1, source_target_pairs={{0,16},{1,17},{2,18},{3,19},{4,20},{5,21},{6,22},{7,23},{8,24},{9,... | collective-permute-start | bytes 221192 | tf_op jit(solution)/shard_map/ppermute | solution.py:50
  17.1 0.1 shard_map.44.band
  17.1 2.8 %shard_map.45 = (f32[3,304,128]{2,1,0:T(8,128)S(1)}, f32[3,288,128]{2,1,0:T(8,128)S(1)}, f32[3,288,128]{2,1,0:T(8,128)S(1)}, f32[3,3,288,128]{3,2,1,0:T(8,128)S(...) custom-call(f32[1,256,256]{2,1,0:T(8,128)S(1)} %get-tuple-element.27.image, ...), custom_call_target="tpu_custom_call" | custom-call | flops 4000000 | bytes 12000000 | tf_op jit(solution)/shard_map/pallas_call | solution.py:625
  19.9 0.0 collective-permute-done.7.near
  19.9 1.7 %collective-permute-done.6.far = f32[144,128]{1,0:T(8,128)S(1)} collective-permute-done((f32[144,128]{1,0:T(8,128)S(1)}, f32[144,128]{1,0:T(8,128)S(1)}, u32[]{:S(2)}, u32[]{:S(2)}) %collective-permute-start.6) | collective-permute-done | bytes 73760 | tf_op jit(solution)/shard_map/ppermute | solution.py:50
  21.6 0.0 collective-permute-done.5.later_near
  21.6 0.0 collective-permute-done.4.later_far
  21.6 3.1 %shard_map.47 = (f32[2,288,256]{2,1,0:T(8,128)S(1)}, f32[2,3,288,128]{3,2,1,0:T(8,128)S(1)}, f32[2,3,288,128]{3,2,1,0:T(8,128)S(1)}, f32[2,3,288,128]{3,2,1,0:T(...) custom-call(f32[3,304,128]{2,1,0:T(8,128)S(1)} %get-tuple-element.32.ext, ...), custom_call_target="tpu_custom_call" | custom-call | flops 5000000 | bytes 15000000 | tf_op jit(solution)/shard_map/pallas_call | solution.py:625
  24.7 0.1 collective-permute-start.8
  24.8 0.9 %collective-permute-start.11 = (f32[688,128]{1,0:T(8,128)S(1)}, f32[688,128]{1,0:T(8,128)S(1)}, u32[]{:S(2)}, u32[]{:S(2)}) collective-permute-start(f32[688,128]{1,0:T(8,128)S(1)} %get-tuple-element.41), channel_id=1, source_target_pairs={{0,16},{1,17},{2,18},{3,19},{4,20},{5,21},{6,22},{7,23},{8,24},{9,... | collective-permute-start | bytes 1056776 | tf_op jit(solution)/shard_map/ppermute | solution.py:50
  25.8 0.7 %collective-permute-done.8.after.near_a = f32[688,128]{1,0:T(8,128)S(1)} collective-permute-done((f32[688,128]{1,0:T(8,128)S(1)}, f32[688,128]{1,0:T(8,128)S(1)}, u32[]{:S(2)}, u32[]{:S(2)}) %collective-permute-start.8) | collective-permute-done | bytes 352288 | tf_op jit(solution)/shard_map/ppermute | solution.py:50
  26.5 0.7 %shard_map.48 = (f32[2,3,288,128]{3,2,1,0:T(8,128)S(1)}, f32[496,128]{1,0:T(8,128)S(1)}) custom-call(f32[2,3,288,128]{3,2,1,0:T(8,128)S(1)} %get-tuple-element.37.rhs, f32[3,3,288,128]{3,2,1,0:T(8,128)S(1)} %get-tuple-element.35.matrix, f32[3,288,128]{2,1,0:T(8,128)S(1)} %get-tuple-element.36.inverse, f32[2,3,288,128]{3,2,1,0:T(8,128)S(1)} %get-tuple-element.38.once, ...), custom_call_target="tpu_custom_call" | custom-call | flops 1000000 | bytes 3000000 | tf_op jit(solution)/shard_map/pallas_call | solution.py:625
  27.1 0.2 collective-permute-start.9
  27.4 1.8 %collective-permute-start.10 = (f32[496,128]{1,0:T(8,128)S(1)}, f32[496,128]{1,0:T(8,128)S(1)}, u32[]{:S(2)}, u32[]{:S(2)}) collective-permute-start(f32[496,128]{1,0:T(8,128)S(1)} %get-tuple-element.43), channel_id=1, source_target_pairs={{0,16},{1,17},{2,18},{3,19},{4,20},{5,21},{6,22},{7,23},{8,24},{9,... | collective-permute-start | bytes 761864 | tf_op jit(solution)/shard_map/ppermute | solution.py:50
  29.2 0.0 collective-permute-done.9.near_b
  29.2 2.6 %shard_map.49 = (f32[2,2,288,128]{3,2,1,0:T(8,128)S(1)}, f32[5,1,256,256]{3,2,1,0:T(8,128)}) custom-call(f32[2,3,288,128]{3,2,1,0:T(8,128)S(1)} %get-tuple-element.37.rhs, f32[3,3,288,128]{3,2,1,0:T(8,128)S(1)} %get-tuple-element.35.matrix, f32[3,288,128]{2,1,0:T(8,128)S(1)} %get-tuple-element.36.inverse, f32[2,3,288,128]{3,2,1,0:T(8,128)S(1)} %get-tuple-element.42.field, ...), custom_call_target="tpu_custom_call" | custom-call | flops 3000000 | bytes 9000000 | tf_op jit(solution)/shard_map/pallas_call | solution.py:625
  31.9 1.3 %collective-permute-done.11.far = f32[688,128]{1,0:T(8,128)S(1)} collective-permute-done((f32[688,128]{1,0:T(8,128)S(1)}, f32[688,128]{1,0:T(8,128)S(1)}, u32[]{:S(2)}, u32[]{:S(2)}) %collective-permute-start.11) | collective-permute-done | bytes 352288 | tf_op jit(solution)/shard_map/ppermute | solution.py:50
  33.2 1.6 %shard_map.50 = (f32[2,1,256,256]{3,2,1,0:T(8,128)}, f32[2,2,16,128]{3,2,1,0:T(8,128)S(1)}) custom-call(f32[3,3,288,128]{3,2,1,0:T(8,128)S(1)} %get-tuple-element.35.matrix, f32[3,288,128]{2,1,0:T(8,128)S(1)} %get-tuple-element.36.inverse, f32[2,2,288,128]{3,2,1,0:T(8,128)S(1)} %get-tuple-element.47.carried, f32[688,128]{1,0:T(8,128)S(1)} %collective-permute-done.11.far), custom_call_target="tpu_custom_call" | custom-call | flops 2000000 | bytes 6000000 | tf_op jit(solution)/shard_map/pallas_call | solution.py:625
  34.8 1.1 %collective-permute-done.10.far = f32[496,128]{1,0:T(8,128)S(1)} collective-permute-done((f32[496,128]{1,0:T(8,128)S(1)}, f32[496,128]{1,0:T(8,128)S(1)}, u32[]{:S(2)}, u32[]{:S(2)}) %collective-permute-start.10) | collective-permute-done | bytes 253984 | tf_op jit(solution)/shard_map/ppermute | solution.py:50
  35.9 1.4 %shard_map.51 = f32[2,1,256,256]{3,2,1,0:T(8,128)} custom-call(f32[3,3,288,128]{3,2,1,0:T(8,128)S(1)} %get-tuple-element.35.matrix, f32[3,288,128]{2,1,0:T(8,128)S(1)} %get-tuple-element.36.inverse, f32[2,2,288,128]{3,2,1,0:T(8,128)S(1)} %get-tuple-element.47.carried, f32[496,128]{1,0:T(8,128)S(1)} %collective-permute-done.10.far, ...), custom_call_target="tpu_custom_call", output_to_operand_aliasing={{}: (5, {})} | custom-call | flops 2000000 | bytes 6000000 | tf_op jit(solution)/shard_map/pallas_call | solution.py:625
  (1 shorter events, 0.0 us)
Async XLA Ops:
  0.6 21.0 %collective-permute-start.5 = (f32[1,256,256]{2,1,0:T(8,128)}, f32[1,256,256]{2,1,0:T(8,128)S(1)}, u32[]{:S(2)}, u32[]{:S(2)}) collective-permute-start(f32[1,256,256]{2,1,0:T(8,128)} %image.3), channel_id=1, source_target_pairs={{0,64},{1,65},{2,66},{3,67},{4,68},{5,69},{6,70},{7,71},{8,72},{9,... | collective-permute-start | bytes 786440 | tf_op jit(solution)/shard_map/ppermute | solution.py:50
  0.7 20.9 %collective-permute-start.4 = (f32[1,256,256]{2,1,0:T(8,128)}, f32[1,256,256]{2,1,0:T(8,128)S(1)}, u32[]{:S(2)}, u32[]{:S(2)}) collective-permute-start(f32[1,256,256]{2,1,0:T(8,128)} %image.3), channel_id=1, source_target_pairs={{0,16},{1,17},{2,18},{3,19},{4,20},{5,21},{6,22},{7,23},{8,24},{9,... | collective-permute-start | bytes 786440 | tf_op jit(solution)/shard_map/ppermute | solution.py:50
  2.9 4.4 %collective-permute-start.1 = (f32[32,256]{1,0:T(8,128)S(1)}, f32[32,256]{1,0:T(8,128)S(1)}, u32[]{:S(2)}, u32[]{:S(2)}) collective-permute-start(f32[32,256]{1,0:T(8,128)S(1)} %get-tuple-element.29), channel_id=1, source_target_pairs={{0,16},{1,17},{2,18},{3,19},{4,20},{5,21},{6,22},{7,23},{8,24},{9,... | collective-permute-start | bytes 98312 | tf_op jit(solution)/shard_map/ppermute | solution.py:50
  4.5 3.9 %collective-permute-start = (f32[32,256]{1,0:T(8,128)S(1)}, f32[32,256]{1,0:T(8,128)S(1)}, u32[]{:S(2)}, u32[]{:S(2)}) collective-permute-start(f32[32,256]{1,0:T(8,128)S(1)} %get-tuple-element.26.after.start), channel_id=1, source_target_pairs={{0,1},{1,0},{2,3},{3,2},{4,5},{5,4},{6,7},{7,6},{8,9},{9,8},{10,11... | collective-permute-start | bytes 98312 | tf_op jit(solution)/shard_map/ppermute | solution.py:50
  8.6 6.2 %collective-permute-start.2 = (f32[80,128]{1,0:T(8,128)S(1)}, f32[80,128]{1,0:T(8,128)S(1)}, u32[]{:S(2)}, u32[]{:S(2)}) collective-permute-start(f32[80,128]{1,0:T(8,128)S(1)} %get-tuple-element.30), channel_id=1, source_target_pairs={{0,16},{1,2},{2,1},{3,4},{4,3},{5,6},{6,5},{7,8},{8,7},{9,10},{10,... | collective-permute-start | bytes 122888 | tf_op jit(solution)/shard_map/ppermute | solution.py:50
  12.2 4.0 %collective-permute-start.3 = (f32[80,128]{1,0:T(8,128)S(1)}, f32[80,128]{1,0:T(8,128)S(1)}, u32[]{:S(2)}, u32[]{:S(2)}) collective-permute-start(f32[80,128]{1,0:T(8,128)S(1)} %get-tuple-element.31), channel_id=1, source_target_pairs={{0,1},{1,0},{2,3},{3,2},{4,5},{5,4},{6,7},{7,6},{8,9},{9,8},{10,11... | collective-permute-start | bytes 122888 | tf_op jit(solution)/shard_map/ppermute | solution.py:50
  16.2 3.7 %collective-permute-start.7 = (f32[144,128]{1,0:T(8,128)S(1)}, f32[144,128]{1,0:T(8,128)S(1)}, u32[]{:S(2)}, u32[]{:S(2)}) collective-permute-start(f32[144,128]{1,0:T(8,128)S(1)} %shard_map.46), channel_id=1, source_target_pairs={{0,64},{1,65},{2,66},{3,67},{4,68},{5,69},{6,70},{7,71},{8,72},{9,... | collective-permute-start | bytes 221192 | tf_op jit(solution)/shard_map/ppermute | solution.py:50
  16.2 5.4 %collective-permute-start.6 = (f32[144,128]{1,0:T(8,128)S(1)}, f32[144,128]{1,0:T(8,128)S(1)}, u32[]{:S(2)}, u32[]{:S(2)}) collective-permute-start(f32[144,128]{1,0:T(8,128)S(1)} %shard_map.46), channel_id=1, source_target_pairs={{0,16},{1,17},{2,18},{3,19},{4,20},{5,21},{6,22},{7,23},{8,24},{9,... | collective-permute-start | bytes 221192 | tf_op jit(solution)/shard_map/ppermute | solution.py:50
  24.7 1.7 %collective-permute-start.8 = (f32[688,128]{1,0:T(8,128)S(1)}, f32[688,128]{1,0:T(8,128)S(1)}, u32[]{:S(2)}, u32[]{:S(2)}) collective-permute-start(f32[688,128]{1,0:T(8,128)S(1)} %get-tuple-element.41), channel_id=1, source_target_pairs={{0,64},{1,65},{2,66},{3,67},{4,68},{5,69},{6,70},{7,71},{8,72},{9,... | collective-permute-start | bytes 1056776 | tf_op jit(solution)/shard_map/ppermute | solution.py:50
  24.8 8.4 %collective-permute-start.11 = (f32[688,128]{1,0:T(8,128)S(1)}, f32[688,128]{1,0:T(8,128)S(1)}, u32[]{:S(2)}, u32[]{:S(2)}) collective-permute-start(f32[688,128]{1,0:T(8,128)S(1)} %get-tuple-element.41), channel_id=1, source_target_pairs={{0,16},{1,17},{2,18},{3,19},{4,20},{5,21},{6,22},{7,23},{8,24},{9,... | collective-permute-start | bytes 1056776 | tf_op jit(solution)/shard_map/ppermute | solution.py:50
  27.1 2.1 %collective-permute-start.9 = (f32[496,128]{1,0:T(8,128)S(1)}, f32[496,128]{1,0:T(8,128)S(1)}, u32[]{:S(2)}, u32[]{:S(2)}) collective-permute-start(f32[496,128]{1,0:T(8,128)S(1)} %get-tuple-element.43), channel_id=1, source_target_pairs={{0,64},{1,65},{2,66},{3,67},{4,68},{5,69},{6,70},{7,71},{8,72},{9,... | collective-permute-start | bytes 761864 | tf_op jit(solution)/shard_map/ppermute | solution.py:50
  27.4 8.5 %collective-permute-start.10 = (f32[496,128]{1,0:T(8,128)S(1)}, f32[496,128]{1,0:T(8,128)S(1)}, u32[]{:S(2)}, u32[]{:S(2)}) collective-permute-start(f32[496,128]{1,0:T(8,128)S(1)} %get-tuple-element.43), channel_id=1, source_target_pairs={{0,16},{1,17},{2,18},{3,19},{4,20},{5,21},{6,22},{7,23},{8,24},{9,... | collective-permute-start | bytes 761864 | tf_op jit(solution)/shard_map/ppermute | solution.py:50
